TPU v7x, 256 devices: a whole 4x4x8 slice. The times are simulated.
256 devices in a mesh: tm: 32 (over y_hi, z, core), head: 8 (over y_lo, x).
Axes of the slice: x: 4, y: 4 (y_hi: 2, y_lo: 2; y = y_hi * 2 + y_lo), z: 8, core: 2. Of those that a mesh axis runs over, the one named last changes fastest.
Arguments:
- frames: bfloat16 [16384, 1024], P('tm'), may hold values from -8 to 8
- norm_gain: float32 [1024], replicated, may hold values from 0.5 to 1.5
- w_qkv: bfloat16 [3, 1024, 1024], P(None, 'tm', 'head'), may hold values from -6 to 6
- slopes: float32 [8], P('head'), may hold values from 1.5258789e-05 to 0.05
- w_out: bfloat16 [1024, 1024], P('head', 'tm'), may hold values from -0.5 to 0.5
Outputs:
- attended: bfloat16 [16384, 1024], P(('tm', 'head'))
All inputs are finite; a program needn't handle non-finite values.
Results may differ from a plain program's by a relative error of at most 0.014.
Values may be sent and summed in bfloat16 or wider, within the bound.
No kernel may reach another device: no remote copies, remote signals or barrier semaphores. Data moves between devices by JAX's collectives and lax.ppermute only.
A program may use at most 128 MiB of HBM per device.

v0:
```python
import jax
import jax.numpy as jnp
from jax import lax
from jax.sharding import PartitionSpec as P


def local(frames, norm_gain, w_qkv, slopes, w_out):
    frame_count = frames.shape[0]
    local_heads = slopes.shape[0]
    head_size = w_qkv.shape[2] // local_heads
    tm_count = lax.axis_size("tm")
    clip_len = frame_count * tm_count
    me_tm = lax.axis_index("tm")
    scale = head_size ** (-0.5)
    wide = frames.astype(jnp.float32)
    mean_square = jnp.mean(wide * wide, axis=-1, keepdims=True)
    inverse_root = lax.rsqrt(mean_square + 1e-06)
    normed = (wide * inverse_root * norm_gain).astype(jnp.bfloat16)
    projected = jnp.einsum(
        "rd,cde->cre",
        normed,
        lax.all_gather(w_qkv, "tm", axis=1, tiled=True),
        preferred_element_type=jnp.float32,
    ).astype(jnp.bfloat16)
    query = projected[0].reshape(frame_count, local_heads, head_size)
    keyed = projected[1].reshape(frame_count, local_heads, head_size)
    valued = projected[2].reshape(frame_count, local_heads, head_size)
    row_pos = me_tm * frame_count + jnp.arange(frame_count, dtype=jnp.int32)
    key_piece = lax.all_gather(keyed, "tm", axis=0, tiled=True)
    peak = jnp.full((local_heads, frame_count), -1e30, jnp.float32)
    scores = (
        jnp.einsum("qhd,khd->hqk", query, key_piece, preferred_element_type=jnp.float32) * scale
    )
    key_pos = jnp.arange(key_piece.shape[0], dtype=jnp.int32)
    differ = (key_pos[None, :] - row_pos[:, None]) % clip_len
    distance = jnp.minimum(differ, clip_len - differ).astype(jnp.float32)
    scores = scores - slopes[:, None, None] * distance[None, :, :]
    new_peak = jnp.maximum(peak, jnp.max(scores, axis=-1))
    expo = jnp.exp(scores - new_peak[:, :, None])
    totals = jnp.sum(expo, axis=-1)
    accum = jnp.einsum(
        "hqk,khd->hqd",
        expo.astype(jnp.bfloat16),
        lax.all_gather(valued, "tm", axis=0, tiled=True),
        preferred_element_type=jnp.float32,
    )
    state = (new_peak, totals, accum)
    peak, totals, accum = state
    mixed = (accum / totals[:, :, None]).astype(jnp.bfloat16)
    mixed = jnp.transpose(mixed, (1, 0, 2)).reshape(frame_count, local_heads * head_size)
    out_local = lax.all_gather(w_out, "tm", axis=1, tiled=True)
    return lax.psum_scatter(
        jnp.dot(mixed, out_local, preferred_element_type=jnp.float32).astype(jnp.bfloat16),
        "head",
        scatter_dimension=0,
        tiled=True,
    )


def solution(mesh):
    in_specs = (P("tm", None), P(), P(None, "tm", "head"), P("head"), P("head", "tm"))
    out_specs = P(("tm", "head"), None)
    return jax.shard_map(local, mesh=mesh, in_specs=in_specs, out_specs=out_specs, check_vma=False)
```

profile of v0, /device:TPU:16, one launch (start us, length us, event | category | flops | bytes accessed | tf_op | source)
XLA Modules:
  0.0 288.0 jit_solution(1928262164631459271)
XLA Ops:
  6.5 0.0 all-gather.5.cloned.1.call-start
  6.5 44.3 %all_gather.12 = bf16[3,1024,128]{2,1,0:T(8,128)(2,1)S(1)} all-gather(bf16[3,32,128]{2,1,0:T(8,128)(2,1)} %param.7), channel_id=1, replica_groups=mesh['tm'=32,'head'=8] {'tm'}, dimensions={1}, use_global_device_ids=true | all-gather | bytes 811008 | tf_op jit(solution)/shard_map/all_gather | solution.py:22
  50.9 1.5 fusion.14
  52.4 2.0 fusion.17
  54.4 0.7 fusion.37
  55.1 0.0 all-gather.5.cloned.1.call-update
  55.1 0.0 all-gather.7.cloned.1.call-start
  55.2 0.7 all-gather.7.cloned.1.call-update
  55.9 0.0 reduce-scatter.2.cloned.1.call-start
  56.6 37.8 %all_gather.15 = bf16[128,1024]{0,1:T(8,128)(2,1)S(1)} all-gather(bf16[128,32]{0,1:T(8,128)(2,1)} %param.9), channel_id=1, replica_groups=mesh['tm'=32,'head'=8] {'tm'}, dimensions={1}, use_global_device_ids=true | all-gather | bytes 270336 | tf_op jit(solution)/shard_map/all_gather | solution.py:51
  94.4 41.8 %all-gather.5.cloned.1.call-done = bf16[1,16384,128]{2,1,0:T(8,128)(2,1)} async-done(((bf16[1,512,128]{2,1,0:T(8,128)(2,1)}), bf16[1,16384,128]{2,1,0:T(8,128)(2,1)}) %all-gather.5.cloned.1.call-update) | async-done | bytes 4194320 | tf_op jit(solution)/shard_map/all_gather | solution.py:29
  136.2 29.7 %fusion.38 = (f32[512]{0:T(512)S(1)}, f32[512,16384]{1,0:T(8,128)}) fusion(s32[512]{0:T(512)S(1)} %iota_add_fusion, f32[]{:T(128)} %bitcast.27, bf16[1,16384,128]{2,1,0:T(8,128)(2,1)} %all-gather.5.cloned.1.call-done, bf16[3,512,128]{2,1,0:T(8,128)(2,1)S(1)} %fusion.17), kind=kOutput, calls=%fused_computation.37 | convolution fusion | flops 2306866688 | bytes 37883908 | tf_op jit(solution)/shard_map/qhd,khd->hqk/dot_general | solution.py:32
  166.0 13.9 %fusion.7 = f32[512]{0:T(512)S(1)} fusion(f32[512,16384]{1,0:T(8,128)} %get-tuple-element.8, f32[512]{0:T(512)S(1)} %broadcast_maximum_fusion), kind=kLoop, calls=%fused_computation.12 | loop fusion | flops 16776704 | bytes 33558528 | tf_op jit(solution)/shard_map/reduce_sum | solution.py:40
  179.8 42.5 %all-gather.7.cloned.1.call-done = bf16[1,16384,128]{2,1,0:T(8,128)(2,1)} async-done(((bf16[1,512,128]{2,1,0:T(8,128)(2,1)}), bf16[1,16384,128]{2,1,0:T(8,128)(2,1)}) %all-gather.7.cloned.1.call-update) | async-done | bytes 4194320 | tf_op jit(solution)/shard_map/all_gather | solution.py:44
  222.4 18.0 %convolution_convert_fusion = bf16[512,1024]{1,0:T(8,128)(2,1)} fusion(bf16[128,1024]{0,1:T(8,128)(2,1)S(1)} %all_gather.15, bf16[1,16384,128]{2,1,0:T(8,128)(2,1)} %all-gather.7.cloned.1.call-done, f32[512,16384]{1,0:T(8,128)} %get-tuple-element.8, f32[512]{0:T(512)S(1)} %broadcast_maximum_fusion, f32[512]{0:T(512)S(1)} %fusion.7), kind=kOutput, calls=%fused_computation.23 | convolution fusion | flops 2299133952 | bytes 39063552 | tf_op jit(solution)/shard_map/dot_general | solution.py:53
  240.4 0.0 reduce-scatter.2.cloned.1.call-update
  240.4 41.1 %reduce-scatter.2.cloned.1.call-done = bf16[64,1024]{1,0:T(8,128)(2,1)} async-done(((bf16[512,1024]{1,0:T(8,128)(2,1)}), bf16[64,1024]{1,0:T(8,128)(2,1)}) %reduce-scatter.2.cloned.1.call-update) | async-done | bytes 131088 | tf_op jit(solution)/shard_map/reduce_scatter | solution.py:52
  (3 shorter events, 0.0 us)
Async XLA Ops:
  6.5 129.7 %all-gather.5.cloned.1.call-start = ((), (), s32[]{:S(2)}) async-start(), calls=%async_computation.2 | async-start | bytes 4325376 | tf_op jit(solution)/shard_map/all_gather | solution.py:29
  55.1 167.2 %all-gather.7.cloned.1.call-start = ((), (), s32[]{:S(2)}) async-start(), calls=%async_computation.3 | async-start | bytes 4325376 | tf_op jit(solution)/shard_map/all_gather | solution.py:44
  55.9 225.6 %reduce-scatter.2.cloned.1.call-start = ((), (), s32[]{:S(2)}) async-start(), calls=%async_computation.1 | async-start | bytes 1179648 | tf_op jit(solution)/shard_map/reduce_scatter | solution.py:52
Sparse Core Ops, SparseCore 0:
  55.2 80.9 all-gather.4
  139.0 83.3 all-gather.6
  240.5 40.8 reduce-scatter.1
where the time goes:
time: 288 us
  waiting for transfers between devices  126 us (44%)
  blocking collectives  82.2 us (29%)
  matrix products  49.7 us (17%)
  other arithmetic  15.4 us (5%)
  between operations  13.8 us (5%)
    all_gather x1, blocking collectives, local(): lax.all_gather(w_qkv, 'tm', axis=1, tiled=True)  44.3 us
    all_gather x1, waiting for transfers between devices, local(): lax.all_gather(valued, 'tm', axis=0, tiled=True)  42.5 us
    all_gather x1, waiting for transfers between devices, local(): key_piece = lax.all_gather(keyed, 'tm', axis=0, tiled=True)  41.8 us
    reduce_scatter x1, waiting for transfers between devices, local(): lax.psum_scatter(jnp.dot(mixed, out_local, preferred_element_type=jnp.flo...  41.1 us
    all_gather x1, blocking collectives, local(): out_local = lax.all_gather(w_out, 'tm', axis=1, tiled=True)  37.8 us
    dot_general x1, matrix products, local(): jnp.einsum('qhd,khd->hqk', query, key_piece, preferred_element_type=jnp.f...  29.7 us
    dot_general x1, matrix products, local(): jnp.dot(mixed, out_local, preferred_element_type=jnp.float32)  18 us
    reduce_sum x1, other arithmetic, local(): totals = jnp.sum(expo, axis=-1)  13.9 us
  transfers between devices with their start and end apart: 3, of which 3 were waited for; matrix products, arithmetic and copies ran while one was open for 15% of the time, Pallas kernels for 0%

commit v1 on v0

v1 whole, which is shorter than its diff:
```python
import functools
import math

import jax
import jax.numpy as jnp
from jax import lax
from jax.experimental import pallas as pl
from jax.experimental.pallas import tpu as pltpu
from jax.sharding import PartitionSpec as P

F32, BF16 = jnp.float32, jnp.bfloat16
LOG2E = math.log2(math.e)
YH, Z, CORE = 2, 8, 2
TM = YH * Z * CORE


def tm_permute(x, d_yh, d_z, d_core):
    pairs = []
    for yh in range(YH):
        for z in range(Z):
            for core in range(CORE):
                source = ((yh + d_yh) % YH * Z + (z + d_z) % Z) * CORE + (core + d_core) % CORE
                pairs.append((source, (yh * Z + z) * CORE + core))
    return lax.ppermute(x, "tm", pairs)


def split_bf16(x):
    high = x.astype(BF16)
    rest = x - high.astype(F32)
    mid = rest.astype(BF16)
    return high, mid, (rest - mid.astype(F32)).astype(BF16)


def pack_partial(out, lse):
    high, mid, low = split_bf16(lse)
    lane = lax.broadcasted_iota(jnp.int32, lse.shape, 1)
    stat = jnp.where(lane < 32, high.astype(F32), jnp.where(lane < 64, mid.astype(F32), low.astype(F32)))
    return jnp.concatenate([out.astype(BF16), stat.astype(BF16)], axis=1)


def unpack_partial(packed):
    out = packed[:, :128].astype(F32)
    stat = packed[:, 128:].astype(F32)
    lse = stat[:, 0:1] + stat[:, 32:33] + stat[:, 64:65]
    return out, jnp.broadcast_to(lse, out.shape)


def attention_kernel(shards, offset, first, last, scale, *refs):
    kind_ref, base_ref = refs[:2]
    q_ref = refs[2]
    kv_refs = refs[3 : 3 + shards]
    bias_refs = refs[3 + shards : 3 + 2 * shards]
    rest = refs[3 + 2 * shards :]
    if not first:
        peak_ref, sums_ref = rest[:2]
        rest = rest[2:]
    out_refs = rest
    block = pl.program_id(0)
    rows = q_ref.shape[0]
    keys = kv_refs[0].shape[0]
    chunk = 256
    ones = jnp.ones((keys, 128), BF16)
    bases = [base_ref[offset + 4 * j + block] for j in range(shards)]
    for start in range(0, rows, chunk):
        here = pl.ds(start, chunk)
        query = q_ref[here, :]
        scores, top = [], None
        for j in range(shards):
            score = lax.dot_general(
                query, kv_refs[j][:, :128], (((1,), (1,)), ((), ())), preferred_element_type=F32
            )
            score = score * scale + bias_refs[j][0, here, :]
            scores.append(score)
            here_top = jnp.max(score, axis=1, keepdims=True) - bases[j]
            top = here_top if top is None else jnp.maximum(top, here_top)
        peak = jnp.broadcast_to(top, (chunk, 128))
        if not first:
            old = peak_ref[here, :]
            peak = jnp.maximum(peak, old)
        total = None
        for j in range(shards):
            weight = jnp.exp2(scores[j] - jnp.tile(peak + bases[j], (1, keys // 128))).astype(BF16)
            value = jnp.concatenate([kv_refs[j][:, 128:], ones], axis=1)
            part = jnp.dot(weight, value, preferred_element_type=F32)
            total = part if total is None else total + part
        if not first:
            total = total + sums_ref[here, :] * jnp.tile(jnp.exp2(old - peak), (1, 2))
        if last:
            norm = total[:, :128] / total[:, 128:]
            lse = peak + jnp.log2(total[:, 128:])
            out_refs[0][here, :] = pack_partial(norm, lse)
            out_refs[1][here, :] = norm
            out_refs[2][here, :] = lse
        else:
            out_refs[0][here, :] = peak
            out_refs[1][here, :] = total


def attention_step(kinds, bases, query, kvs, bias, state, first_shard, last, scale):
    shards = len(kvs)
    total_rows = query.shape[0]
    keys = kvs[0].shape[0]
    rows = bias.shape[1]
    first = state is None
    offset = 4 * first_shard
    in_specs = [pl.BlockSpec((rows, 128), lambda i, kind, base: (i, 0))]
    in_specs += [pl.BlockSpec((keys, 256), lambda i, kind, base: (0, 0)) for _ in kvs]
    for j in range(shards):
        in_specs.append(
            pl.BlockSpec((1, rows, keys), lambda i, kind, base, j=j: (kind[offset + 4 * j + i], 0, 0))
        )
    args = [kinds, bases, query, *kvs] + [bias] * shards
    if not first:
        in_specs += [
            pl.BlockSpec((rows, 128), lambda i, kind, base: (i, 0)),
            pl.BlockSpec((rows, 256), lambda i, kind, base: (i, 0)),
        ]
        args += list(state)
    if last:
        shapes = [((total_rows, 256), BF16), ((total_rows, 128), F32), ((total_rows, 128), F32)]
    else:
        shapes = [((total_rows, 128), F32), ((total_rows, 256), F32)]
    out_specs = [pl.BlockSpec((rows, s[1]), lambda i, kind, base: (i, 0)) for s, _ in shapes]
    return pl.pallas_call(
        functools.partial(attention_kernel, shards, offset, first, last, scale),
        out_shape=[jax.ShapeDtypeStruct(s, t) for s, t in shapes],
        grid_spec=pltpu.PrefetchScalarGridSpec(
            num_scalar_prefetch=2,
            grid=(total_rows // rows,),
            in_specs=in_specs,
            out_specs=out_specs,
        ),
        cost_estimate=pl.CostEstimate(
            flops=4 * total_rows * keys * shards * 256,
            bytes_accessed=total_rows * 3072 + shards * keys * 512,
            transcendentals=total_rows * keys * shards,
        ),
    )(*args)


def merge(out_a, lse_a, out_b, lse_b):
    top = jnp.maximum(lse_a, lse_b)
    part_a, part_b = jnp.exp2(lse_a - top), jnp.exp2(lse_b - top)
    both = part_a + part_b
    return (out_a * part_a + out_b * part_b) / both, top + jnp.log2(both)


def merge_core_kernel(out_ref, lse_ref, got_ref, send_ref, keep_ref, keep_lse_ref):
    block = pl.program_id(0)
    got, got_lse = unpack_partial(got_ref[...])
    out, lse = merge(out_ref[...], lse_ref[...], got, got_lse)

    @pl.when(block == 0)
    def _():
        keep_ref[...] = out
        keep_lse_ref[...] = lse

    @pl.when(block == 1)
    def _():
        send_ref[...] = pack_partial(out, lse)


def merge_core(out, lse, got, rows):
    row_block = lambda i: (i, 0)
    fixed = lambda i: (0, 0)
    return pl.pallas_call(
        merge_core_kernel,
        out_shape=[
            jax.ShapeDtypeStruct((rows, 256), BF16),
            jax.ShapeDtypeStruct((rows, 128), F32),
            jax.ShapeDtypeStruct((rows, 128), F32),
        ],
        grid=(2,),
        in_specs=[
            pl.BlockSpec((rows, 128), row_block),
            pl.BlockSpec((rows, 128), row_block),
            pl.BlockSpec((rows, 256), row_block),
        ],
        out_specs=[
            pl.BlockSpec((rows, 256), fixed),
            pl.BlockSpec((rows, 128), fixed),
            pl.BlockSpec((rows, 128), fixed),
        ],
    )(out, lse, got)


def merge_project_kernel(out_ref, lse_ref, got_ref, w_ref, partial_ref):
    got, got_lse = unpack_partial(got_ref[...])
    out, _ = merge(out_ref[...], lse_ref[...], got, got_lse)
    partial_ref[...] = lax.dot_general(
        out.astype(BF16), w_ref[...], (((1,), (1,)), ((), ())), preferred_element_type=F32
    ).astype(BF16)


def merge_project(out, lse, got, w_out_t):
    rows, width = out.shape[0], w_out_t.shape[0]
    return pl.pallas_call(
        merge_project_kernel,
        out_shape=jax.ShapeDtypeStruct((rows, width), BF16),
    )(out, lse, got, w_out_t)


def local(frames, norm_gain, w_qkv, slopes, w_out):
    rows, width = frames.shape
    me = lax.axis_index("tm")
    core, z, yh = me % CORE, me // CORE % Z, me // (CORE * Z)

    part = w_qkv.shape[1]
    own = jnp.concatenate([w_qkv.reshape(3 * part, 128), w_out.T], axis=0)
    held = jnp.zeros((Z,) + own.shape, BF16)
    held = lax.dynamic_update_slice(held, own[None], (z, 0, 0))
    up = down = own
    for step in range(1, Z // 2 + 1):
        up = tm_permute(up, 0, 1, 0)
        held = lax.dynamic_update_slice(held, up[None], ((z + step) % Z, 0, 0))
        if step < Z // 2:
            down = tm_permute(down, 0, -1, 0)
            held = lax.dynamic_update_slice(held, down[None], ((z - step) % Z, 0, 0))
    other = tm_permute(held, 1, 0, 0)
    flip = yh == 1
    held = jnp.stack([jnp.where(flip, other, held), jnp.where(flip, held, other)])
    other = tm_permute(held, 0, 0, 1)
    flip = core == 1
    held = jnp.stack([jnp.where(flip, other, held), jnp.where(flip, held, other)], axis=2)
    held = held.reshape(TM, 4, part, 128)
    w_all = jnp.transpose(held[:, :3], (0, 2, 1, 3)).reshape(width, 384)
    w_out_t = held[:, 3].reshape(width, 128)

    wide = frames.astype(F32)
    mean_square = jnp.mean(wide * wide, axis=-1, keepdims=True)
    normed = (wide * lax.rsqrt(mean_square + 1e-06) * norm_gain).astype(BF16)
    projected = jnp.dot(normed, w_all, preferred_element_type=F32).astype(BF16)
    query, kv = projected[:, :128], projected[:, 128:]

    slope = slopes[0] * LOG2E
    spot = jnp.arange(rows, dtype=jnp.int32)
    ahead = (spot[None, :] - spot[:, None]).astype(F32) * slope
    apart = jnp.abs(ahead)
    bias = jnp.stack([-ahead, ahead, -apart, apart])
    moves = [0]
    for step in range(1, Z // 2):
        moves += [step, -step]
    moves.append(Z // 2)
    key_block = (yh * Z + (z + jnp.array(moves, jnp.int32)) % Z) * CORE + core
    turn = jnp.arange(4, dtype=jnp.int32)
    query_block = ((yh + turn % 2) % 2 * Z + z) * CORE + (core + turn // 2) % 2
    gap = (key_block[:, None] - query_block[None, :]) % TM
    half = TM // 2
    kinds = jnp.where(gap == 0, 2, jnp.where(gap < half, 0, jnp.where(gap == half, 3, 1)))
    bases = jnp.minimum(gap, TM - gap).astype(F32) * rows * slope
    kinds, bases = kinds.astype(jnp.int32).reshape(-1), bases.reshape(-1)

    both = jnp.concatenate([query, tm_permute(query, 1, 0, 0)], axis=0)
    queries = jnp.concatenate([both, tm_permute(both, 0, 0, 1)], axis=0)

    scale = 128 ** (-0.5) * LOG2E
    step_of = functools.partial(attention_step, kinds, bases, queries)
    up = tm_permute(kv, 0, 1, 0)
    down = tm_permute(kv, 0, -1, 0)
    state = step_of([kv], bias, None, 0, False, scale)
    for step in range(1, Z // 2):
        next_up = tm_permute(up, 0, 1, 0)
        if step + 1 < Z // 2:
            next_down = tm_permute(down, 0, -1, 0)
        state = step_of([up, down], bias, state, 2 * step - 1, False, scale)
        up, down = next_up, next_down
    packed, out, lse = step_of([up], bias, state, Z - 1, True, scale)

    got = tm_permute(packed[2 * rows :], 0, 0, 1)
    send, keep, keep_lse = merge_core(out, lse, got, rows)
    got = tm_permute(send, 1, 0, 0)
    partial = merge_project(keep, keep_lse, got, w_out_t)
    heads = lax.axis_size("head")
    pieces = lax.all_to_all(
        partial.reshape(heads, rows // heads, width), "head", split_axis=0, concat_axis=0, tiled=True
    )
    return jnp.sum(pieces.astype(F32), axis=0).astype(BF16)


def solution(mesh):
    in_specs = (P("tm", None), P(), P(None, "tm", "head"), P("head"), P("head", "tm"))
    out_specs = P(("tm", "head"), None)
    return jax.shard_map(local, mesh=mesh, in_specs=in_specs, out_specs=out_specs, check_vma=False)
```

time: 288 us -> 151 us (0.52)
  waiting for transfers between devices: 126 us -> 26.6 us
  blocking collectives: 82.2 us -> 21 us
  Pallas kernels: 0 us -> 50.5 us
  matrix products: 49.7 us -> 0.76 us
  starting transfers between devices: 0.08 us -> 34.9 us
  between operations: 13.8 us -> 1.09 us
  other arithmetic: 15.4 us -> 8.62 us
  local copies, waits for them, and re-layouts: 0.7 us -> 5.59 us
    all_gather x2 -> x0, waiting for transfers between devices: 84.3 us -> none  [the longest x1 42.5 us: local(): lax.all_gather(valued, 'tm', axis=0, tiled=True)]
    all_gather x2 -> x0, blocking collectives: 82.2 us -> none  [the longest x1 44.3 us: local(): lax.all_gather(w_qkv, 'tm', axis=1, tiled=True)]
    pallas_call x0 -> x7, Pallas kernels: none -> 50.5 us  [the longest x5 44.9 us: attention_step(): pl.pallas_call(functools.partial(attention_kernel, shards, offset, first,...]
    dot_general x3 -> x1, matrix products: 49.7 us -> 0.76 us  [local(): projected = jnp.dot(normed, w_all, preferred_element_type=F32).astype(BF16)]
    reduce_scatter x1 -> x0, waiting for transfers between devices: 41.1 us -> none  [local(): lax.psum_scatter(jnp.dot(mixed, out_local, preferred_element_type=jnp.flo...]
    ppermute x0 -> x20, starting transfers between devices: none -> 34.9 us  [tm_permute(): return lax.ppermute(x, 'tm', pairs)]
    ppermute x0 -> x20, waiting for transfers between devices: none -> 26.6 us  [tm_permute(): return lax.ppermute(x, 'tm', pairs)]
    all_to_all x0 -> x1, blocking collectives: none -> 21 us  [local(): lax.all_to_all(partial.reshape(heads, rows // heads, width), 'head', spli...]
  transfers between devices with their start and end apart: 3 -> 20, of which waited for: 3 -> 10; matrix products, arithmetic and copies ran while one was open for 15% -> 5% of each run, Pallas kernels for 0% -> 25%
where the time goes in v1:
time: 151 us; the launch traced here: 149 us
  Pallas kernels  50.5 us (33%)
  starting transfers between devices  34.9 us (23%)
  waiting for transfers between devices  26.6 us (18%)
  blocking collectives  21 us (14%)
  other arithmetic  8.62 us (6%)
  local copies, waits for them, and re-layouts  5.59 us (4%)
    pallas_call x5, Pallas kernels, attention_step(): pl.pallas_call(functools.partial(attention_kernel, shards, offset, first,...  44.9 us
    ppermute x20, starting transfers between devices, tm_permute(): return lax.ppermute(x, 'tm', pairs)  34.9 us
    ppermute x20, waiting for transfers between devices, tm_permute(): return lax.ppermute(x, 'tm', pairs)  26.6 us
    all_to_all x1, blocking collectives, local(): lax.all_to_all(partial.reshape(heads, rows // heads, width), 'head', spli...  21 us
  transfers between devices with their start and end apart: 20, of which 10 were waited for; matrix products, arithmetic and copies ran while one was open for 5% of the time, Pallas kernels for 25%

profile of v1, /device:TPU:16, one launch (start us, length us, event | category | flops | bytes accessed | tf_op | source)
XLA Modules:
  0.0 149.1 jit_solution(11016227516716197241)
XLA Ops:
  0.0 0.8 pad_maximum_fusion.5
  0.8 5.9 %collective-permute-start = (bf16[128,128]{1,0:T(8,128)(2,1)S(1)}, bf16[128,128]{1,0:T(8,128)(2,1)S(1)}, u32[]{:S(2)}, u32[]{:S(2)}) collective-permute-start(bf16[128,128]{1,0:T(8,128)(2,1)S(1)} %pad_maximum_fusion.5), channel_id=1, source_target_pairs={{16,0},{24,8},{32,16},{40,24},{48,32},{56,40},{64,48},{72,56},{80,... | collective-permute-start | bytes 98312 | tf_op jit(solution)/shard_map/ppermute | solution.py:24
  6.7 0.0 collective-permute-start.1
  6.7 0.8 bitcast_dynamic-update-slice_fusion.7
  7.5 0.7 fusion.15
  8.3 0.0 collective-permute-done
  8.4 3.5 %collective-permute-start.2 = (bf16[128,128]{1,0:T(8,128)(2,1)S(1)}, bf16[128,128]{1,0:T(8,128)(2,1)S(1)}, u32[]{:S(2)}, u32[]{:S(2)}) collective-permute-start(bf16[128,128]{1,0:T(8,128)(2,1)S(1)} %collective-permute-done), channel_id=1, source_target_pairs={{16,0},{24,8},{32,16},{40,24},{48,32},{56,40},{64,48},{72,56},{80,... | collective-permute-start | bytes 98312 | tf_op jit(solution)/shard_map/ppermute | solution.py:24
  11.9 1.6 %collective-permute-done.2 = bf16[128,128]{1,0:T(8,128)(2,1)S(1)} collective-permute-done((bf16[128,128]{1,0:T(8,128)(2,1)S(1)}, bf16[128,128]{1,0:T(8,128)(2,1)S(1)}, u32[]{:S(2)}, u32[]{:S(2)}) %collective-permute-start.2) | collective-permute-done | bytes 32800 | tf_op jit(solution)/shard_map/ppermute | solution.py:24
  13.4 3.5 %collective-permute-start.4 = (bf16[128,128]{1,0:T(8,128)(2,1)S(1)}, bf16[128,128]{1,0:T(8,128)(2,1)S(1)}, u32[]{:S(2)}, u32[]{:S(2)}) collective-permute-start(bf16[128,128]{1,0:T(8,128)(2,1)S(1)} %collective-permute-done.2), channel_id=1, source_target_pairs={{16,0},{24,8},{32,16},{40,24},{48,32},{56,40},{64,48},{72,56},{80,... | collective-permute-start | bytes 98312 | tf_op jit(solution)/shard_map/ppermute | solution.py:24
  17.0 0.0 collective-permute-done.3
  17.0 1.6 %collective-permute-done.4 = bf16[128,128]{1,0:T(8,128)(2,1)S(1)} collective-permute-done((bf16[128,128]{1,0:T(8,128)(2,1)S(1)}, bf16[128,128]{1,0:T(8,128)(2,1)S(1)}, u32[]{:S(2)}, u32[]{:S(2)}) %collective-permute-start.4) | collective-permute-done | bytes 32800 | tf_op jit(solution)/shard_map/ppermute | solution.py:24
  18.6 3.5 %collective-permute-start.6 = (bf16[128,128]{1,0:T(8,128)(2,1)S(1)}, bf16[128,128]{1,0:T(8,128)(2,1)S(1)}, u32[]{:S(2)}, u32[]{:S(2)}) collective-permute-start(bf16[128,128]{1,0:T(8,128)(2,1)S(1)} %collective-permute-done.4), channel_id=1, source_target_pairs={{16,0},{24,8},{32,16},{40,24},{48,32},{56,40},{64,48},{72,56},{80,... | collective-permute-start | bytes 98312 | tf_op jit(solution)/shard_map/ppermute | solution.py:24
  22.1 1.6 %collective-permute-done.6 = bf16[128,128]{1,0:T(8,128)(2,1)S(1)} collective-permute-done((bf16[128,128]{1,0:T(8,128)(2,1)S(1)}, bf16[128,128]{1,0:T(8,128)(2,1)S(1)}, u32[]{:S(2)}, u32[]{:S(2)}) %collective-permute-start.6) | collective-permute-done | bytes 32800 | tf_op jit(solution)/shard_map/ppermute | solution.py:24
  23.7 0.3 collective-permute-start.7
  24.0 0.1 broadcast_subtract_fusion
  24.1 0.1 sub.81
  24.8 0.5 fusion.17
  25.3 6.2 %collective-permute-done.7 = bf16[8,128,128]{2,1,0:T(8,128)(2,1)S(1)} collective-permute-done((bf16[8,128,128]{2,1,0:T(8,128)(2,1)S(1)}, bf16[8,128,128]{2,1,0:T(8,128)(2,1)S(1)}, u32[]{:S(2)}, u32[]{:S(2)}) %collective-permute-start.7) | collective-permute-done | bytes 262176 | tf_op jit(solution)/shard_map/ppermute | solution.py:24
  31.6 0.1 pad_maximum_fusion.2
  31.7 0.1 collective-permute-start.8
  31.8 0.3 fusion
  32.1 0.5 compare_select_fusion.10.refs_0_
  32.6 1.1 collective-permute-done.8
  33.7 0.1 select_bitcast_fusion.1
  33.7 0.1 pad_maximum_fusion.1
  33.9 0.0 copy-start.11
  33.9 0.1 slice_bitcast_fusion
  33.9 0.5 copy.8
  34.5 0.1 copy-done.11
  34.5 0.8 convolution_convert_fusion
  35.3 0.4 collective-permute-start.9
  35.8 0.3 convert_multiply_fusion.2
  36.1 3.6 %collective-permute-start.11 = (bf16[512,256]{1,0:T(8,128)(2,1)S(1)}, bf16[512,256]{1,0:T(8,128)(2,1)S(1)}, u32[]{:S(2)}, u32[]{:S(2)}) collective-permute-start(bf16[512,256]{1,0:T(8,128)(2,1)S(1)} %slice.22.refs_3_), channel_id=1, source_target_pairs={{16,0},{24,8},{32,16},{40,24},{48,32},{56,40},{64,48},{72,56},{80,... | collective-permute-start | bytes 786440 | tf_op jit(solution)/shard_map/ppermute | solution.py:24
  39.7 2.8 %collective-permute-done.9 = bf16[512,128]{1,0:T(8,128)(2,1)S(1)} collective-permute-done((bf16[512,128]{1,0:T(8,128)(2,1)S(1)}, bf16[512,128]{1,0:T(8,128)(2,1)S(1)}, u32[]{:S(2)}, u32[]{:S(2)}) %collective-permute-start.9) | collective-permute-done | bytes 131104 | tf_op jit(solution)/shard_map/ppermute | solution.py:24
  42.5 0.1 collective-permute-start.10
  42.6 0.3 fusion.7
  42.9 2.4 %collective-permute-done.11.refs_3_ = bf16[512,256]{1,0:T(8,128)(2,1)S(1)} collective-permute-done((bf16[512,256]{1,0:T(8,128)(2,1)S(1)}, bf16[512,256]{1,0:T(8,128)(2,1)S(1)}, u32[]{:S(2)}, u32[]{:S(2)}) %collective-permute-start.11) | collective-permute-done | bytes 262176 | tf_op jit(solution)/shard_map/ppermute | solution.py:24
  45.3 3.7 %collective-permute-start.12 = (bf16[512,256]{1,0:T(8,128)(2,1)S(1)}, bf16[512,256]{1,0:T(8,128)(2,1)S(1)}, u32[]{:S(2)}, u32[]{:S(2)}) collective-permute-start(bf16[512,256]{1,0:T(8,128)(2,1)S(1)} %collective-permute-done.11.refs_3_), channel_id=1, source_target_pairs={{16,0},{24,8},{32,16},{40,24},{48,32},{56,40},{64,48},{72,56},{80,... | collective-permute-start | bytes 786440 | tf_op jit(solution)/shard_map/ppermute | solution.py:24
  49.0 2.4 %pad_maximum_fusion.refs_4_.refs_5_.refs_6_ = f32[4,512,512]{2,1,0:T(8,128)} fusion(f32[1,512,512]{2,1,0:T(8,128)S(1)} %get-tuple-element.40, f32[1,512,512]{2,1,0:T(8,128)S(1)} %get-tuple-element.42, f32[1,512,512]{2,1,0:T(8,128)S(1)} %get-tuple-element.39, f32[1,512,512]{2,1,0:T(8,128)S(1)} %get-tuple-element.41), kind=kLoop, calls=%fused_computation | loop fusion | flops 3145728 | bytes 8388608 | tf_op jit(solution)/shard_map/stack | solution.py:239
  51.4 0.1 collective-permute-start.16
  51.5 0.8 pad_maximum_fusion.3.refs_2_
  52.3 1.4 collective-permute-done.12.refs_3_
  53.7 3.7 %collective-permute-start.13 = (bf16[512,256]{1,0:T(8,128)(2,1)S(1)}, bf16[512,256]{1,0:T(8,128)(2,1)S(1)}, u32[]{:S(2)}, u32[]{:S(2)}) collective-permute-start(bf16[512,256]{1,0:T(8,128)(2,1)S(1)} %collective-permute-done.12.refs_3_), channel_id=1, source_target_pairs={{16,0},{24,8},{32,16},{40,24},{48,32},{56,40},{64,48},{72,56},{80,... | collective-permute-start | bytes 786440 | tf_op jit(solution)/shard_map/ppermute | solution.py:24
  57.4 6.6 %shard_map.64 = (f32[2048,128]{1,0:T(8,128)}, f32[2048,256]{1,0:T(8,128)}) custom-call(s32[32]{0:T(128)} %compare_select_fusion.10.refs_0_, f32[32]{0:T(128)} %get-tuple-element.33.refs_1_, bf16[2048,128]{1,0:T(8,128)(2,1)} %pad_maximum_fusion.3.refs_2_, bf16[512,256]{1,0:T(8,128)(2,1)} %copy-done.1, f32[4,512,512]{2,1,0:T(8,128)} %pad_maximum_fusion.refs_4_.refs_5_.refs_6_), custom_call_target="tpu_custom_call" | custom-call | flops 1073741824 | bytes 6553600 | tf_op jit(solution)/shard_map/pallas_call | solution.py:124
  64.0 0.1 collective-permute-start.17
  64.1 10.2 %shard_map.65 = (f32[2048,128]{1,0:T(8,128)}, f32[2048,256]{1,0:T(8,128)}) custom-call(s32[32]{0:T(128)} %compare_select_fusion.10.refs_0_, f32[32]{0:T(128)} %get-tuple-element.33.refs_1_, bf16[2048,128]{1,0:T(8,128)(2,1)} %pad_maximum_fusion.3.refs_2_, bf16[512,256]{1,0:T(8,128)(2,1)} %copy-done.3, bf16[512,256]{1,0:T(8,128)(2,1)} %copy-done.4, ...), custom_call_target="tpu_custom_call" | custom-call | flops 2147483648 | bytes 6815744 | tf_op jit(solution)/shard_map/pallas_call | solution.py:124
  74.3 3.1 %collective-permute-start.14 = (bf16[512,256]{1,0:T(8,128)(2,1)S(1)}, bf16[512,256]{1,0:T(8,128)(2,1)S(1)}, u32[]{:S(2)}, u32[]{:S(2)}) collective-permute-start(bf16[512,256]{1,0:T(8,128)(2,1)S(1)} %collective-permute-done.13.refs_3_), channel_id=1, source_target_pairs={{16,0},{24,8},{32,16},{40,24},{48,32},{56,40},{64,48},{72,56},{80,... | collective-permute-start | bytes 786440 | tf_op jit(solution)/shard_map/ppermute | solution.py:24
  77.5 10.1 %shard_map.66 = (f32[2048,128]{1,0:T(8,128)}, f32[2048,256]{1,0:T(8,128)}) custom-call(s32[32]{0:T(128)} %compare_select_fusion.10.refs_0_, f32[32]{0:T(128)} %get-tuple-element.33.refs_1_, bf16[2048,128]{1,0:T(8,128)(2,1)} %pad_maximum_fusion.3.refs_2_, bf16[512,256]{1,0:T(8,128)(2,1)} %copy-done.5, bf16[512,256]{1,0:T(8,128)(2,1)} %copy-done.6, ...), custom_call_target="tpu_custom_call" | custom-call | flops 2147483648 | bytes 6815744 | tf_op jit(solution)/shard_map/pallas_call | solution.py:124
  87.6 0.7 copy-done.9
  88.3 10.2 %shard_map.67 = (f32[2048,128]{1,0:T(8,128)}, f32[2048,256]{1,0:T(8,128)}) custom-call(s32[32]{0:T(128)} %compare_select_fusion.10.refs_0_, f32[32]{0:T(128)} %get-tuple-element.33.refs_1_, bf16[2048,128]{1,0:T(8,128)(2,1)} %pad_maximum_fusion.3.refs_2_, bf16[512,256]{1,0:T(8,128)(2,1)} %copy-done.7, bf16[512,256]{1,0:T(8,128)(2,1)} %copy-done.9, ...), custom_call_target="tpu_custom_call" | custom-call | flops 2147483648 | bytes 6815744 | tf_op jit(solution)/shard_map/pallas_call | solution.py:124
  98.5 0.7 copy-done.8
  99.2 7.8 %shard_map.68 = (bf16[2048,256]{1,0:T(8,128)(2,1)}, f32[2048,128]{1,0:T(8,128)}, f32[2048,128]{1,0:T(8,128)}) custom-call(s32[32]{0:T(128)} %compare_select_fusion.10.refs_0_, f32[32]{0:T(128)} %get-tuple-element.33.refs_1_, bf16[2048,128]{1,0:T(8,128)(2,1)} %pad_maximum_fusion.3.refs_2_, bf16[512,256]{1,0:T(8,128)(2,1)} %copy-done.8, ...), custom_call_target="tpu_custom_call" | custom-call | flops 1073741824 | bytes 6553600 | tf_op jit(solution)/shard_map/pallas_call | solution.py:124
  106.9 1.1 slice.18
  108.0 0.1 collective-permute-start.18
  108.1 1.9 %collective-permute-done.18.got_ref = bf16[1024,256]{1,0:T(8,128)(2,1)S(1)} collective-permute-done((bf16[1024,256]{1,0:T(8,128)(2,1)S(1)}, bf16[1024,256]{1,0:T(8,128)(2,1)S(1)}, u32[]{:S(2)}, u32[]{:S(2)}) %collective-permute-start.18) | collective-permute-done | bytes 524320 | tf_op jit(solution)/shard_map/ppermute | solution.py:24
  110.0 0.8 copy-done.2
  110.8 2.8 %shard_map.69 = (bf16[512,256]{1,0:T(8,128)(2,1)}, f32[512,128]{1,0:T(8,128)}, f32[512,128]{1,0:T(8,128)}) custom-call(f32[2048,128]{1,0:T(8,128)} %get-tuple-element.27.out_ref, f32[2048,128]{1,0:T(8,128)} %get-tuple-element.28.lse_ref, bf16[1024,256]{1,0:T(8,128)(2,1)} %copy-done.2), custom_call_target="tpu_custom_call" | custom-call | tf_op jit(solution)/shard_map/pallas_call | solution.py:166
  113.6 3.2 %collective-permute-start.19 = (bf16[512,256]{1,0:T(8,128)(2,1)}, bf16[512,256]{1,0:T(8,128)(2,1)S(1)}, u32[]{:S(2)}, u32[]{:S(2)}) collective-permute-start(bf16[512,256]{1,0:T(8,128)(2,1)} %get-tuple-element.32), channel_id=1, source_target_pairs={{128,0},{136,8},{144,16},{152,24},{160,32},{168,40},{176,48},{184,... | collective-permute-start | bytes 786440 | tf_op jit(solution)/shard_map/ppermute | solution.py:24
  116.8 0.7 slice.23
  117.5 6.2 %collective-permute-done.19.got_ref = bf16[512,256]{1,0:T(8,128)(2,1)S(1)} collective-permute-done((bf16[512,256]{1,0:T(8,128)(2,1)}, bf16[512,256]{1,0:T(8,128)(2,1)S(1)}, u32[]{:S(2)}, u32[]{:S(2)}) %collective-permute-start.19) | collective-permute-done | bytes 262176 | tf_op jit(solution)/shard_map/ppermute | solution.py:24
  123.7 0.7 copy-done.10
  124.4 2.9 %shard_map.70 = bf16[512,1024]{1,0:T(8,128)(2,1)} custom-call(f32[512,128]{1,0:T(8,128)} %get-tuple-element.30.out_ref, f32[512,128]{1,0:T(8,128)} %get-tuple-element.31.lse_ref, bf16[512,256]{1,0:T(8,128)(2,1)} %copy-done.10, bf16[1024,128]{1,0:T(8,128)(2,1)} %bitcast.44), custom_call_target="tpu_custom_call" | custom-call | tf_op jit(solution)/shard_map/pallas_call | solution.py:197
  127.2 21.0 %all_to_all.5 = bf16[8,64,1024]{2,1,0:T(8,128)(2,1)S(1)} all-to-all(bf16[8,64,1024]{2,1,0:T(8,128)(2,1)} %bitcast.42), channel_id=1, replica_groups=mesh['tm'=32,'head'=8] {'head'}, dimensions={0} | all-to-all | bytes 2097152 | tf_op jit(solution)/shard_map/all_to_all | solution.py:274
  148.2 0.8 reduce_sum.22
  (43 shorter events, 0.3 us)
Async XLA Ops:
  0.0 31.8 %copy-start = (bf16[512,1024]{1,0:T(8,128)(2,1)S(1)}, bf16[512,1024]{1,0:T(8,128)(2,1)}, u32[]{:S(2)}) copy-start(bf16[512,1024]{1,0:T(8,128)(2,1)} %param.6) | copy-start | bytes 3145732
  0.8 7.5 %collective-permute-start = (bf16[128,128]{1,0:T(8,128)(2,1)S(1)}, bf16[128,128]{1,0:T(8,128)(2,1)S(1)}, u32[]{:S(2)}, u32[]{:S(2)}) collective-permute-start(bf16[128,128]{1,0:T(8,128)(2,1)S(1)} %pad_maximum_fusion.5), channel_id=1, source_target_pairs={{16,0},{24,8},{32,16},{40,24},{48,32},{56,40},{64,48},{72,56},{80,... | collective-permute-start | bytes 98312 | tf_op jit(solution)/shard_map/ppermute | solution.py:24
  6.7 5.1 %collective-permute-start.1 = (bf16[128,128]{1,0:T(8,128)(2,1)S(1)}, bf16[128,128]{1,0:T(8,128)(2,1)S(1)}, u32[]{:S(2)}, u32[]{:S(2)}) collective-permute-start(bf16[128,128]{1,0:T(8,128)(2,1)S(1)} %pad_maximum_fusion.5), channel_id=1, source_target_pairs={{112,0},{120,8},{0,16},{8,24},{16,32},{24,40},{32,48},{40,56},{48,... | collective-permute-start | bytes 98312 | tf_op jit(solution)/shard_map/ppermute | solution.py:24
  8.4 5.1 %collective-permute-start.2 = (bf16[128,128]{1,0:T(8,128)(2,1)S(1)}, bf16[128,128]{1,0:T(8,128)(2,1)S(1)}, u32[]{:S(2)}, u32[]{:S(2)}) collective-permute-start(bf16[128,128]{1,0:T(8,128)(2,1)S(1)} %collective-permute-done), channel_id=1, source_target_pairs={{16,0},{24,8},{32,16},{40,24},{48,32},{56,40},{64,48},{72,56},{80,... | collective-permute-start | bytes 98312 | tf_op jit(solution)/shard_map/ppermute | solution.py:24
  11.8 5.1 %collective-permute-start.3 = (bf16[128,128]{1,0:T(8,128)(2,1)S(1)}, bf16[128,128]{1,0:T(8,128)(2,1)S(1)}, u32[]{:S(2)}, u32[]{:S(2)}) collective-permute-start(bf16[128,128]{1,0:T(8,128)(2,1)S(1)} %collective-permute-done.1), channel_id=1, source_target_pairs={{112,0},{120,8},{0,16},{8,24},{16,32},{24,40},{32,48},{40,56},{48,... | collective-permute-start | bytes 98312 | tf_op jit(solution)/shard_map/ppermute | solution.py:24
  13.4 5.1 %collective-permute-start.4 = (bf16[128,128]{1,0:T(8,128)(2,1)S(1)}, bf16[128,128]{1,0:T(8,128)(2,1)S(1)}, u32[]{:S(2)}, u32[]{:S(2)}) collective-permute-start(bf16[128,128]{1,0:T(8,128)(2,1)S(1)} %collective-permute-done.2), channel_id=1, source_target_pairs={{16,0},{24,8},{32,16},{40,24},{48,32},{56,40},{64,48},{72,56},{80,... | collective-permute-start | bytes 98312 | tf_op jit(solution)/shard_map/ppermute | solution.py:24
  17.0 5.1 %collective-permute-start.5 = (bf16[128,128]{1,0:T(8,128)(2,1)S(1)}, bf16[128,128]{1,0:T(8,128)(2,1)S(1)}, u32[]{:S(2)}, u32[]{:S(2)}) collective-permute-start(bf16[128,128]{1,0:T(8,128)(2,1)S(1)} %collective-permute-done.3), channel_id=1, source_target_pairs={{112,0},{120,8},{0,16},{8,24},{16,32},{24,40},{32,48},{40,56},{48,... | collective-permute-start | bytes 98312 | tf_op jit(solution)/shard_map/ppermute | solution.py:24
  18.6 5.1 %collective-permute-start.6 = (bf16[128,128]{1,0:T(8,128)(2,1)S(1)}, bf16[128,128]{1,0:T(8,128)(2,1)S(1)}, u32[]{:S(2)}, u32[]{:S(2)}) collective-permute-start(bf16[128,128]{1,0:T(8,128)(2,1)S(1)} %collective-permute-done.4), channel_id=1, source_target_pairs={{16,0},{24,8},{32,16},{40,24},{48,32},{56,40},{64,48},{72,56},{80,... | collective-permute-start | bytes 98312 | tf_op jit(solution)/shard_map/ppermute | solution.py:24
  23.7 7.9 %collective-permute-start.7 = (bf16[8,128,128]{2,1,0:T(8,128)(2,1)S(1)}, bf16[8,128,128]{2,1,0:T(8,128)(2,1)S(1)}, u32[]{:S(2)}, u32[]{:S(2)}) collective-permute-start(bf16[8,128,128]{2,1,0:T(8,128)(2,1)S(1)} %bitcast_dynamic-update-slice_fusion), channel_id=1, source_target_pairs={{128,0},{136,8},{144,16},{152,24},{160,32},{168,40},{176,48},{184,... | collective-permute-start | bytes 786440 | tf_op jit(solution)/shard_map/ppermute | solution.py:24
  31.7 2.0 %collective-permute-start.8 = (bf16[2,8,128,128]{3,2,1,0:T(8,128)(2,1)S(1)}, bf16[2,8,128,128]{3,2,1,0:T(8,128)(2,1)S(1)}, u32[]{:S(2)}, u32[]{:S(2)}) collective-permute-start(bf16[2,8,128,128]{3,2,1,0:T(8,128)(2,1)S(1)} %pad_maximum_fusion.2), channel_id=1, source_target_pairs={{8,0},{0,8},{24,16},{16,24},{40,32},{32,40},{56,48},{48,56},{72,64... | collective-permute-start | bytes 1572872 | tf_op jit(solution)/shard_map/ppermute | solution.py:24
  33.9 0.7 copy-start.11
  35.3 7.1 %collective-permute-start.9 = (bf16[512,128]{1,0:T(8,128)(2,1)S(1)}, bf16[512,128]{1,0:T(8,128)(2,1)S(1)}, u32[]{:S(2)}, u32[]{:S(2)}) collective-permute-start(bf16[512,128]{1,0:T(8,128)(2,1)S(1)} %slice.21), channel_id=1, source_target_pairs={{128,0},{136,8},{144,16},{152,24},{160,32},{168,40},{176,48},{184,... | collective-permute-start | bytes 393224 | tf_op jit(solution)/shard_map/ppermute | solution.py:24
  36.1 15.3 %copy-start.1 = (bf16[512,256]{1,0:T(8,128)(2,1)}, bf16[512,256]{1,0:T(8,128)(2,1)S(1)}, u32[]{:S(2)}) copy-start(bf16[512,256]{1,0:T(8,128)(2,1)S(1)} %slice.22.refs_3_) | copy-start | bytes 786436
  36.1 9.2 %collective-permute-start.11 = (bf16[512,256]{1,0:T(8,128)(2,1)S(1)}, bf16[512,256]{1,0:T(8,128)(2,1)S(1)}, u32[]{:S(2)}, u32[]{:S(2)}) collective-permute-start(bf16[512,256]{1,0:T(8,128)(2,1)S(1)} %slice.22.refs_3_), channel_id=1, source_target_pairs={{16,0},{24,8},{32,16},{40,24},{48,32},{56,40},{64,48},{72,56},{80,... | collective-permute-start | bytes 786440 | tf_op jit(solution)/shard_map/ppermute | solution.py:24
  39.7 11.7 %collective-permute-start.15 = (bf16[512,256]{1,0:T(8,128)(2,1)S(1)}, bf16[512,256]{1,0:T(8,128)(2,1)S(1)}, u32[]{:S(2)}, u32[]{:S(2)}) collective-permute-start(bf16[512,256]{1,0:T(8,128)(2,1)S(1)} %slice.22.refs_3_), channel_id=1, source_target_pairs={{112,0},{120,8},{0,16},{8,24},{16,32},{24,40},{32,48},{40,56},{48,... | collective-permute-start | bytes 786440 | tf_op jit(solution)/shard_map/ppermute | solution.py:24
  42.5 9.0 %collective-permute-start.10 = (bf16[1024,128]{1,0:T(8,128)(2,1)S(1)}, bf16[1024,128]{1,0:T(8,128)(2,1)S(1)}, u32[]{:S(2)}, u32[]{:S(2)}) collective-permute-start(bf16[1024,128]{1,0:T(8,128)(2,1)S(1)} %pad_maximum_fusion.4), channel_id=1, source_target_pairs={{8,0},{0,8},{24,16},{16,24},{40,32},{32,40},{56,48},{48,56},{72,64... | collective-permute-start | bytes 786440 | tf_op jit(solution)/shard_map/ppermute | solution.py:24
  45.3 6.1 %copy-start.3 = (bf16[512,256]{1,0:T(8,128)(2,1)}, bf16[512,256]{1,0:T(8,128)(2,1)S(1)}, u32[]{:S(2)}) copy-start(bf16[512,256]{1,0:T(8,128)(2,1)S(1)} %collective-permute-done.11.refs_3_) | copy-start | bytes 786436
  45.3 8.4 %collective-permute-start.12 = (bf16[512,256]{1,0:T(8,128)(2,1)S(1)}, bf16[512,256]{1,0:T(8,128)(2,1)S(1)}, u32[]{:S(2)}, u32[]{:S(2)}) collective-permute-start(bf16[512,256]{1,0:T(8,128)(2,1)S(1)} %collective-permute-done.11.refs_3_), channel_id=1, source_target_pairs={{16,0},{24,8},{32,16},{40,24},{48,32},{56,40},{64,48},{72,56},{80,... | collective-permute-start | bytes 786440 | tf_op jit(solution)/shard_map/ppermute | solution.py:24
  51.4 12.6 %copy-start.4 = (bf16[512,256]{1,0:T(8,128)(2,1)}, bf16[512,256]{1,0:T(8,128)(2,1)S(1)}, u32[]{:S(2)}) copy-start(bf16[512,256]{1,0:T(8,128)(2,1)S(1)} %collective-permute-done.15.refs_4_) | copy-start | bytes 786436
  51.4 12.6 %collective-permute-start.16 = (bf16[512,256]{1,0:T(8,128)(2,1)S(1)}, bf16[512,256]{1,0:T(8,128)(2,1)S(1)}, u32[]{:S(2)}, u32[]{:S(2)}) collective-permute-start(bf16[512,256]{1,0:T(8,128)(2,1)S(1)} %collective-permute-done.15.refs_4_), channel_id=1, source_target_pairs={{112,0},{120,8},{0,16},{8,24},{16,32},{24,40},{32,48},{40,56},{48,... | collective-permute-start | bytes 786440 | tf_op jit(solution)/shard_map/ppermute | solution.py:24
  53.7 10.3 %copy-start.5 = (bf16[512,256]{1,0:T(8,128)(2,1)}, bf16[512,256]{1,0:T(8,128)(2,1)S(1)}, u32[]{:S(2)}) copy-start(bf16[512,256]{1,0:T(8,128)(2,1)S(1)} %collective-permute-done.12.refs_3_) | copy-start | bytes 786436
  53.7 20.6 %collective-permute-start.13 = (bf16[512,256]{1,0:T(8,128)(2,1)S(1)}, bf16[512,256]{1,0:T(8,128)(2,1)S(1)}, u32[]{:S(2)}, u32[]{:S(2)}) collective-permute-start(bf16[512,256]{1,0:T(8,128)(2,1)S(1)} %collective-permute-done.12.refs_3_), channel_id=1, source_target_pairs={{16,0},{24,8},{32,16},{40,24},{48,32},{56,40},{64,48},{72,56},{80,... | collective-permute-start | bytes 786440 | tf_op jit(solution)/shard_map/ppermute | solution.py:24
  64.0 10.3 %copy-start.6 = (bf16[512,256]{1,0:T(8,128)(2,1)}, bf16[512,256]{1,0:T(8,128)(2,1)S(1)}, u32[]{:S(2)}) copy-start(bf16[512,256]{1,0:T(8,128)(2,1)S(1)} %collective-permute-done.16.refs_4_) | copy-start | bytes 786436
  64.0 23.6 %collective-permute-start.17 = (bf16[512,256]{1,0:T(8,128)(2,1)S(1)}, bf16[512,256]{1,0:T(8,128)(2,1)S(1)}, u32[]{:S(2)}, u32[]{:S(2)}) collective-permute-start(bf16[512,256]{1,0:T(8,128)(2,1)S(1)} %collective-permute-done.16.refs_4_), channel_id=1, source_target_pairs={{112,0},{120,8},{0,16},{8,24},{16,32},{24,40},{32,48},{40,56},{48,... | collective-permute-start | bytes 786440 | tf_op jit(solution)/shard_map/ppermute | solution.py:24
  74.3 13.3 %copy-start.7 = (bf16[512,256]{1,0:T(8,128)(2,1)}, bf16[512,256]{1,0:T(8,128)(2,1)S(1)}, u32[]{:S(2)}) copy-start(bf16[512,256]{1,0:T(8,128)(2,1)S(1)} %collective-permute-done.13.refs_3_) | copy-start | bytes 786436
  74.3 24.1 %collective-permute-start.14 = (bf16[512,256]{1,0:T(8,128)(2,1)S(1)}, bf16[512,256]{1,0:T(8,128)(2,1)S(1)}, u32[]{:S(2)}, u32[]{:S(2)}) collective-permute-start(bf16[512,256]{1,0:T(8,128)(2,1)S(1)} %collective-permute-done.13.refs_3_), channel_id=1, source_target_pairs={{16,0},{24,8},{32,16},{40,24},{48,32},{56,40},{64,48},{72,56},{80,... | collective-permute-start | bytes 786440 | tf_op jit(solution)/shard_map/ppermute | solution.py:24
  87.6 0.7 copy-start.9
  98.5 0.7 copy-start.8
  108.0 2.0 %collective-permute-start.18 = (bf16[1024,256]{1,0:T(8,128)(2,1)S(1)}, bf16[1024,256]{1,0:T(8,128)(2,1)S(1)}, u32[]{:S(2)}, u32[]{:S(2)}) collective-permute-start(bf16[1024,256]{1,0:T(8,128)(2,1)S(1)} %slice.18), channel_id=1, source_target_pairs={{8,0},{0,8},{24,16},{16,24},{40,32},{32,40},{56,48},{48,56},{72,64... | collective-permute-start | bytes 1572872 | tf_op jit(solution)/shard_map/ppermute | solution.py:24
  110.0 0.8 copy-start.2
  113.6 10.1 %collective-permute-start.19 = (bf16[512,256]{1,0:T(8,128)(2,1)}, bf16[512,256]{1,0:T(8,128)(2,1)S(1)}, u32[]{:S(2)}, u32[]{:S(2)}) collective-permute-start(bf16[512,256]{1,0:T(8,128)(2,1)} %get-tuple-element.32), channel_id=1, source_target_pairs={{128,0},{136,8},{144,16},{152,24},{160,32},{168,40},{176,48},{184,... | collective-permute-start | bytes 786440 | tf_op jit(solution)/shard_map/ppermute | solution.py:24
  123.7 0.7 copy-start.10

commit v2 on v1

--- a/solution.py
+++ b/solution.py
@@ -22,6 +22,53 @@
                 source = ((yh + d_yh) % YH * Z + (z + d_z) % Z) * CORE + (core + d_core) % CORE
                 pairs.append((source, (yh * Z + z) * CORE + core))
     return lax.ppermute(x, "tm", pairs)
+
+
+def ring_permute(x):
+    pairs = []
+    for yh in range(YH):
+        for z in range(Z):
+            for core in range(CORE):
+                ahead = 1 if core == 0 else -1
+                pairs.append(((yh * Z + (z + ahead) % Z) * CORE + core, (yh * Z + z) * CORE + core))
+    return lax.ppermute(x, "tm", pairs)
+
+
+def project_kernel(mine_ref, other_ref, w_ref, query_ref, kv_ref):
+    block = pl.program_id(0)
+
+    def project(ref):
+        query_ref[...] = jnp.dot(ref[...], w_ref[:, :128], preferred_element_type=F32).astype(BF16)
+
+        @pl.when(block % 2 == 0)
+        def _():
+            kv_ref[...] = jnp.dot(ref[...], w_ref[:, 128:], preferred_element_type=F32).astype(BF16)
+
+    @pl.when(block < 2)
+    def _():
+        project(mine_ref)
+
+    @pl.when(block >= 2)
+    def _():
+        project(other_ref)
+
+
+def project(mine, other, w_all, rows):
+    width = mine.shape[1]
+    return pl.pallas_call(
+        project_kernel,
+        out_shape=[jax.ShapeDtypeStruct((4 * rows, 128), BF16), jax.ShapeDtypeStruct((2 * rows, 256), BF16)],
+        grid=(4,),
+        in_specs=[
+            pl.BlockSpec((rows, width), lambda i: (jnp.minimum(i, 1), 0)),
+            pl.BlockSpec((rows, width), lambda i: (jnp.maximum(i - 2, 0), 0)),
+            pl.BlockSpec((width, 384), lambda i: (0, 0)),
+        ],
+        out_specs=[
+            pl.BlockSpec((rows, 128), lambda i: (i, 0)),
+            pl.BlockSpec((rows, 256), lambda i: (i // 2, 0)),
+        ],
+    )(mine, other, w_all)
 
 
 def split_bf16(x):
@@ -88,28 +135,32 @@
         if last:
             norm = total[:, :128] / total[:, 128:]
             lse = peak + jnp.log2(total[:, 128:])
-            out_refs[0][here, :] = pack_partial(norm, lse)
-            out_refs[1][here, :] = norm
-            out_refs[2][here, :] = lse
+
+            @pl.when(block < 2)
+            def _(norm=norm, lse=lse, here=here):
+                out_refs[1][here, :] = norm
+                out_refs[2][here, :] = lse
+
+            @pl.when(block >= 2)
+            def _(norm=norm, lse=lse, here=here):
+                out_refs[0][here, :] = pack_partial(norm, lse)
         else:
             out_refs[0][here, :] = peak
             out_refs[1][here, :] = total
 
 
-def attention_step(kinds, bases, query, kvs, bias, state, first_shard, last, scale):
-    shards = len(kvs)
+def attention_step(kinds, bases, query, bias, kv, shards, state, first_shard, last, scale):
     total_rows = query.shape[0]
-    keys = kvs[0].shape[0]
-    rows = bias.shape[1]
+    rows = keys = bias.shape[1]
     first = state is None
     offset = 4 * first_shard
     in_specs = [pl.BlockSpec((rows, 128), lambda i, kind, base: (i, 0))]
-    in_specs += [pl.BlockSpec((keys, 256), lambda i, kind, base: (0, 0)) for _ in kvs]
+    in_specs += [pl.BlockSpec((keys, 256), lambda i, kind, base, j=j: (j, 0)) for j in range(shards)]
     for j in range(shards):
         in_specs.append(
             pl.BlockSpec((1, rows, keys), lambda i, kind, base, j=j: (kind[offset + 4 * j + i], 0, 0))
         )
-    args = [kinds, bases, query, *kvs] + [bias] * shards
+    args = [kinds, bases, query] + [kv] * shards + [bias] * shards
     if not first:
         in_specs += [
             pl.BlockSpec((rows, 128), lambda i, kind, base: (i, 0)),
@@ -117,10 +168,15 @@
         ]
         args += list(state)
     if last:
-        shapes = [((total_rows, 256), BF16), ((total_rows, 128), F32), ((total_rows, 128), F32)]
+        half = total_rows // 2
+        shapes = [((half, 256), BF16), ((half, 128), F32), ((half, 128), F32)]
+        late = lambda i, kind, base: (jnp.maximum(i - 2, 0), 0)
+        early = lambda i, kind, base: (jnp.minimum(i, 1), 0)
+        where = [late, early, early]
     else:
         shapes = [((total_rows, 128), F32), ((total_rows, 256), F32)]
-    out_specs = [pl.BlockSpec((rows, s[1]), lambda i, kind, base: (i, 0)) for s, _ in shapes]
+        where = [lambda i, kind, base: (i, 0)] * 2
+    out_specs = [pl.BlockSpec((rows, s[1]), index) for (s, _), index in zip(shapes, where)]
     return pl.pallas_call(
         functools.partial(attention_kernel, shards, offset, first, last, scale),
         out_shape=[jax.ShapeDtypeStruct(s, t) for s, t in shapes],
@@ -205,6 +261,29 @@
     me = lax.axis_index("tm")
     core, z, yh = me % CORE, me // CORE % Z, me // (CORE * Z)
 
+    wide = frames.astype(F32)
+    mean_square = jnp.mean(wide * wide, axis=-1, keepdims=True)
+    normed = (wide * lax.rsqrt(mean_square + 1e-06) * norm_gain).astype(BF16)
+    mine = jnp.concatenate([normed, tm_permute(normed, 1, 0, 0)], axis=0)
+    other = tm_permute(mine, 0, 0, 1)
+
+    slope = slopes[0] * LOG2E
+    spot = jnp.arange(rows, dtype=jnp.int32)
+    rise = (spot[None, :] - spot[:, None]).astype(F32) * slope
+    apart = jnp.abs(rise)
+    bias = jnp.stack([-rise, rise, -apart, apart])
+    ahead = 1 - 2 * core
+    far = jnp.array([0, 1, 1, 2, 2, 3, 3, 4], jnp.int32)
+    flip = jnp.array([0, 0, 1, 0, 1, 0, 1, 0], jnp.int32)
+    key_block = (yh * Z + (z + ahead * far) % Z) * CORE + (core + flip) % 2
+    turn = jnp.arange(4, dtype=jnp.int32)
+    query_block = ((yh + turn % 2) % 2 * Z + z) * CORE + (core + turn // 2) % 2
+    gap = (key_block[:, None] - query_block[None, :]) % TM
+    half = TM // 2
+    kinds = jnp.where(gap == 0, 2, jnp.where(gap < half, 0, jnp.where(gap == half, 3, 1)))
+    bases = jnp.minimum(gap, TM - gap).astype(F32) * rows * slope
+    kinds, bases = kinds.astype(jnp.int32).reshape(-1), bases.reshape(-1)
+
     part = w_qkv.shape[1]
     own = jnp.concatenate([w_qkv.reshape(3 * part, 128), w_out.T], axis=0)
     held = jnp.zeros((Z,) + own.shape, BF16)
@@ -216,57 +295,30 @@
         if step < Z // 2:
             down = tm_permute(down, 0, -1, 0)
             held = lax.dynamic_update_slice(held, down[None], ((z - step) % Z, 0, 0))
-    other = tm_permute(held, 1, 0, 0)
+    held, bias, kinds, bases = lax.optimization_barrier((held, bias, kinds, bases))
+    far = tm_permute(held, 1, 0, 0)
     flip = yh == 1
-    held = jnp.stack([jnp.where(flip, other, held), jnp.where(flip, held, other)])
-    other = tm_permute(held, 0, 0, 1)
+    held = jnp.stack([jnp.where(flip, far, held), jnp.where(flip, held, far)])
+    far = tm_permute(held, 0, 0, 1)
     flip = core == 1
-    held = jnp.stack([jnp.where(flip, other, held), jnp.where(flip, held, other)], axis=2)
+    held = jnp.stack([jnp.where(flip, far, held), jnp.where(flip, held, far)], axis=2)
     held = held.reshape(TM, 4, part, 128)
     w_all = jnp.transpose(held[:, :3], (0, 2, 1, 3)).reshape(width, 384)
     w_out_t = held[:, 3].reshape(width, 128)
 
-    wide = frames.astype(F32)
-    mean_square = jnp.mean(wide * wide, axis=-1, keepdims=True)
-    normed = (wide * lax.rsqrt(mean_square + 1e-06) * norm_gain).astype(BF16)
-    projected = jnp.dot(normed, w_all, preferred_element_type=F32).astype(BF16)
-    query, kv = projected[:, :128], projected[:, 128:]
-
-    slope = slopes[0] * LOG2E
-    spot = jnp.arange(rows, dtype=jnp.int32)
-    ahead = (spot[None, :] - spot[:, None]).astype(F32) * slope
-    apart = jnp.abs(ahead)
-    bias = jnp.stack([-ahead, ahead, -apart, apart])
-    moves = [0]
+    queries, kv = project(mine, other, w_all, rows)
+
+    scale = 128 ** (-0.5) * LOG2E
+    step_of = functools.partial(attention_step, kinds, bases, queries, bias)
+    coming = ring_permute(kv)
+    state = step_of(kv, 1, None, 0, False, scale)
     for step in range(1, Z // 2):
-        moves += [step, -step]
-    moves.append(Z // 2)
-    key_block = (yh * Z + (z + jnp.array(moves, jnp.int32)) % Z) * CORE + core
-    turn = jnp.arange(4, dtype=jnp.int32)
-    query_block = ((yh + turn % 2) % 2 * Z + z) * CORE + (core + turn // 2) % 2
-    gap = (key_block[:, None] - query_block[None, :]) % TM
-    half = TM // 2
-    kinds = jnp.where(gap == 0, 2, jnp.where(gap < half, 0, jnp.where(gap == half, 3, 1)))
-    bases = jnp.minimum(gap, TM - gap).astype(F32) * rows * slope
-    kinds, bases = kinds.astype(jnp.int32).reshape(-1), bases.reshape(-1)
-
-    both = jnp.concatenate([query, tm_permute(query, 1, 0, 0)], axis=0)
-    queries = jnp.concatenate([both, tm_permute(both, 0, 0, 1)], axis=0)
-
-    scale = 128 ** (-0.5) * LOG2E
-    step_of = functools.partial(attention_step, kinds, bases, queries)
-    up = tm_permute(kv, 0, 1, 0)
-    down = tm_permute(kv, 0, -1, 0)
-    state = step_of([kv], bias, None, 0, False, scale)
-    for step in range(1, Z // 2):
-        next_up = tm_permute(up, 0, 1, 0)
-        if step + 1 < Z // 2:
-            next_down = tm_permute(down, 0, -1, 0)
-        state = step_of([up, down], bias, state, 2 * step - 1, False, scale)
-        up, down = next_up, next_down
-    packed, out, lse = step_of([up], bias, state, Z - 1, True, scale)
-
-    got = tm_permute(packed[2 * rows :], 0, 0, 1)
+        held = coming
+        coming = ring_permute(held if step < Z // 2 - 1 else held[:rows])
+        state = step_of(held, 2, state, 2 * step - 1, False, scale)
+    packed, out, lse = step_of(coming, 1, state, Z - 1, True, scale)
+
+    got = tm_permute(packed, 0, 0, 1)
     send, keep, keep_lse = merge_core(out, lse, got, rows)
     got = tm_permute(send, 1, 0, 0)
     partial = merge_project(keep, keep_lse, got, w_out_t)

time: 151 us -> 171 us (1.13)
  waiting for transfers between devices: 26.6 us -> 44 us
  Pallas kernels: 50.5 us -> 57.6 us
  starting transfers between devices: 34.9 us -> 27.8 us
  other arithmetic: 8.62 us -> 14.4 us
    ppermute x20 -> x13, starting transfers between devices: 34.9 us -> 17.5 us  [tm_permute(): return lax.ppermute(x, 'tm', pairs)]
    ppermute x0 -> x4, waiting for transfers between devices: none -> 13.7 us  [ring_permute(): return lax.ppermute(x, 'tm', pairs)]
    ppermute x0 -> x4, starting transfers between devices: none -> 10.3 us  [ring_permute(): return lax.ppermute(x, 'tm', pairs)]
    pallas_call x0 -> x1, Pallas kernels: none -> 5.75 us  [project(): pl.pallas_call(project_kernel, out_shape=[jax.ShapeDtypeStruct((4 * rows,...]
    ppermute x20 -> x13, waiting for transfers between devices: 26.6 us -> 30.3 us  [tm_permute(): return lax.ppermute(x, 'tm', pairs)]
    another operation x5, other arithmetic: 2.68 us -> 5.24 us  [the longest x1 4.13 us: local(): bias = jnp.stack([-rise, rise, -apart, apart])]
  transfers between devices with their start and end apart: 20 -> 17, of which waited for: 10 -> 9; matrix products, arithmetic and copies ran while one was open for 5% -> 9% of each run, Pallas kernels for 25% -> 22%
where the time goes in v2:
time: 171 us; the launch traced here: 170 us
  Pallas kernels  57.6 us (34%)
  waiting for transfers between devices  44 us (26%)
  starting transfers between devices  27.8 us (16%)
  blocking collectives  20.2 us (12%)
  other arithmetic  14.4 us (8%)
  local copies, waits for them, and re-layouts  4.85 us (3%)
    pallas_call x5, Pallas kernels, attention_step(): pl.pallas_call(functools.partial(attention_kernel, shards, offset, first,...  46.2 us
    ppermute x13, waiting for transfers between devices, tm_permute(): return lax.ppermute(x, 'tm', pairs)  30.3 us
    all_to_all x1, blocking collectives, local(): lax.all_to_all(partial.reshape(heads, rows // heads, width), 'head', spli...  20.2 us
    ppermute x13, starting transfers between devices, tm_permute(): return lax.ppermute(x, 'tm', pairs)  17.5 us
    ppermute x4, waiting for transfers between devices, ring_permute(): return lax.ppermute(x, 'tm', pairs)  13.7 us
    ppermute x4, starting transfers between devices, ring_permute(): return lax.ppermute(x, 'tm', pairs)  10.3 us
    pallas_call x1, Pallas kernels, project(): pl.pallas_call(project_kernel, out_shape=[jax.ShapeDtypeStruct((4 * rows,...  5.75 us
    another operation x1, other arithmetic, local(): bias = jnp.stack([-rise, rise, -apart, apart])  4.13 us
  transfers between devices with their start and end apart: 17, of which 9 were waited for; matrix products, arithmetic and copies ran while one was open for 9% of the time, Pallas kernels for 22%

profile of v2, /device:TPU:16, one launch (start us, length us, event | category | flops | bytes accessed | tf_op | source)
XLA Modules:
  0.0 169.8 jit_solution(17730266641579035385)
XLA Ops:
  0.0 0.8 pad_maximum_fusion.4
  0.8 5.9 %collective-permute-start = (bf16[128,128]{1,0:T(8,128)(2,1)S(1)}, bf16[128,128]{1,0:T(8,128)(2,1)S(1)}, u32[]{:S(2)}, u32[]{:S(2)}) collective-permute-start(bf16[128,128]{1,0:T(8,128)(2,1)S(1)} %pad_maximum_fusion.4), channel_id=1, source_target_pairs={{16,0},{24,8},{32,16},{40,24},{48,32},{56,40},{64,48},{72,56},{80,... | collective-permute-start | bytes 98312 | tf_op jit(solution)/shard_map/ppermute | solution.py:24
  6.6 0.0 collective-permute-start.1
  6.6 1.5 fusion
  8.1 1.5 fusion.2
  9.7 0.4 collective-permute-start.7
  10.8 0.0 copy-start.9
  10.8 0.0 copy-start.10
  10.8 0.3 convert_multiply_fusion.2
  11.1 1.6 fusion.4
  12.7 0.1 broadcast_subtract_fusion
  12.8 0.1 sub.91
  12.9 0.6 fusion.10
  13.5 0.5 compare_select_fusion.12.refs_0_
  14.0 4.1 %pad_maximum_fusion.refs_4_.refs_5_.refs_6_ = f32[4,512,512]{2,1,0:T(8,128)} fusion(f32[1,512,512]{2,1,0:T(8,128)S(1)} %get-tuple-element.52, f32[1,512,512]{2,1,0:T(8,128)} %get-tuple-element.54, f32[1,512,512]{2,1,0:T(8,128)S(1)} %get-tuple-element.51, f32[1,512,512]{2,1,0:T(8,128)} %get-tuple-element.53), kind=kLoop, calls=%fused_computation | loop fusion | flops 3145728 | bytes 8388608 | tf_op jit(solution)/shard_map/stack | solution.py:274
  18.3 0.0 collective-permute-done
  18.4 3.3 %collective-permute-start.2 = (bf16[128,128]{1,0:T(8,128)(2,1)S(1)}, bf16[128,128]{1,0:T(8,128)(2,1)S(1)}, u32[]{:S(2)}, u32[]{:S(2)}) collective-permute-start(bf16[128,128]{1,0:T(8,128)(2,1)S(1)} %collective-permute-done), channel_id=1, source_target_pairs={{16,0},{24,8},{32,16},{40,24},{48,32},{56,40},{64,48},{72,56},{80,... | collective-permute-start | bytes 98312 | tf_op jit(solution)/shard_map/ppermute | solution.py:24
  21.7 0.0 collective-permute-done.1
  21.7 1.6 collective-permute-done.2
  23.3 3.5 %collective-permute-start.4 = (bf16[128,128]{1,0:T(8,128)(2,1)S(1)}, bf16[128,128]{1,0:T(8,128)(2,1)S(1)}, u32[]{:S(2)}, u32[]{:S(2)}) collective-permute-start(bf16[128,128]{1,0:T(8,128)(2,1)S(1)} %collective-permute-done.2), channel_id=1, source_target_pairs={{16,0},{24,8},{32,16},{40,24},{48,32},{56,40},{64,48},{72,56},{80,... | collective-permute-start | bytes 98312 | tf_op jit(solution)/shard_map/ppermute | solution.py:24
  26.8 0.0 collective-permute-done.3
  26.8 1.6 collective-permute-done.4
  28.4 3.5 %collective-permute-start.6 = (bf16[128,128]{1,0:T(8,128)(2,1)S(1)}, bf16[128,128]{1,0:T(8,128)(2,1)S(1)}, u32[]{:S(2)}, u32[]{:S(2)}) collective-permute-start(bf16[128,128]{1,0:T(8,128)(2,1)S(1)} %collective-permute-done.4), channel_id=1, source_target_pairs={{16,0},{24,8},{32,16},{40,24},{48,32},{56,40},{64,48},{72,56},{80,... | collective-permute-start | bytes 98312 | tf_op jit(solution)/shard_map/ppermute | solution.py:24
  31.9 4.1 %collective-permute-done.7 = bf16[512,1024]{1,0:T(8,128)(2,1)} collective-permute-done((bf16[512,1024]{1,0:T(8,128)(2,1)S(1)}, bf16[512,1024]{1,0:T(8,128)(2,1)}, u32[]{:S(2)}, u32[]{:S(2)}) %collective-permute-start.7) | collective-permute-done | bytes 1048608 | tf_op jit(solution)/shard_map/ppermute | solution.py:24
  36.0 1.4 pad_maximum_fusion.1.mine_ref
  37.4 0.1 collective-permute-start.8
  37.5 0.0 collective-permute-done.5
  37.5 0.0 collective-permute-done.6
  37.6 0.4 collective-permute-start.9
  38.0 9.9 %collective-permute-done.9 = bf16[8,128,128]{2,1,0:T(8,128)(2,1)S(1)} collective-permute-done((bf16[8,128,128]{2,1,0:T(8,128)(2,1)S(1)}, bf16[8,128,128]{2,1,0:T(8,128)(2,1)S(1)}, u32[]{:S(2)}, u32[]{:S(2)}) %collective-permute-start.9) | collective-permute-done | bytes 262176 | tf_op jit(solution)/shard_map/ppermute | solution.py:24
  47.9 0.9 pad_maximum_fusion.3
  48.8 0.0 collective-permute-start.10
  48.8 2.1 %collective-permute-done.10 = bf16[2,8,128,128]{3,2,1,0:T(8,128)(2,1)S(1)} collective-permute-done((bf16[2,8,128,128]{3,2,1,0:T(8,128)(2,1)}, bf16[2,8,128,128]{3,2,1,0:T(8,128)(2,1)S(1)}, u32[]{:S(2)}, u32[]{:S(2)}) %collective-permute-start.10) | collective-permute-done | bytes 524320 | tf_op jit(solution)/shard_map/ppermute | solution.py:24
  50.9 0.1 select_bitcast_fusion.1
  51.0 0.1 pad_maximum_fusion.2
  51.1 0.1 slice_bitcast_fusion
  51.2 0.5 copy.10
  51.7 1.1 copy.13
  52.8 0.0 collective-permute-done.8.other_ref
  52.8 5.7 %shard_map.73 = (bf16[2048,128]{1,0:T(8,128)(2,1)}, bf16[1024,256]{1,0:T(8,128)(2,1)}) custom-call(bf16[1024,1024]{1,0:T(8,128)(2,1)} %copy-done, bf16[1024,1024]{1,0:T(8,128)(2,1)} %collective-permute-done.8.other_ref, bf16[1024,384]{1,0:T(8,128)(2,1)} %bitcast.44), custom_call_target="tpu_custom_call" | custom-call | tf_op jit(solution)/shard_map/pallas_call | solution.py:58
  58.5 3.0 %collective-permute-start.11 = (bf16[1024,256]{1,0:T(8,128)(2,1)}, bf16[1024,256]{1,0:T(8,128)(2,1)S(1)}, u32[]{:S(2)}, u32[]{:S(2)}) collective-permute-start(bf16[1024,256]{1,0:T(8,128)(2,1)} %get-tuple-element.29.refs_3_), channel_id=1, source_target_pairs={{16,0},{120,8},{32,16},{8,24},{48,32},{24,40},{64,48},{40,56},{80,... | collective-permute-start | bytes 1572872 | tf_op jit(solution)/shard_map/ppermute | solution.py:34
  61.5 7.0 %collective-permute-done.11.refs_3_.refs_4_ = bf16[1024,256]{1,0:T(8,128)(2,1)S(1)} collective-permute-done((bf16[1024,256]{1,0:T(8,128)(2,1)}, bf16[1024,256]{1,0:T(8,128)(2,1)S(1)}, u32[]{:S(2)}, u32[]{:S(2)}) %collective-permute-start.11) | collective-permute-done | bytes 524320 | tf_op jit(solution)/shard_map/ppermute | solution.py:34
  68.5 3.6 %collective-permute-start.12 = (bf16[1024,256]{1,0:T(8,128)(2,1)S(1)}, bf16[1024,256]{1,0:T(8,128)(2,1)S(1)}, u32[]{:S(2)}, u32[]{:S(2)}) collective-permute-start(bf16[1024,256]{1,0:T(8,128)(2,1)S(1)} %collective-permute-done.11.refs_3_.refs_4_), channel_id=1, source_target_pairs={{16,0},{120,8},{32,16},{8,24},{48,32},{24,40},{64,48},{40,56},{80,... | collective-permute-start | bytes 1572872 | tf_op jit(solution)/shard_map/ppermute | solution.py:34
  72.1 6.7 %collective-permute-done.12.refs_3_.refs_4_ = bf16[1024,256]{1,0:T(8,128)(2,1)S(1)} collective-permute-done((bf16[1024,256]{1,0:T(8,128)(2,1)S(1)}, bf16[1024,256]{1,0:T(8,128)(2,1)S(1)}, u32[]{:S(2)}, u32[]{:S(2)}) %collective-permute-start.12) | collective-permute-done | bytes 524320 | tf_op jit(solution)/shard_map/ppermute | solution.py:34
  78.8 3.7 %collective-permute-start.13 = (bf16[1024,256]{1,0:T(8,128)(2,1)S(1)}, bf16[1024,256]{1,0:T(8,128)(2,1)S(1)}, u32[]{:S(2)}, u32[]{:S(2)}) collective-permute-start(bf16[1024,256]{1,0:T(8,128)(2,1)S(1)} %collective-permute-done.12.refs_3_.refs_4_), channel_id=1, source_target_pairs={{16,0},{120,8},{32,16},{8,24},{48,32},{24,40},{64,48},{40,56},{80,... | collective-permute-start | bytes 1572872 | tf_op jit(solution)/shard_map/ppermute | solution.py:34
  82.5 6.6 %shard_map.74 = (f32[2048,128]{1,0:T(8,128)}, f32[2048,256]{1,0:T(8,128)}) custom-call(s32[32]{0:T(128)} %compare_select_fusion.12.refs_0_, f32[32]{0:T(128)} %get-tuple-element.26.refs_1_, bf16[2048,128]{1,0:T(8,128)(2,1)} %get-tuple-element.28.refs_2_, bf16[1024,256]{1,0:T(8,128)(2,1)} %get-tuple-element.29.refs_3_, ...), custom_call_target="tpu_custom_call" | custom-call | flops 1073741824 | bytes 6553600 | tf_op jit(solution)/shard_map/pallas_call | solution.py:180
  89.1 10.2 %shard_map.75 = (f32[2048,128]{1,0:T(8,128)}, f32[2048,256]{1,0:T(8,128)}) custom-call(s32[32]{0:T(128)} %compare_select_fusion.12.refs_0_, f32[32]{0:T(128)} %get-tuple-element.26.refs_1_, bf16[2048,128]{1,0:T(8,128)(2,1)} %get-tuple-element.28.refs_2_, bf16[1024,256]{1,0:T(8,128)(2,1)} %copy-done.3, bf16[1024,256]{1,0:T(8,128)(2,1)} %copy-done.3, ...), custom_call_target="tpu_custom_call" | custom-call | flops 2147483648 | bytes 6815744 | tf_op jit(solution)/shard_map/pallas_call | solution.py:180
  99.3 0.0 collective-permute-done.13.refs_3_.refs_4_
  99.3 0.1 collective-permute-start.14
  99.4 10.3 %shard_map.76 = (f32[2048,128]{1,0:T(8,128)}, f32[2048,256]{1,0:T(8,128)}) custom-call(s32[32]{0:T(128)} %compare_select_fusion.12.refs_0_, f32[32]{0:T(128)} %get-tuple-element.26.refs_1_, bf16[2048,128]{1,0:T(8,128)(2,1)} %get-tuple-element.28.refs_2_, bf16[1024,256]{1,0:T(8,128)(2,1)} %copy-done.2, bf16[1024,256]{1,0:T(8,128)(2,1)} %copy-done.2, ...), custom_call_target="tpu_custom_call" | custom-call | flops 2147483648 | bytes 6815744 | tf_op jit(solution)/shard_map/pallas_call | solution.py:180
  109.7 10.2 %shard_map.77 = (f32[2048,128]{1,0:T(8,128)}, f32[2048,256]{1,0:T(8,128)}) custom-call(s32[32]{0:T(128)} %compare_select_fusion.12.refs_0_, f32[32]{0:T(128)} %get-tuple-element.26.refs_1_, bf16[2048,128]{1,0:T(8,128)(2,1)} %get-tuple-element.28.refs_2_, bf16[1024,256]{1,0:T(8,128)(2,1)} %copy-done.1, bf16[1024,256]{1,0:T(8,128)(2,1)} %copy-done.1, ...), custom_call_target="tpu_custom_call" | custom-call | flops 2147483648 | bytes 6815744 | tf_op jit(solution)/shard_map/pallas_call | solution.py:180
  119.9 0.0 collective-permute-done.14.refs_3_
  120.0 0.7 copy-done.5
  120.7 8.8 %shard_map.78 = (bf16[1024,256]{1,0:T(8,128)(2,1)}, f32[1024,128]{1,0:T(8,128)}, f32[1024,128]{1,0:T(8,128)}) custom-call(s32[32]{0:T(128)} %compare_select_fusion.12.refs_0_, f32[32]{0:T(128)} %get-tuple-element.26.refs_1_, bf16[2048,128]{1,0:T(8,128)(2,1)} %get-tuple-element.28.refs_2_, bf16[512,256]{1,0:T(8,128)(2,1)} %copy-done.5, ...), custom_call_target="tpu_custom_call" | custom-call | flops 1073741824 | bytes 6553600 | tf_op jit(solution)/shard_map/pallas_call | solution.py:180
  129.5 2.1 %collective-permute-done.15.got_ref = bf16[1024,256]{1,0:T(8,128)(2,1)S(1)} collective-permute-done((bf16[1024,256]{1,0:T(8,128)(2,1)}, bf16[1024,256]{1,0:T(8,128)(2,1)S(1)}, u32[]{:S(2)}, u32[]{:S(2)}) %collective-permute-start.15) | collective-permute-done | bytes 524320 | tf_op jit(solution)/shard_map/ppermute | solution.py:24
  131.6 0.8 copy-done.4
  132.4 2.8 %shard_map.79 = (bf16[512,256]{1,0:T(8,128)(2,1)}, f32[512,128]{1,0:T(8,128)}, f32[512,128]{1,0:T(8,128)}) custom-call(f32[1024,128]{1,0:T(8,128)} %get-tuple-element.39.out_ref, f32[1024,128]{1,0:T(8,128)} %get-tuple-element.40.lse_ref, bf16[1024,256]{1,0:T(8,128)(2,1)} %copy-done.4), custom_call_target="tpu_custom_call" | custom-call | tf_op jit(solution)/shard_map/pallas_call | solution.py:222
  135.2 0.3 collective-permute-start.16
  135.5 0.7 slice.14
  136.2 9.0 %collective-permute-done.16.got_ref = bf16[512,256]{1,0:T(8,128)(2,1)S(1)} collective-permute-done((bf16[512,256]{1,0:T(8,128)(2,1)}, bf16[512,256]{1,0:T(8,128)(2,1)S(1)}, u32[]{:S(2)}, u32[]{:S(2)}) %collective-permute-start.16) | collective-permute-done | bytes 262176 | tf_op jit(solution)/shard_map/ppermute | solution.py:24
  145.2 0.7 copy-done.6
  145.9 2.9 %shard_map.80 = bf16[512,1024]{1,0:T(8,128)(2,1)} custom-call(f32[512,128]{1,0:T(8,128)} %get-tuple-element.42.out_ref, f32[512,128]{1,0:T(8,128)} %get-tuple-element.43.lse_ref, bf16[512,256]{1,0:T(8,128)(2,1)} %copy-done.6, bf16[1024,128]{1,0:T(8,128)(2,1)} %bitcast.45), custom_call_target="tpu_custom_call" | custom-call | tf_op jit(solution)/shard_map/pallas_call | solution.py:253
  148.8 20.2 %all_to_all.5 = bf16[8,64,1024]{2,1,0:T(8,128)(2,1)S(1)} all-to-all(bf16[8,64,1024]{2,1,0:T(8,128)(2,1)} %bitcast.43), channel_id=1, replica_groups=mesh['tm'=32,'head'=8] {'head'}, dimensions={0} | all-to-all | bytes 2097152 | tf_op jit(solution)/shard_map/all_to_all | solution.py:326
  169.0 0.8 reduce_sum.22
  (34 shorter events, 0.3 us)
Async XLA Ops:
  0.8 17.6 %collective-permute-start = (bf16[128,128]{1,0:T(8,128)(2,1)S(1)}, bf16[128,128]{1,0:T(8,128)(2,1)S(1)}, u32[]{:S(2)}, u32[]{:S(2)}) collective-permute-start(bf16[128,128]{1,0:T(8,128)(2,1)S(1)} %pad_maximum_fusion.4), channel_id=1, source_target_pairs={{16,0},{24,8},{32,16},{40,24},{48,32},{56,40},{64,48},{72,56},{80,... | collective-permute-start | bytes 98312 | tf_op jit(solution)/shard_map/ppermute | solution.py:24
  6.6 15.1 %collective-permute-start.1 = (bf16[128,128]{1,0:T(8,128)(2,1)S(1)}, bf16[128,128]{1,0:T(8,128)(2,1)S(1)}, u32[]{:S(2)}, u32[]{:S(2)}) collective-permute-start(bf16[128,128]{1,0:T(8,128)(2,1)S(1)} %pad_maximum_fusion.4), channel_id=1, source_target_pairs={{112,0},{120,8},{0,16},{8,24},{16,32},{24,40},{32,48},{40,56},{48,... | collective-permute-start | bytes 98312 | tf_op jit(solution)/shard_map/ppermute | solution.py:24
  9.7 26.3 %collective-permute-start.7 = (bf16[512,1024]{1,0:T(8,128)(2,1)S(1)}, bf16[512,1024]{1,0:T(8,128)(2,1)}, u32[]{:S(2)}, u32[]{:S(2)}) collective-permute-start(bf16[512,1024]{1,0:T(8,128)(2,1)S(1)} %fusion.2), channel_id=1, source_target_pairs={{128,0},{136,8},{144,16},{152,24},{160,32},{168,40},{176,48},{184,... | collective-permute-start | bytes 3145736 | tf_op jit(solution)/shard_map/ppermute | solution.py:24
  10.8 2.0 %copy-start.9 = (s32[8]{0:T(128)S(1)}, s32[8]{0:T(128)}, u32[]{:S(2)}) copy-start(s32[8]{0:T(128)} %constant.174.clone) | copy-start | bytes 100
  10.8 1.9 %copy-start.10 = (s32[8]{0:T(128)S(1)}, s32[8]{0:T(128)}, u32[]{:S(2)}) copy-start(s32[8]{0:T(128)} %constant.175.clone) | copy-start | bytes 100
  14.0 4.2 %copy-start.7 = (bf16[3,32,128]{2,1,0:T(8,128)(2,1)S(1)}, bf16[3,32,128]{2,1,0:T(8,128)(2,1)}, u32[]{:S(2)}) copy-start(bf16[3,32,128]{2,1,0:T(8,128)(2,1)} %param.9) | copy-start | bytes 73732
  14.0 4.2 %copy-start.8 = (bf16[128,32]{0,1:T(8,128)(2,1)S(1)}, bf16[128,32]{0,1:T(8,128)(2,1)}, u32[]{:S(2)}) copy-start(bf16[128,32]{0,1:T(8,128)(2,1)} %param.11) | copy-start | bytes 24580
  18.4 4.9 %collective-permute-start.2 = (bf16[128,128]{1,0:T(8,128)(2,1)S(1)}, bf16[128,128]{1,0:T(8,128)(2,1)S(1)}, u32[]{:S(2)}, u32[]{:S(2)}) collective-permute-start(bf16[128,128]{1,0:T(8,128)(2,1)S(1)} %collective-permute-done), channel_id=1, source_target_pairs={{16,0},{24,8},{32,16},{40,24},{48,32},{56,40},{64,48},{72,56},{80,... | collective-permute-start | bytes 98312 | tf_op jit(solution)/shard_map/ppermute | solution.py:24
  21.7 5.1 %collective-permute-start.3 = (bf16[128,128]{1,0:T(8,128)(2,1)S(1)}, bf16[128,128]{1,0:T(8,128)(2,1)S(1)}, u32[]{:S(2)}, u32[]{:S(2)}) collective-permute-start(bf16[128,128]{1,0:T(8,128)(2,1)S(1)} %collective-permute-done.1), channel_id=1, source_target_pairs={{112,0},{120,8},{0,16},{8,24},{16,32},{24,40},{32,48},{40,56},{48,... | collective-permute-start | bytes 98312 | tf_op jit(solution)/shard_map/ppermute | solution.py:24
  23.3 5.1 %collective-permute-start.4 = (bf16[128,128]{1,0:T(8,128)(2,1)S(1)}, bf16[128,128]{1,0:T(8,128)(2,1)S(1)}, u32[]{:S(2)}, u32[]{:S(2)}) collective-permute-start(bf16[128,128]{1,0:T(8,128)(2,1)S(1)} %collective-permute-done.2), channel_id=1, source_target_pairs={{16,0},{24,8},{32,16},{40,24},{48,32},{56,40},{64,48},{72,56},{80,... | collective-permute-start | bytes 98312 | tf_op jit(solution)/shard_map/ppermute | solution.py:24
  26.8 10.7 %collective-permute-start.5 = (bf16[128,128]{1,0:T(8,128)(2,1)S(1)}, bf16[128,128]{1,0:T(8,128)(2,1)S(1)}, u32[]{:S(2)}, u32[]{:S(2)}) collective-permute-start(bf16[128,128]{1,0:T(8,128)(2,1)S(1)} %collective-permute-done.3), channel_id=1, source_target_pairs={{112,0},{120,8},{0,16},{8,24},{16,32},{24,40},{32,48},{40,56},{48,... | collective-permute-start | bytes 98312 | tf_op jit(solution)/shard_map/ppermute | solution.py:24
  28.4 9.1 %collective-permute-start.6 = (bf16[128,128]{1,0:T(8,128)(2,1)S(1)}, bf16[128,128]{1,0:T(8,128)(2,1)S(1)}, u32[]{:S(2)}, u32[]{:S(2)}) collective-permute-start(bf16[128,128]{1,0:T(8,128)(2,1)S(1)} %collective-permute-done.4), channel_id=1, source_target_pairs={{16,0},{24,8},{32,16},{40,24},{48,32},{56,40},{64,48},{72,56},{80,... | collective-permute-start | bytes 98312 | tf_op jit(solution)/shard_map/ppermute | solution.py:24
  37.4 13.6 %copy-start = (bf16[1024,1024]{1,0:T(8,128)(2,1)}, bf16[1024,1024]{1,0:T(8,128)(2,1)S(1)}, u32[]{:S(2)}) copy-start(bf16[1024,1024]{1,0:T(8,128)(2,1)S(1)} %pad_maximum_fusion.1.mine_ref) | copy-start | bytes 6291460
  37.4 15.4 %collective-permute-start.8 = (bf16[1024,1024]{1,0:T(8,128)(2,1)S(1)}, bf16[1024,1024]{1,0:T(8,128)(2,1)}, u32[]{:S(2)}, u32[]{:S(2)}) collective-permute-start(bf16[1024,1024]{1,0:T(8,128)(2,1)S(1)} %pad_maximum_fusion.1.mine_ref), channel_id=1, source_target_pairs={{8,0},{0,8},{24,16},{16,24},{40,32},{32,40},{56,48},{48,56},{72,64... | collective-permute-start | bytes 6291464 | tf_op jit(solution)/shard_map/ppermute | solution.py:24
  37.6 10.3 %collective-permute-start.9 = (bf16[8,128,128]{2,1,0:T(8,128)(2,1)S(1)}, bf16[8,128,128]{2,1,0:T(8,128)(2,1)S(1)}, u32[]{:S(2)}, u32[]{:S(2)}) collective-permute-start(bf16[8,128,128]{2,1,0:T(8,128)(2,1)S(1)} %bitcast_dynamic-update-slice_fusion), channel_id=1, source_target_pairs={{128,0},{136,8},{144,16},{152,24},{160,32},{168,40},{176,48},{184,... | collective-permute-start | bytes 786440 | tf_op jit(solution)/shard_map/ppermute | solution.py:24
  48.8 2.1 %collective-permute-start.10 = (bf16[2,8,128,128]{3,2,1,0:T(8,128)(2,1)}, bf16[2,8,128,128]{3,2,1,0:T(8,128)(2,1)S(1)}, u32[]{:S(2)}, u32[]{:S(2)}) collective-permute-start(bf16[2,8,128,128]{3,2,1,0:T(8,128)(2,1)} %pad_maximum_fusion.3), channel_id=1, source_target_pairs={{8,0},{0,8},{24,16},{16,24},{40,32},{32,40},{56,48},{48,56},{72,64... | collective-permute-start | bytes 1572872 | tf_op jit(solution)/shard_map/ppermute | solution.py:24
  58.5 10.0 %collective-permute-start.11 = (bf16[1024,256]{1,0:T(8,128)(2,1)}, bf16[1024,256]{1,0:T(8,128)(2,1)S(1)}, u32[]{:S(2)}, u32[]{:S(2)}) collective-permute-start(bf16[1024,256]{1,0:T(8,128)(2,1)} %get-tuple-element.29.refs_3_), channel_id=1, source_target_pairs={{16,0},{120,8},{32,16},{8,24},{48,32},{24,40},{64,48},{40,56},{80,... | collective-permute-start | bytes 1572872 | tf_op jit(solution)/shard_map/ppermute | solution.py:34
  68.5 20.6 %copy-start.3 = (bf16[1024,256]{1,0:T(8,128)(2,1)}, bf16[1024,256]{1,0:T(8,128)(2,1)S(1)}, u32[]{:S(2)}) copy-start(bf16[1024,256]{1,0:T(8,128)(2,1)S(1)} %collective-permute-done.11.refs_3_.refs_4_) | copy-start | bytes 1572868
  68.5 10.3 %collective-permute-start.12 = (bf16[1024,256]{1,0:T(8,128)(2,1)S(1)}, bf16[1024,256]{1,0:T(8,128)(2,1)S(1)}, u32[]{:S(2)}, u32[]{:S(2)}) collective-permute-start(bf16[1024,256]{1,0:T(8,128)(2,1)S(1)} %collective-permute-done.11.refs_3_.refs_4_), channel_id=1, source_target_pairs={{16,0},{120,8},{32,16},{8,24},{48,32},{24,40},{64,48},{40,56},{80,... | collective-permute-start | bytes 1572872 | tf_op jit(solution)/shard_map/ppermute | solution.py:34
  78.8 10.3 %copy-start.2 = (bf16[1024,256]{1,0:T(8,128)(2,1)}, bf16[1024,256]{1,0:T(8,128)(2,1)S(1)}, u32[]{:S(2)}) copy-start(bf16[1024,256]{1,0:T(8,128)(2,1)S(1)} %collective-permute-done.12.refs_3_.refs_4_) | copy-start | bytes 1572868
  78.8 20.5 %collective-permute-start.13 = (bf16[1024,256]{1,0:T(8,128)(2,1)S(1)}, bf16[1024,256]{1,0:T(8,128)(2,1)S(1)}, u32[]{:S(2)}, u32[]{:S(2)}) collective-permute-start(bf16[1024,256]{1,0:T(8,128)(2,1)S(1)} %collective-permute-done.12.refs_3_.refs_4_), channel_id=1, source_target_pairs={{16,0},{120,8},{32,16},{8,24},{48,32},{24,40},{64,48},{40,56},{80,... | collective-permute-start | bytes 1572872 | tf_op jit(solution)/shard_map/ppermute | solution.py:34
  99.3 10.5 %copy-start.1 = (bf16[1024,256]{1,0:T(8,128)(2,1)}, bf16[1024,256]{1,0:T(8,128)(2,1)S(1)}, u32[]{:S(2)}) copy-start(bf16[1024,256]{1,0:T(8,128)(2,1)S(1)} %collective-permute-done.13.refs_3_.refs_4_) | copy-start | bytes 1572868
  99.3 20.6 %collective-permute-start.14 = (bf16[512,256]{1,0:T(8,128)(2,1)S(1)}, bf16[512,256]{1,0:T(8,128)(2,1)S(1)}, u32[]{:S(2)}, u32[]{:S(2)}) collective-permute-start(bf16[512,256]{1,0:T(8,128)(2,1)S(1)} %slice.13), channel_id=1, source_target_pairs={{16,0},{120,8},{32,16},{8,24},{48,32},{24,40},{64,48},{40,56},{80,... | collective-permute-start | bytes 786440 | tf_op jit(solution)/shard_map/ppermute | solution.py:34
  119.9 0.7 copy-start.5
  129.5 2.1 %collective-permute-start.15 = (bf16[1024,256]{1,0:T(8,128)(2,1)}, bf16[1024,256]{1,0:T(8,128)(2,1)S(1)}, u32[]{:S(2)}, u32[]{:S(2)}) collective-permute-start(bf16[1024,256]{1,0:T(8,128)(2,1)} %get-tuple-element.41), channel_id=1, source_target_pairs={{8,0},{0,8},{24,16},{16,24},{40,32},{32,40},{56,48},{48,56},{72,64... | collective-permute-start | bytes 1572872 | tf_op jit(solution)/shard_map/ppermute | solution.py:24
  131.6 0.8 copy-start.4
  135.2 10.1 %collective-permute-start.16 = (bf16[512,256]{1,0:T(8,128)(2,1)}, bf16[512,256]{1,0:T(8,128)(2,1)S(1)}, u32[]{:S(2)}, u32[]{:S(2)}) collective-permute-start(bf16[512,256]{1,0:T(8,128)(2,1)} %get-tuple-element.44), channel_id=1, source_target_pairs={{128,0},{136,8},{144,16},{152,24},{160,32},{168,40},{176,48},{184,... | collective-permute-start | bytes 786440 | tf_op jit(solution)/shard_map/ppermute | solution.py:24
  145.2 0.7 copy-start.6

commit v3 on v1

v3 whole, which is shorter than its diff:
```python
import functools
import math

import jax
import jax.numpy as jnp
from jax import lax
from jax.experimental import pallas as pl
from jax.experimental.pallas import tpu as pltpu
from jax.sharding import PartitionSpec as P

F32, BF16 = jnp.float32, jnp.bfloat16
LOG2E = math.log2(math.e)
YH, Z, CORE = 2, 8, 2
TM = YH * Z * CORE


def tm_permute(x, d_yh, d_z, d_core):
    pairs = []
    for yh in range(YH):
        for z in range(Z):
            for core in range(CORE):
                source = ((yh + d_yh) % YH * Z + (z + d_z) % Z) * CORE + (core + d_core) % CORE
                pairs.append((source, (yh * Z + z) * CORE + core))
    return lax.ppermute(x, "tm", pairs)


def split_bf16(x):
    high = x.astype(BF16)
    rest = x - high.astype(F32)
    mid = rest.astype(BF16)
    return high, mid, (rest - mid.astype(F32)).astype(BF16)


def pack_partial(out, lse):
    high, mid, low = split_bf16(lse)
    lane = lax.broadcasted_iota(jnp.int32, lse.shape, 1)
    stat = jnp.where(lane < 32, high.astype(F32), jnp.where(lane < 64, mid.astype(F32), low.astype(F32)))
    return jnp.concatenate([out.astype(BF16), stat.astype(BF16)], axis=1)


def unpack_partial(packed):
    out = packed[:, :128].astype(F32)
    stat = packed[:, 128:].astype(F32)
    lse = stat[:, 0:1] + stat[:, 32:33] + stat[:, 64:65]
    return out, jnp.broadcast_to(lse, out.shape)


def attention_kernel(shards, scale, blocks, *refs):
    sign_ref, base_ref, slope_ref, query_ref = refs[:4]
    kv_refs = refs[4 : 4 + shards]
    send_ref, keep_ref, keep_lse_ref = refs[4 + shards :]
    step = pl.program_id(0)
    rows = query_ref.shape[0]
    keys = kv_refs[0].shape[0]
    parts = keys // rows
    block = step // parts
    first_row = (step % parts) * rows
    query = query_ref[...]
    ones = jnp.ones((keys, 128), BF16)
    row = (lax.broadcasted_iota(jnp.int32, (rows, 128), 0) + first_row).astype(F32)
    column = lax.broadcasted_iota(jnp.int32, (1, keys), 1).astype(F32)
    peak = total = None
    for start in range(0, shards, 2):
        scores, offsets, top = [], [], None
        for j in (start, start + 1):
            sign, base = sign_ref[blocks * j + block], base_ref[blocks * j + block]
            score = lax.dot_general(
                query, kv_refs[j][:, :128], (((1,), (1,)), ((), ())), preferred_element_type=F32
            )
            if j == 0:
                slope = jnp.where(block == 0, -slope_ref[0], slope_ref[0])
                score = score * scale + jnp.abs(column - row[:, :1]) * slope
                offset = jnp.full((rows, 128), base, F32)
            else:
                score = score * scale + column * sign
                offset = row * sign + base
            scores.append(score)
            offsets.append(offset)
            here_top = jnp.broadcast_to(jnp.max(score, axis=1, keepdims=True), (rows, 128)) - offset
            top = here_top if top is None else jnp.maximum(top, here_top)
        old = peak
        peak = top if old is None else jnp.maximum(top, old)
        part = None
        for j, score, offset in zip((start, start + 1), scores, offsets):
            weight = jnp.exp2(score - jnp.tile(peak + offset, (1, keys // 128))).astype(BF16)
            value = jnp.concatenate([kv_refs[j][:, 128:], ones], axis=1)
            more = jnp.dot(weight, value, preferred_element_type=F32)
            part = more if part is None else part + more
        total = part if total is None else part + total * jnp.tile(jnp.exp2(old - peak), (1, 2))
    out = total[:, :128] / total[:, 128:]
    lse = peak + jnp.log2(total[:, 128:])

    @pl.when(block == 0)
    def _():
        keep_ref[...] = out
        keep_lse_ref[...] = lse

    @pl.when(block == 1)
    def _():
        send_ref[...] = pack_partial(out, lse)


def attention(signs, bases, slope, query, kvs, scale):
    blocks, shards = 2, len(kvs)
    keys = kvs[0].shape[0]
    rows = keys // 2
    early = lambda i, *_: (jnp.minimum(i, 1), 0)
    late = lambda i, *_: (jnp.maximum(i - 2, 0), 0)
    return pl.pallas_call(
        functools.partial(attention_kernel, shards, scale, blocks),
        out_shape=[
            jax.ShapeDtypeStruct((keys, 256), BF16),
            jax.ShapeDtypeStruct((keys, 128), F32),
            jax.ShapeDtypeStruct((keys, 128), F32),
        ],
        grid_spec=pltpu.PrefetchScalarGridSpec(
            num_scalar_prefetch=3,
            grid=(blocks * 2,),
            in_specs=[pl.BlockSpec((rows, 128), lambda i, *_: (i, 0))]
            + [pl.BlockSpec((keys, 256), lambda i, *_: (0, 0)) for _ in kvs],
            out_specs=[
                pl.BlockSpec((rows, 256), late),
                pl.BlockSpec((rows, 128), early),
                pl.BlockSpec((rows, 128), early),
            ],
        ),
        cost_estimate=pl.CostEstimate(
            flops=4 * blocks * keys * keys * shards * 256,
            bytes_accessed=shards * keys * 512 + blocks * keys * 1024,
            transcendentals=blocks * keys * keys * shards,
        ),
    )(signs, bases, slope, query, *kvs)


def merge(out_a, lse_a, out_b, lse_b):
    top = jnp.maximum(lse_a, lse_b)
    part_a, part_b = jnp.exp2(lse_a - top), jnp.exp2(lse_b - top)
    both = part_a + part_b
    return (out_a * part_a + out_b * part_b) / both, top + jnp.log2(both)


def merge_project_kernel(out_ref, lse_ref, got_ref, w_ref, partial_ref):
    got, got_lse = unpack_partial(got_ref[...])
    out, _ = merge(out_ref[...], lse_ref[...], got, got_lse)
    partial_ref[...] = lax.dot_general(
        out.astype(BF16), w_ref[...], (((1,), (1,)), ((), ())), preferred_element_type=F32
    ).astype(BF16)


def merge_project(out, lse, got, w_out_t):
    rows, width = out.shape[0], w_out_t.shape[0]
    return pl.pallas_call(
        merge_project_kernel,
        out_shape=jax.ShapeDtypeStruct((rows, width), BF16),
    )(out, lse, got, w_out_t)


def local(frames, norm_gain, w_qkv, slopes, w_out):
    rows, width = frames.shape
    me = lax.axis_index("tm")
    core, z, yh = me % CORE, me // CORE % Z, me // (CORE * Z)

    part = w_qkv.shape[1]
    own = jnp.concatenate([w_qkv.reshape(3 * part, 128), w_out.T], axis=0)
    held = jnp.zeros((Z,) + own.shape, BF16)
    held = lax.dynamic_update_slice(held, own[None], (z, 0, 0))
    up = down = own
    for step in range(1, Z // 2 + 1):
        up = tm_permute(up, 0, 1, 0)
        held = lax.dynamic_update_slice(held, up[None], ((z + step) % Z, 0, 0))
        if step < Z // 2:
            down = tm_permute(down, 0, -1, 0)
            held = lax.dynamic_update_slice(held, down[None], ((z - step) % Z, 0, 0))
    other = tm_permute(held, 1, 0, 0)
    flip = yh == 1
    held = jnp.stack([jnp.where(flip, other, held), jnp.where(flip, held, other)])
    other = tm_permute(held, 0, 0, 1)
    flip = core == 1
    held = jnp.stack([jnp.where(flip, other, held), jnp.where(flip, held, other)], axis=2)
    held = held.reshape(TM, 4, part, 128)
    w_all = jnp.transpose(held[:, :3], (0, 2, 1, 3)).reshape(width, 384)
    w_out_t = held[:, 3].reshape(width, 128)

    wide = frames.astype(F32)
    mean_square = jnp.mean(wide * wide, axis=-1, keepdims=True)
    normed = (wide * lax.rsqrt(mean_square + 1e-06) * norm_gain).astype(BF16)
    projected = jnp.dot(normed, w_all, preferred_element_type=F32).astype(BF16)
    query, kv = projected[:, :128], projected[:, 128:]

    slope = slopes * LOG2E
    ring = [0]
    for step in range(1, Z // 2):
        ring += [step, -step]
    ring.append(Z // 2)
    far = jnp.array([move for move in ring for _ in range(CORE)], jnp.int32)
    swap = jnp.array([0, 1] * Z, jnp.int32)
    key_block = (yh * Z + (z + far) % Z) * CORE + (core + swap) % CORE
    query_block = ((yh + jnp.arange(YH, dtype=jnp.int32)) % YH * Z + z) * CORE + core
    gap = (key_block[:, None] - query_block[None, :]) % TM
    signs = jnp.where(gap < TM // 2, -slope[0], slope[0]).reshape(-1)
    bases = (jnp.minimum(gap, TM - gap).astype(F32) * (rows * slope[0])).reshape(-1)

    up = tm_permute(kv, 0, 1, 0)
    down = tm_permute(kv, 0, -1, 0)
    kvs = [kv, tm_permute(kv, 0, 0, 1)]
    queries = jnp.concatenate([query, tm_permute(query, 1, 0, 0)], axis=0)
    for step in range(1, Z // 2 + 1):
        got = [up] if step == Z // 2 else [up, down]
        if step < Z // 2:
            up = tm_permute(up, 0, 1, 0)
        if step < Z // 2 - 1:
            down = tm_permute(down, 0, -1, 0)
        for piece in got:
            kvs += [piece, tm_permute(piece, 0, 0, 1)]

    send, keep, keep_lse = attention(signs, bases, slope, queries, kvs, 128 ** (-0.5) * LOG2E)
    got = tm_permute(send, 1, 0, 0)
    partial = merge_project(keep, keep_lse, got, w_out_t)
    heads = lax.axis_size("head")
    pieces = lax.all_to_all(
        partial.reshape(heads, rows // heads, width), "head", split_axis=0, concat_axis=0, tiled=True
    )
    return jnp.sum(pieces.astype(F32), axis=0).astype(BF16)


def solution(mesh):
    in_specs = (P("tm", None), P(), P(None, "tm", "head"), P("head"), P("head", "tm"))
    out_specs = P(("tm", "head"), None)
    return jax.shard_map(local, mesh=mesh, in_specs=in_specs, out_specs=out_specs, check_vma=False)
```

time: 151 us -> 125 us (0.83); the launches traced: 149 us -> 125 us
  Pallas kernels: 50.5 us -> 19.8 us
  waiting for transfers between devices: 26.6 us -> 39.7 us
  other arithmetic: 8.62 us -> 4.88 us
    pallas_call x6 -> x1, Pallas kernels: 47.6 us -> 16.9 us  [attention(): pl.pallas_call(functools.partial(attention_kernel, shards, scale, blocks)...]
    ppermute x20 -> x26, waiting for transfers between devices: 26.6 us -> 39.7 us  [tm_permute(): return lax.ppermute(x, 'tm', pairs)]
    another operation x1 -> x0, other arithmetic: 2.41 us -> none  [local(): bias = jnp.stack([-ahead, ahead, -apart, apart])]
    ppermute x20 -> x26, starting transfers between devices: 34.9 us -> 33.8 us  [tm_permute(): return lax.ppermute(x, 'tm', pairs)]
  transfers between devices with their start and end apart: 20 -> 26, of which waited for: 10 -> 12; matrix products, arithmetic and copies ran while one was open for 5% -> 3% of each run, Pallas kernels for 25% -> 0%
where the time goes in v3:
time: 125 us
  waiting for transfers between devices  39.7 us (32%)
  starting transfers between devices  33.8 us (27%)
  blocking collectives  20.5 us (16%)
  Pallas kernels  19.8 us (16%)
  other arithmetic  4.88 us (4%)
  local copies, waits for them, and re-layouts  4.49 us (4%)
    ppermute x26, waiting for transfers between devices, tm_permute(): return lax.ppermute(x, 'tm', pairs)  39.7 us
    ppermute x26, starting transfers between devices, tm_permute(): return lax.ppermute(x, 'tm', pairs)  33.8 us
    all_to_all x1, blocking collectives, local(): lax.all_to_all(partial.reshape(heads, rows // heads, width), 'head', spli...  20.5 us
    pallas_call x1, Pallas kernels, attention(): pl.pallas_call(functools.partial(attention_kernel, shards, scale, blocks)...  16.9 us
    unnamed x36, local copies, waits for them, and re-layouts  2.95 us
    pallas_call x1, Pallas kernels, merge_project(): pl.pallas_call(merge_project_kernel, out_shape=jax.ShapeDtypeStruct((rows...  2.89 us
  transfers between devices with their start and end apart: 26, of which 12 were waited for; matrix products, arithmetic and copies ran while one was open for 3% of the time, Pallas kernels for 0%

profile of v3, /device:TPU:16, one launch (start us, length us, event | category | flops | bytes accessed | tf_op | source)
XLA Modules:
  0.0 124.8 jit_solution(18320498924633832116)
XLA Ops:
  0.0 0.8 pad_maximum_fusion.3
  0.8 5.9 %collective-permute-start = (bf16[128,128]{1,0:T(8,128)(2,1)S(1)}, bf16[128,128]{1,0:T(8,128)(2,1)S(1)}, u32[]{:S(2)}, u32[]{:S(2)}) collective-permute-start(bf16[128,128]{1,0:T(8,128)(2,1)S(1)} %pad_maximum_fusion.3), channel_id=1, source_target_pairs={{16,0},{24,8},{32,16},{40,24},{48,32},{56,40},{64,48},{72,56},{80,... | collective-permute-start | bytes 98312 | tf_op jit(solution)/shard_map/ppermute | solution.py:24
  6.6 0.0 collective-permute-start.1
  6.7 0.8 bitcast_dynamic-update-slice_fusion.7
  7.4 0.8 collective-permute-done
  8.2 3.5 %collective-permute-start.2 = (bf16[128,128]{1,0:T(8,128)(2,1)S(1)}, bf16[128,128]{1,0:T(8,128)(2,1)S(1)}, u32[]{:S(2)}, u32[]{:S(2)}) collective-permute-start(bf16[128,128]{1,0:T(8,128)(2,1)S(1)} %collective-permute-done), channel_id=1, source_target_pairs={{16,0},{24,8},{32,16},{40,24},{48,32},{56,40},{64,48},{72,56},{80,... | collective-permute-start | bytes 98312 | tf_op jit(solution)/shard_map/ppermute | solution.py:24
  11.8 1.6 %collective-permute-done.2 = bf16[128,128]{1,0:T(8,128)(2,1)S(1)} collective-permute-done((bf16[128,128]{1,0:T(8,128)(2,1)S(1)}, bf16[128,128]{1,0:T(8,128)(2,1)S(1)}, u32[]{:S(2)}, u32[]{:S(2)}) %collective-permute-start.2) | collective-permute-done | bytes 32800 | tf_op jit(solution)/shard_map/ppermute | solution.py:24
  13.3 3.5 %collective-permute-start.4 = (bf16[128,128]{1,0:T(8,128)(2,1)S(1)}, bf16[128,128]{1,0:T(8,128)(2,1)S(1)}, u32[]{:S(2)}, u32[]{:S(2)}) collective-permute-start(bf16[128,128]{1,0:T(8,128)(2,1)S(1)} %collective-permute-done.2), channel_id=1, source_target_pairs={{16,0},{24,8},{32,16},{40,24},{48,32},{56,40},{64,48},{72,56},{80,... | collective-permute-start | bytes 98312 | tf_op jit(solution)/shard_map/ppermute | solution.py:24
  16.9 0.0 collective-permute-done.3
  16.9 0.0 collective-permute-start.5
  16.9 1.6 %collective-permute-done.4 = bf16[128,128]{1,0:T(8,128)(2,1)S(1)} collective-permute-done((bf16[128,128]{1,0:T(8,128)(2,1)S(1)}, bf16[128,128]{1,0:T(8,128)(2,1)S(1)}, u32[]{:S(2)}, u32[]{:S(2)}) %collective-permute-start.4) | collective-permute-done | bytes 32800 | tf_op jit(solution)/shard_map/ppermute | solution.py:24
  18.5 3.5 %collective-permute-start.6 = (bf16[128,128]{1,0:T(8,128)(2,1)S(1)}, bf16[128,128]{1,0:T(8,128)(2,1)S(1)}, u32[]{:S(2)}, u32[]{:S(2)}) collective-permute-start(bf16[128,128]{1,0:T(8,128)(2,1)S(1)} %collective-permute-done.4), channel_id=1, source_target_pairs={{16,0},{24,8},{32,16},{40,24},{48,32},{56,40},{64,48},{72,56},{80,... | collective-permute-start | bytes 98312 | tf_op jit(solution)/shard_map/ppermute | solution.py:24
  22.0 0.0 collective-permute-done.5
  22.0 1.6 %collective-permute-done.6 = bf16[128,128]{1,0:T(8,128)(2,1)S(1)} collective-permute-done((bf16[128,128]{1,0:T(8,128)(2,1)S(1)}, bf16[128,128]{1,0:T(8,128)(2,1)S(1)}, u32[]{:S(2)}, u32[]{:S(2)}) %collective-permute-start.6) | collective-permute-done | bytes 32800 | tf_op jit(solution)/shard_map/ppermute | solution.py:24
  23.6 0.3 collective-permute-start.7
  23.9 7.5 %collective-permute-done.7 = bf16[8,128,128]{2,1,0:T(8,128)(2,1)S(1)} collective-permute-done((bf16[8,128,128]{2,1,0:T(8,128)(2,1)S(1)}, bf16[8,128,128]{2,1,0:T(8,128)(2,1)S(1)}, u32[]{:S(2)}, u32[]{:S(2)}) %collective-permute-start.7) | collective-permute-done | bytes 262176 | tf_op jit(solution)/shard_map/ppermute | solution.py:24
  31.5 0.1 pad_maximum_fusion.1
  31.6 0.1 collective-permute-start.8
  31.7 0.3 fusion
  32.0 1.6 %collective-permute-done.8 = bf16[2,8,128,128]{3,2,1,0:T(8,128)(2,1)S(1)} collective-permute-done((bf16[2,8,128,128]{3,2,1,0:T(8,128)(2,1)S(1)}, bf16[2,8,128,128]{3,2,1,0:T(8,128)(2,1)S(1)}, u32[]{:S(2)}, u32[]{:S(2)}) %collective-permute-start.8) | collective-permute-done | bytes 524320 | tf_op jit(solution)/shard_map/ppermute | solution.py:24
  33.6 0.1 select_bitcast_fusion.1
  33.7 0.1 pad_maximum_fusion
  33.8 0.1 slice_bitcast_fusion
  33.8 0.0 copy-start.17
  33.8 0.5 copy.9
  34.4 0.1 copy-done.17
  34.5 0.8 convolution_convert_fusion
  35.3 3.6 %collective-permute-start.11 = (bf16[512,256]{1,0:T(8,128)(2,1)S(1)}, bf16[512,256]{1,0:T(8,128)(2,1)S(1)}, u32[]{:S(2)}, u32[]{:S(2)}) collective-permute-start(bf16[512,256]{1,0:T(8,128)(2,1)S(1)} %slice.18.refs_4_), channel_id=1, source_target_pairs={{16,0},{24,8},{32,16},{40,24},{48,32},{56,40},{64,48},{72,56},{80,... | collective-permute-start | bytes 786440 | tf_op jit(solution)/shard_map/ppermute | solution.py:24
  38.9 5.9 %collective-permute-done.11.refs_6_ = bf16[512,256]{1,0:T(8,128)(2,1)S(1)} collective-permute-done((bf16[512,256]{1,0:T(8,128)(2,1)S(1)}, bf16[512,256]{1,0:T(8,128)(2,1)S(1)}, u32[]{:S(2)}, u32[]{:S(2)}) %collective-permute-start.11) | collective-permute-done | bytes 262176 | tf_op jit(solution)/shard_map/ppermute | solution.py:24
  44.8 3.7 %collective-permute-start.15 = (bf16[512,256]{1,0:T(8,128)(2,1)S(1)}, bf16[512,256]{1,0:T(8,128)(2,1)S(1)}, u32[]{:S(2)}, u32[]{:S(2)}) collective-permute-start(bf16[512,256]{1,0:T(8,128)(2,1)S(1)} %collective-permute-done.11.refs_6_), channel_id=1, source_target_pairs={{16,0},{24,8},{32,16},{40,24},{48,32},{56,40},{64,48},{72,56},{80,... | collective-permute-start | bytes 786440 | tf_op jit(solution)/shard_map/ppermute | solution.py:24
  48.5 0.4 collective-permute-start.9
  48.9 0.0 collective-permute-start.17
  48.9 4.6 %collective-permute-done.15.refs_10_ = bf16[512,256]{1,0:T(8,128)(2,1)S(1)} collective-permute-done((bf16[512,256]{1,0:T(8,128)(2,1)S(1)}, bf16[512,256]{1,0:T(8,128)(2,1)S(1)}, u32[]{:S(2)}, u32[]{:S(2)}) %collective-permute-start.15) | collective-permute-done | bytes 262176 | tf_op jit(solution)/shard_map/ppermute | solution.py:24
  53.5 3.7 %collective-permute-start.19 = (bf16[512,256]{1,0:T(8,128)(2,1)S(1)}, bf16[512,256]{1,0:T(8,128)(2,1)S(1)}, u32[]{:S(2)}, u32[]{:S(2)}) collective-permute-start(bf16[512,256]{1,0:T(8,128)(2,1)S(1)} %collective-permute-done.15.refs_10_), channel_id=1, source_target_pairs={{16,0},{24,8},{32,16},{40,24},{48,32},{56,40},{64,48},{72,56},{80,... | collective-permute-start | bytes 786440 | tf_op jit(solution)/shard_map/ppermute | solution.py:24
  57.2 0.1 collective-permute-start.10
  57.3 0.5 collective-permute-start.14
  57.8 0.0 collective-permute-done.9
  57.8 0.1 collective-permute-start.12
  57.9 0.0 collective-permute-start.21
  58.0 3.4 %collective-permute-done.19.refs_14_ = bf16[512,256]{1,0:T(8,128)(2,1)S(1)} collective-permute-done((bf16[512,256]{1,0:T(8,128)(2,1)S(1)}, bf16[512,256]{1,0:T(8,128)(2,1)S(1)}, u32[]{:S(2)}, u32[]{:S(2)}) %collective-permute-start.19) | collective-permute-done | bytes 262176 | tf_op jit(solution)/shard_map/ppermute | solution.py:24
  61.4 3.7 %collective-permute-start.23 = (bf16[512,256]{1,0:T(8,128)(2,1)S(1)}, bf16[512,256]{1,0:T(8,128)(2,1)}, u32[]{:S(2)}, u32[]{:S(2)}) collective-permute-start(bf16[512,256]{1,0:T(8,128)(2,1)S(1)} %collective-permute-done.19.refs_14_), channel_id=1, source_target_pairs={{16,0},{24,8},{32,16},{40,24},{48,32},{56,40},{64,48},{72,56},{80,... | collective-permute-start | bytes 786440 | tf_op jit(solution)/shard_map/ppermute | solution.py:24
  65.0 0.1 broadcast_subtract_fusion
  65.8 0.1 sub.44
  65.9 0.6 fusion.14
  66.4 0.0 collective-permute-done.14.refs_9_
  66.4 0.5 collective-permute-start.16
  66.9 0.1 collective-permute-start.20
  67.0 0.8 collective-permute-done.21.refs_16_
  67.9 1.1 collective-permute-done.23.refs_18_
  68.9 0.6 compare_select_fusion.8.refs_0_
  69.5 0.7 pad_maximum_fusion.2.refs_3_
  70.3 0.6 copy-done.12
  70.9 0.1 copy-done.13
  71.1 0.1 copy-done.15
  71.1 0.5 copy-done.14
  71.7 0.7 copy-done.16
  72.4 16.9 %shard_map.73 = (bf16[512,256]{1,0:T(8,128)(2,1)}, f32[512,128]{1,0:T(8,128)}, f32[512,128]{1,0:T(8,128)}) custom-call(f32[32]{0:T(128)} %compare_select_fusion.8.refs_0_, f32[32]{0:T(128)} %get-tuple-element.11.refs_1_, f32[1]{0:T(128)} %mul.53.refs_2_, bf16[1024,128]{1,0:T(8,128)(2,1)} %pad_maximum_fusion.2.refs_3_, bf16[512,256]{1,0:T(8,128)(2,1)} %copy-done.1, ...), custom_call_target="tpu_custom_call" | custom-call | flops 8589934592 | bytes 5242880 | tf_op jit(solution)/shard_map/pallas_call | solution.py:109
  89.3 0.5 collective-permute-start.25
  89.8 0.7 slice.19
  90.5 9.3 %collective-permute-done.25.got_ref = bf16[512,256]{1,0:T(8,128)(2,1)S(1)} collective-permute-done((bf16[512,256]{1,0:T(8,128)(2,1)}, bf16[512,256]{1,0:T(8,128)(2,1)S(1)}, u32[]{:S(2)}, u32[]{:S(2)}) %collective-permute-start.25) | collective-permute-done | bytes 262176 | tf_op jit(solution)/shard_map/ppermute | solution.py:24
  99.8 0.7 copy-done.2
  100.5 2.9 %shard_map.74 = bf16[512,1024]{1,0:T(8,128)(2,1)} custom-call(f32[512,128]{1,0:T(8,128)} %get-tuple-element.8.out_ref, f32[512,128]{1,0:T(8,128)} %get-tuple-element.9.lse_ref, bf16[512,256]{1,0:T(8,128)(2,1)} %copy-done.2, bf16[1024,128]{1,0:T(8,128)(2,1)} %bitcast.43), custom_call_target="tpu_custom_call" | custom-call | tf_op jit(solution)/shard_map/pallas_call | solution.py:152
  103.4 20.5 %all_to_all.5 = bf16[8,64,1024]{2,1,0:T(8,128)(2,1)S(1)} all-to-all(bf16[8,64,1024]{2,1,0:T(8,128)(2,1)} %bitcast.41), channel_id=1, replica_groups=mesh['tm'=32,'head'=8] {'head'}, dimensions={0} | all-to-all | bytes 2097152 | tf_op jit(solution)/shard_map/all_to_all | solution.py:220
  124.0 0.8 reduce_sum.22
  (57 shorter events, 0.3 us)
Async XLA Ops:
  0.8 7.5 %collective-permute-start = (bf16[128,128]{1,0:T(8,128)(2,1)S(1)}, bf16[128,128]{1,0:T(8,128)(2,1)S(1)}, u32[]{:S(2)}, u32[]{:S(2)}) collective-permute-start(bf16[128,128]{1,0:T(8,128)(2,1)S(1)} %pad_maximum_fusion.3), channel_id=1, source_target_pairs={{16,0},{24,8},{32,16},{40,24},{48,32},{56,40},{64,48},{72,56},{80,... | collective-permute-start | bytes 98312 | tf_op jit(solution)/shard_map/ppermute | solution.py:24
  6.6 5.1 %collective-permute-start.1 = (bf16[128,128]{1,0:T(8,128)(2,1)S(1)}, bf16[128,128]{1,0:T(8,128)(2,1)S(1)}, u32[]{:S(2)}, u32[]{:S(2)}) collective-permute-start(bf16[128,128]{1,0:T(8,128)(2,1)S(1)} %pad_maximum_fusion.3), channel_id=1, source_target_pairs={{112,0},{120,8},{0,16},{8,24},{16,32},{24,40},{32,48},{40,56},{48,... | collective-permute-start | bytes 98312 | tf_op jit(solution)/shard_map/ppermute | solution.py:24
  8.2 5.1 %collective-permute-start.2 = (bf16[128,128]{1,0:T(8,128)(2,1)S(1)}, bf16[128,128]{1,0:T(8,128)(2,1)S(1)}, u32[]{:S(2)}, u32[]{:S(2)}) collective-permute-start(bf16[128,128]{1,0:T(8,128)(2,1)S(1)} %collective-permute-done), channel_id=1, source_target_pairs={{16,0},{24,8},{32,16},{40,24},{48,32},{56,40},{64,48},{72,56},{80,... | collective-permute-start | bytes 98312 | tf_op jit(solution)/shard_map/ppermute | solution.py:24
  11.7 5.1 %collective-permute-start.3 = (bf16[128,128]{1,0:T(8,128)(2,1)S(1)}, bf16[128,128]{1,0:T(8,128)(2,1)S(1)}, u32[]{:S(2)}, u32[]{:S(2)}) collective-permute-start(bf16[128,128]{1,0:T(8,128)(2,1)S(1)} %collective-permute-done.1), channel_id=1, source_target_pairs={{112,0},{120,8},{0,16},{8,24},{16,32},{24,40},{32,48},{40,56},{48,... | collective-permute-start | bytes 98312 | tf_op jit(solution)/shard_map/ppermute | solution.py:24
  13.3 5.1 %collective-permute-start.4 = (bf16[128,128]{1,0:T(8,128)(2,1)S(1)}, bf16[128,128]{1,0:T(8,128)(2,1)S(1)}, u32[]{:S(2)}, u32[]{:S(2)}) collective-permute-start(bf16[128,128]{1,0:T(8,128)(2,1)S(1)} %collective-permute-done.2), channel_id=1, source_target_pairs={{16,0},{24,8},{32,16},{40,24},{48,32},{56,40},{64,48},{72,56},{80,... | collective-permute-start | bytes 98312 | tf_op jit(solution)/shard_map/ppermute | solution.py:24
  16.9 5.1 %collective-permute-start.5 = (bf16[128,128]{1,0:T(8,128)(2,1)S(1)}, bf16[128,128]{1,0:T(8,128)(2,1)S(1)}, u32[]{:S(2)}, u32[]{:S(2)}) collective-permute-start(bf16[128,128]{1,0:T(8,128)(2,1)S(1)} %collective-permute-done.3), channel_id=1, source_target_pairs={{112,0},{120,8},{0,16},{8,24},{16,32},{24,40},{32,48},{40,56},{48,... | collective-permute-start | bytes 98312 | tf_op jit(solution)/shard_map/ppermute | solution.py:24
  18.5 5.1 %collective-permute-start.6 = (bf16[128,128]{1,0:T(8,128)(2,1)S(1)}, bf16[128,128]{1,0:T(8,128)(2,1)S(1)}, u32[]{:S(2)}, u32[]{:S(2)}) collective-permute-start(bf16[128,128]{1,0:T(8,128)(2,1)S(1)} %collective-permute-done.4), channel_id=1, source_target_pairs={{16,0},{24,8},{32,16},{40,24},{48,32},{56,40},{64,48},{72,56},{80,... | collective-permute-start | bytes 98312 | tf_op jit(solution)/shard_map/ppermute | solution.py:24
  23.6 7.9 %collective-permute-start.7 = (bf16[8,128,128]{2,1,0:T(8,128)(2,1)S(1)}, bf16[8,128,128]{2,1,0:T(8,128)(2,1)S(1)}, u32[]{:S(2)}, u32[]{:S(2)}) collective-permute-start(bf16[8,128,128]{2,1,0:T(8,128)(2,1)S(1)} %bitcast_dynamic-update-slice_fusion), channel_id=1, source_target_pairs={{128,0},{136,8},{144,16},{152,24},{160,32},{168,40},{176,48},{184,... | collective-permute-start | bytes 786440 | tf_op jit(solution)/shard_map/ppermute | solution.py:24
  23.9 7.8 %copy-start = (bf16[512,1024]{1,0:T(8,128)(2,1)S(1)}, bf16[512,1024]{1,0:T(8,128)(2,1)}, u32[]{:S(2)}) copy-start(bf16[512,1024]{1,0:T(8,128)(2,1)} %param.7) | copy-start | bytes 3145732
  31.6 2.0 %collective-permute-start.8 = (bf16[2,8,128,128]{3,2,1,0:T(8,128)(2,1)S(1)}, bf16[2,8,128,128]{3,2,1,0:T(8,128)(2,1)S(1)}, u32[]{:S(2)}, u32[]{:S(2)}) collective-permute-start(bf16[2,8,128,128]{3,2,1,0:T(8,128)(2,1)S(1)} %pad_maximum_fusion.1), channel_id=1, source_target_pairs={{8,0},{0,8},{24,16},{16,24},{40,32},{32,40},{56,48},{48,56},{72,64... | collective-permute-start | bytes 1572872 | tf_op jit(solution)/shard_map/ppermute | solution.py:24
  33.8 0.7 copy-start.17
  34.5 22.7 %copy-start.3 = (s32[16]{0:T(128)S(1)}, s32[16]{0:T(128)}, u32[]{:S(2)}) copy-start(s32[16]{0:T(128)} %constant.149.clone) | copy-start | bytes 196
  34.5 22.7 %copy-start.4 = (s32[16]{0:T(128)S(1)}, s32[16]{0:T(128)}, u32[]{:S(2)}) copy-start(s32[16]{0:T(128)} %constant.148.clone) | copy-start | bytes 196
  35.3 37.1 %copy-start.1 = (bf16[512,256]{1,0:T(8,128)(2,1)}, bf16[512,256]{1,0:T(8,128)(2,1)S(1)}, u32[]{:S(2)}) copy-start(bf16[512,256]{1,0:T(8,128)(2,1)S(1)} %slice.18.refs_4_) | copy-start | bytes 786436
  35.3 9.5 %collective-permute-start.11 = (bf16[512,256]{1,0:T(8,128)(2,1)S(1)}, bf16[512,256]{1,0:T(8,128)(2,1)S(1)}, u32[]{:S(2)}, u32[]{:S(2)}) collective-permute-start(bf16[512,256]{1,0:T(8,128)(2,1)S(1)} %slice.18.refs_4_), channel_id=1, source_target_pairs={{16,0},{24,8},{32,16},{40,24},{48,32},{56,40},{64,48},{72,56},{80,... | collective-permute-start | bytes 786440 | tf_op jit(solution)/shard_map/ppermute | solution.py:24
  38.9 10.0 %collective-permute-start.13 = (bf16[512,256]{1,0:T(8,128)(2,1)S(1)}, bf16[512,256]{1,0:T(8,128)(2,1)S(1)}, u32[]{:S(2)}, u32[]{:S(2)}) collective-permute-start(bf16[512,256]{1,0:T(8,128)(2,1)S(1)} %slice.18.refs_4_), channel_id=1, source_target_pairs={{112,0},{120,8},{0,16},{8,24},{16,32},{24,40},{32,48},{40,56},{48,... | collective-permute-start | bytes 786440 | tf_op jit(solution)/shard_map/ppermute | solution.py:24
  44.8 27.6 %copy-start.5 = (bf16[512,256]{1,0:T(8,128)(2,1)}, bf16[512,256]{1,0:T(8,128)(2,1)S(1)}, u32[]{:S(2)}) copy-start(bf16[512,256]{1,0:T(8,128)(2,1)S(1)} %collective-permute-done.11.refs_6_) | copy-start | bytes 786436
  44.8 8.7 %collective-permute-start.15 = (bf16[512,256]{1,0:T(8,128)(2,1)S(1)}, bf16[512,256]{1,0:T(8,128)(2,1)S(1)}, u32[]{:S(2)}, u32[]{:S(2)}) collective-permute-start(bf16[512,256]{1,0:T(8,128)(2,1)S(1)} %collective-permute-done.11.refs_6_), channel_id=1, source_target_pairs={{16,0},{24,8},{32,16},{40,24},{48,32},{56,40},{64,48},{72,56},{80,... | collective-permute-start | bytes 786440 | tf_op jit(solution)/shard_map/ppermute | solution.py:24
  48.5 9.3 %collective-permute-start.9 = (bf16[512,128]{1,0:T(8,128)(2,1)S(1)}, bf16[512,128]{1,0:T(8,128)(2,1)S(1)}, u32[]{:S(2)}, u32[]{:S(2)}) collective-permute-start(bf16[512,128]{1,0:T(8,128)(2,1)S(1)} %slice.17), channel_id=1, source_target_pairs={{128,0},{136,8},{144,16},{152,24},{160,32},{168,40},{176,48},{184,... | collective-permute-start | bytes 393224 | tf_op jit(solution)/shard_map/ppermute | solution.py:24
  48.9 23.4 %copy-start.6 = (bf16[512,256]{1,0:T(8,128)(2,1)}, bf16[512,256]{1,0:T(8,128)(2,1)S(1)}, u32[]{:S(2)}) copy-start(bf16[512,256]{1,0:T(8,128)(2,1)S(1)} %collective-permute-done.13.refs_8_) | copy-start | bytes 786436
  48.9 9.0 %collective-permute-start.17 = (bf16[512,256]{1,0:T(8,128)(2,1)S(1)}, bf16[512,256]{1,0:T(8,128)(2,1)S(1)}, u32[]{:S(2)}, u32[]{:S(2)}) collective-permute-start(bf16[512,256]{1,0:T(8,128)(2,1)S(1)} %collective-permute-done.13.refs_8_), channel_id=1, source_target_pairs={{112,0},{120,8},{0,16},{8,24},{16,32},{24,40},{32,48},{40,56},{48,... | collective-permute-start | bytes 786440 | tf_op jit(solution)/shard_map/ppermute | solution.py:24
  53.5 18.9 %copy-start.7 = (bf16[512,256]{1,0:T(8,128)(2,1)}, bf16[512,256]{1,0:T(8,128)(2,1)S(1)}, u32[]{:S(2)}) copy-start(bf16[512,256]{1,0:T(8,128)(2,1)S(1)} %collective-permute-done.15.refs_10_) | copy-start | bytes 786436
  53.5 7.8 %collective-permute-start.19 = (bf16[512,256]{1,0:T(8,128)(2,1)S(1)}, bf16[512,256]{1,0:T(8,128)(2,1)S(1)}, u32[]{:S(2)}, u32[]{:S(2)}) collective-permute-start(bf16[512,256]{1,0:T(8,128)(2,1)S(1)} %collective-permute-done.15.refs_10_), channel_id=1, source_target_pairs={{16,0},{24,8},{32,16},{40,24},{48,32},{56,40},{64,48},{72,56},{80,... | collective-permute-start | bytes 786440 | tf_op jit(solution)/shard_map/ppermute | solution.py:24
  57.2 9.2 %collective-permute-start.10 = (bf16[512,256]{1,0:T(8,128)(2,1)S(1)}, bf16[512,256]{1,0:T(8,128)(2,1)S(1)}, u32[]{:S(2)}, u32[]{:S(2)}) collective-permute-start(bf16[512,256]{1,0:T(8,128)(2,1)S(1)} %slice.18.refs_4_), channel_id=1, source_target_pairs={{8,0},{0,8},{24,16},{16,24},{40,32},{32,40},{56,48},{48,56},{72,64... | collective-permute-start | bytes 786440 | tf_op jit(solution)/shard_map/ppermute | solution.py:24
  57.3 9.1 %collective-permute-start.14 = (bf16[512,256]{1,0:T(8,128)(2,1)S(1)}, bf16[512,256]{1,0:T(8,128)(2,1)S(1)}, u32[]{:S(2)}, u32[]{:S(2)}) collective-permute-start(bf16[512,256]{1,0:T(8,128)(2,1)S(1)} %collective-permute-done.13.refs_8_), channel_id=1, source_target_pairs={{8,0},{0,8},{24,16},{16,24},{40,32},{32,40},{56,48},{48,56},{72,64... | collective-permute-start | bytes 786440 | tf_op jit(solution)/shard_map/ppermute | solution.py:24
  57.8 9.1 %collective-permute-start.12 = (bf16[512,256]{1,0:T(8,128)(2,1)S(1)}, bf16[512,256]{1,0:T(8,128)(2,1)}, u32[]{:S(2)}, u32[]{:S(2)}) collective-permute-start(bf16[512,256]{1,0:T(8,128)(2,1)S(1)} %collective-permute-done.11.refs_6_), channel_id=1, source_target_pairs={{8,0},{0,8},{24,16},{16,24},{40,32},{32,40},{56,48},{48,56},{72,64... | collective-permute-start | bytes 786440 | tf_op jit(solution)/shard_map/ppermute | solution.py:24
  57.9 14.4 %copy-start.8 = (bf16[512,256]{1,0:T(8,128)(2,1)}, bf16[512,256]{1,0:T(8,128)(2,1)S(1)}, u32[]{:S(2)}) copy-start(bf16[512,256]{1,0:T(8,128)(2,1)S(1)} %collective-permute-done.17.refs_12_) | copy-start | bytes 786436
  57.9 9.9 %collective-permute-start.21 = (bf16[512,256]{1,0:T(8,128)(2,1)S(1)}, bf16[512,256]{1,0:T(8,128)(2,1)}, u32[]{:S(2)}, u32[]{:S(2)}) collective-permute-start(bf16[512,256]{1,0:T(8,128)(2,1)S(1)} %collective-permute-done.17.refs_12_), channel_id=1, source_target_pairs={{112,0},{120,8},{0,16},{8,24},{16,32},{24,40},{32,48},{40,56},{48,... | collective-permute-start | bytes 786440 | tf_op jit(solution)/shard_map/ppermute | solution.py:24
  61.4 11.0 %copy-start.9 = (bf16[512,256]{1,0:T(8,128)(2,1)}, bf16[512,256]{1,0:T(8,128)(2,1)S(1)}, u32[]{:S(2)}) copy-start(bf16[512,256]{1,0:T(8,128)(2,1)S(1)} %collective-permute-done.19.refs_14_) | copy-start | bytes 786436
  61.4 7.6 %collective-permute-start.23 = (bf16[512,256]{1,0:T(8,128)(2,1)S(1)}, bf16[512,256]{1,0:T(8,128)(2,1)}, u32[]{:S(2)}, u32[]{:S(2)}) collective-permute-start(bf16[512,256]{1,0:T(8,128)(2,1)S(1)} %collective-permute-done.19.refs_14_), channel_id=1, source_target_pairs={{16,0},{24,8},{32,16},{40,24},{48,32},{56,40},{64,48},{72,56},{80,... | collective-permute-start | bytes 786440 | tf_op jit(solution)/shard_map/ppermute | solution.py:24
  66.4 6.0 %copy-start.10 = (bf16[512,256]{1,0:T(8,128)(2,1)}, bf16[512,256]{1,0:T(8,128)(2,1)S(1)}, u32[]{:S(2)}) copy-start(bf16[512,256]{1,0:T(8,128)(2,1)S(1)} %collective-permute-done.10.refs_5_) | copy-start | bytes 786436
  66.4 3.8 %collective-permute-start.18 = (bf16[512,256]{1,0:T(8,128)(2,1)S(1)}, bf16[512,256]{1,0:T(8,128)(2,1)S(1)}, u32[]{:S(2)}, u32[]{:S(2)}) collective-permute-start(bf16[512,256]{1,0:T(8,128)(2,1)S(1)} %collective-permute-done.17.refs_12_), channel_id=1, source_target_pairs={{8,0},{0,8},{24,16},{16,24},{40,32},{32,40},{56,48},{48,56},{72,64... | collective-permute-start | bytes 786440 | tf_op jit(solution)/shard_map/ppermute | solution.py:24
  66.4 6.0 %copy-start.11 = (bf16[512,256]{1,0:T(8,128)(2,1)}, bf16[512,256]{1,0:T(8,128)(2,1)S(1)}, u32[]{:S(2)}) copy-start(bf16[512,256]{1,0:T(8,128)(2,1)S(1)} %collective-permute-done.14.refs_9_) | copy-start | bytes 786436
  66.4 3.8 %collective-permute-start.16 = (bf16[512,256]{1,0:T(8,128)(2,1)S(1)}, bf16[512,256]{1,0:T(8,128)(2,1)S(1)}, u32[]{:S(2)}, u32[]{:S(2)}) collective-permute-start(bf16[512,256]{1,0:T(8,128)(2,1)S(1)} %collective-permute-done.15.refs_10_), channel_id=1, source_target_pairs={{8,0},{0,8},{24,16},{16,24},{40,32},{32,40},{56,48},{48,56},{72,64... | collective-permute-start | bytes 786440 | tf_op jit(solution)/shard_map/ppermute | solution.py:24
  66.9 3.3 %collective-permute-start.20 = (bf16[512,256]{1,0:T(8,128)(2,1)S(1)}, bf16[512,256]{1,0:T(8,128)(2,1)S(1)}, u32[]{:S(2)}, u32[]{:S(2)}) collective-permute-start(bf16[512,256]{1,0:T(8,128)(2,1)S(1)} %collective-permute-done.19.refs_14_), channel_id=1, source_target_pairs={{8,0},{0,8},{24,16},{16,24},{40,32},{32,40},{56,48},{48,56},{72,64... | collective-permute-start | bytes 786440 | tf_op jit(solution)/shard_map/ppermute | solution.py:24
  67.9 2.4 %collective-permute-start.22 = (bf16[512,256]{1,0:T(8,128)(2,1)}, bf16[512,256]{1,0:T(8,128)(2,1)S(1)}, u32[]{:S(2)}, u32[]{:S(2)}) collective-permute-start(bf16[512,256]{1,0:T(8,128)(2,1)} %collective-permute-done.21.refs_16_), channel_id=1, source_target_pairs={{8,0},{0,8},{24,16},{16,24},{40,32},{32,40},{56,48},{48,56},{72,64... | collective-permute-start | bytes 786440 | tf_op jit(solution)/shard_map/ppermute | solution.py:24
  68.9 2.0 %collective-permute-start.24 = (bf16[512,256]{1,0:T(8,128)(2,1)}, bf16[512,256]{1,0:T(8,128)(2,1)S(1)}, u32[]{:S(2)}, u32[]{:S(2)}) collective-permute-start(bf16[512,256]{1,0:T(8,128)(2,1)} %collective-permute-done.23.refs_18_), channel_id=1, source_target_pairs={{8,0},{0,8},{24,16},{16,24},{40,32},{32,40},{56,48},{48,56},{72,64... | collective-permute-start | bytes 786440 | tf_op jit(solution)/shard_map/ppermute | solution.py:24
  70.2 0.7 copy-start.12
  70.3 0.8 copy-start.13
  70.3 0.9 copy-start.15
  70.9 0.7 copy-start.14
  71.7 0.7 copy-start.16
  89.3 10.5 %collective-permute-start.25 = (bf16[512,256]{1,0:T(8,128)(2,1)}, bf16[512,256]{1,0:T(8,128)(2,1)S(1)}, u32[]{:S(2)}, u32[]{:S(2)}) collective-permute-start(bf16[512,256]{1,0:T(8,128)(2,1)} %get-tuple-element.10), channel_id=1, source_target_pairs={{128,0},{136,8},{144,16},{152,24},{160,32},{168,40},{176,48},{184,... | collective-permute-start | bytes 786440 | tf_op jit(solution)/shard_map/ppermute | solution.py:24
  99.8 0.7 copy-start.2

commit v4 on v3

--- a/solution.py
+++ b/solution.py
@@ -12,6 +12,7 @@
 LOG2E = math.log2(math.e)
 YH, Z, CORE = 2, 8, 2
 TM = YH * Z * CORE
+YL, X = 2, 4
 
 
 def tm_permute(x, d_yh, d_z, d_core):
@@ -22,6 +23,14 @@
                 source = ((yh + d_yh) % YH * Z + (z + d_z) % Z) * CORE + (core + d_core) % CORE
                 pairs.append((source, (yh * Z + z) * CORE + core))
     return lax.ppermute(x, "tm", pairs)
+
+
+def head_permute(x, d_yl, d_x):
+    pairs = []
+    for yl in range(YL):
+        for column in range(X):
+            pairs.append(((yl + d_yl) % YL * X + (column + d_x) % X, yl * X + column))
+    return lax.ppermute(x, "head", pairs)
 
 
 def split_bf16(x):
@@ -139,20 +148,43 @@
     return (out_a * part_a + out_b * part_b) / both, top + jnp.log2(both)
 
 
-def merge_project_kernel(out_ref, lse_ref, got_ref, w_ref, partial_ref):
+def merge_kernel(out_ref, lse_ref, got_ref, mixed_ref):
     got, got_lse = unpack_partial(got_ref[...])
-    out, _ = merge(out_ref[...], lse_ref[...], got, got_lse)
-    partial_ref[...] = lax.dot_general(
-        out.astype(BF16), w_ref[...], (((1,), (1,)), ((), ())), preferred_element_type=F32
-    ).astype(BF16)
-
-
-def merge_project(out, lse, got, w_out_t):
-    rows, width = out.shape[0], w_out_t.shape[0]
+    mixed_ref[...] = merge(out_ref[...], lse_ref[...], got, got_lse)[0].astype(BF16)
+
+
+def merge_halves(out, lse, got):
+    return pl.pallas_call(merge_kernel, out_shape=jax.ShapeDtypeStruct(out.shape, BF16))(out, lse, got)
+
+
+def output_kernel(head_ref, mixed_ref, *refs):
+    out_ref = refs[-1]
+    total = None
+    for j, weight_ref in enumerate(refs[:-1]):
+        for turn in range(YL):
+            part = lax.dot_general(
+                mixed_ref[head_ref[YL * j + turn]],
+                weight_ref[turn],
+                (((1,), (1,)), ((), ())),
+                preferred_element_type=F32,
+            )
+            total = part if total is None else total + part
+    out_ref[...] = total.astype(BF16)
+
+
+def output_projection(heads, mixed, weights):
+    rows, width = mixed.shape[1], weights[0].shape[1]
     return pl.pallas_call(
-        merge_project_kernel,
+        output_kernel,
         out_shape=jax.ShapeDtypeStruct((rows, width), BF16),
-    )(out, lse, got, w_out_t)
+        grid_spec=pltpu.PrefetchScalarGridSpec(
+            num_scalar_prefetch=1,
+            grid=(1,),
+            in_specs=[pl.BlockSpec(mixed.shape, lambda i, _: (0, 0, 0))]
+            + [pl.BlockSpec(w.shape, lambda i, _: (0, 0, 0)) for w in weights],
+            out_specs=pl.BlockSpec((rows, width), lambda i, _: (0, 0)),
+        ),
+    )(heads, mixed, *weights)
 
 
 def local(frames, norm_gain, w_qkv, slopes, w_out):
@@ -162,15 +194,14 @@
 
     part = w_qkv.shape[1]
     own = jnp.concatenate([w_qkv.reshape(3 * part, 128), w_out.T], axis=0)
+    above, below = tm_permute(own, 0, 1, 0), tm_permute(own, 0, -1, 0)
+    trio = jnp.stack([below, own, above])
+    high = tm_permute(trio, 0, 3, 0)
+    low = tm_permute(trio[1:], 0, -3, 0)
     held = jnp.zeros((Z,) + own.shape, BF16)
-    held = lax.dynamic_update_slice(held, own[None], (z, 0, 0))
-    up = down = own
-    for step in range(1, Z // 2 + 1):
-        up = tm_permute(up, 0, 1, 0)
-        held = lax.dynamic_update_slice(held, up[None], ((z + step) % Z, 0, 0))
-        if step < Z // 2:
-            down = tm_permute(down, 0, -1, 0)
-            held = lax.dynamic_update_slice(held, down[None], ((z - step) % Z, 0, 0))
+    found = [low[0], low[1], below, own, above, high[0], high[1], high[2]]
+    for move, piece in zip(range(-3, 5), found):
+        held = lax.dynamic_update_slice(held, piece[None], ((z + move) % Z, 0, 0))
     other = tm_permute(held, 1, 0, 0)
     flip = yh == 1
     held = jnp.stack([jnp.where(flip, other, held), jnp.where(flip, held, other)])
@@ -205,6 +236,15 @@
     kvs = [kv, tm_permute(kv, 0, 0, 1)]
     queries = jnp.concatenate([query, tm_permute(query, 1, 0, 0)], axis=0)
     for step in range(1, Z // 2 + 1):
+        if step == 1:
+            up, w_out_t = lax.optimization_barrier((up, w_out_t))
+            weights = [jnp.stack([w_out_t, head_permute(w_out_t, 1, 0)])]
+        elif step == 2:
+            up, weights[0] = lax.optimization_barrier((up, weights[0]))
+            weights += [head_permute(weights[0], 0, 1), head_permute(weights[0], 0, -1)]
+        elif step == 4:
+            up, weights[1] = lax.optimization_barrier((up, weights[1]))
+            weights.append(head_permute(weights[1], 0, 1))
         got = [up] if step == Z // 2 else [up, down]
         if step < Z // 2:
             up = tm_permute(up, 0, 1, 0)
@@ -215,12 +255,12 @@
 
     send, keep, keep_lse = attention(signs, bases, slope, queries, kvs, 128 ** (-0.5) * LOG2E)
     got = tm_permute(send, 1, 0, 0)
-    partial = merge_project(keep, keep_lse, got, w_out_t)
-    heads = lax.axis_size("head")
-    pieces = lax.all_to_all(
-        partial.reshape(heads, rows // heads, width), "head", split_axis=0, concat_axis=0, tiled=True
-    )
-    return jnp.sum(pieces.astype(F32), axis=0).astype(BF16)
+    mixed = merge_halves(keep, keep_lse, got).reshape(YL * X, rows // (YL * X), 128)
+    mixed = lax.all_to_all(mixed, "head", split_axis=0, concat_axis=0, tiled=True)
+    place = lax.axis_index("head")
+    turn, shift = jnp.array([0, 1] * X, jnp.int32), jnp.array([0, 0, 1, 1, 3, 3, 2, 2], jnp.int32)
+    heads = (place // X + turn) % YL * X + (place + shift) % X
+    return output_projection(heads, mixed, weights)
 
 
 def solution(mesh):

time: 125 us -> 127 us (1.016); the launches traced: 125 us -> 125 us
  blocking collectives: 20.5 us -> 0 us
  waiting for transfers between devices: 39.7 us -> 59.1 us
  Pallas kernels: 19.8 us -> 22.6 us
    all_to_all x1 -> x0, blocking collectives: 20.5 us -> none  [local(): lax.all_to_all(partial.reshape(heads, rows // heads, width), 'head', spli...]
    ppermute x26 -> x23, starting transfers between devices: 33.8 us -> 21.9 us  [tm_permute(): return lax.ppermute(x, 'tm', pairs)]
    ppermute x26 -> x23, waiting for transfers between devices: 39.7 us -> 48.9 us  [tm_permute(): return lax.ppermute(x, 'tm', pairs)]
    ppermute x0 -> x4, starting transfers between devices: none -> 7.42 us  [head_permute(): return lax.ppermute(x, 'head', pairs)]
    all_to_all x0 -> x1, waiting for transfers between devices: none -> 6.06 us  [local(): lax.all_to_all(mixed, 'head', split_axis=0, concat_axis=0, tiled=True)]
    ppermute x0 -> x4, waiting for transfers between devices: none -> 4.18 us  [head_permute(): return lax.ppermute(x, 'head', pairs)]
    all_to_all x0 -> x1, starting transfers between devices: none -> 3.5 us  [local(): lax.all_to_all(mixed, 'head', split_axis=0, concat_axis=0, tiled=True)]
    pallas_call x1 -> x2, Pallas kernels: 2.89 us -> 5.75 us  [the longest x1 3.7 us: output_projection(): pl.pallas_call(output_kernel, out_shape=jax.ShapeDtypeStruct((rows, width...]
  transfers between devices with their start and end apart: 26 -> 28, of which waited for: 12 -> 15; matrix products, arithmetic and copies ran while one was open for 3% -> 2% of each run, Pallas kernels for 0% -> 15%
where the time goes in v4:
time: 127 us; the launch traced here: 125 us
  waiting for transfers between devices  59.1 us (47%)
  starting transfers between devices  32.9 us (26%)
  Pallas kernels  22.6 us (18%)
  local copies, waits for them, and re-layouts  4.51 us (4%)
  other arithmetic  3.84 us (3%)
    ppermute x23, waiting for transfers between devices, tm_permute(): return lax.ppermute(x, 'tm', pairs)  48.9 us
    ppermute x23, starting transfers between devices, tm_permute(): return lax.ppermute(x, 'tm', pairs)  21.9 us
    pallas_call x1, Pallas kernels, attention(): pl.pallas_call(functools.partial(attention_kernel, shards, scale, blocks)...  16.9 us
    ppermute x4, starting transfers between devices, head_permute(): return lax.ppermute(x, 'head', pairs)  7.42 us
    all_to_all x1, waiting for transfers between devices, local(): lax.all_to_all(mixed, 'head', split_axis=0, concat_axis=0, tiled=True)  6.06 us
    ppermute x4, waiting for transfers between devices, head_permute(): return lax.ppermute(x, 'head', pairs)  4.18 us
    pallas_call x1, Pallas kernels, output_projection(): pl.pallas_call(output_kernel, out_shape=jax.ShapeDtypeStruct((rows, width...  3.7 us
    unnamed x48, local copies, waits for them, and re-layouts  3.64 us
  transfers between devices with their start and end apart: 28, of which 15 were waited for; matrix products, arithmetic and copies ran while one was open for 2% of the time, Pallas kernels for 15%

profile of v4, /device:TPU:16, one launch (start us, length us, event | category | flops | bytes accessed | tf_op | source)
XLA Modules:
  0.0 124.8 jit_solution(6055253976545146661)
XLA Ops:
  0.0 0.8 fusion.25
  0.8 5.9 %collective-permute-start = (bf16[128,128]{1,0:T(8,128)(2,1)S(1)}, bf16[128,128]{1,0:T(8,128)(2,1)S(1)}, u32[]{:S(2)}, u32[]{:S(2)}) collective-permute-start(bf16[128,128]{1,0:T(8,128)(2,1)S(1)} %get-tuple-element.30), channel_id=1, source_target_pairs={{16,0},{24,8},{32,16},{40,24},{48,32},{56,40},{64,48},{72,56},{80,... | collective-permute-start | bytes 98312 | tf_op jit(solution)/shard_map/ppermute | solution.py:25
  6.8 1.6 %collective-permute-done = bf16[128,128]{1,0:T(8,128)(2,1)S(1)} collective-permute-done((bf16[128,128]{1,0:T(8,128)(2,1)S(1)}, bf16[128,128]{1,0:T(8,128)(2,1)S(1)}, u32[]{:S(2)}, u32[]{:S(2)}) %collective-permute-start) | collective-permute-done | bytes 32800 | tf_op jit(solution)/shard_map/ppermute | solution.py:25
  8.4 2.4 %collective-permute-start.1 = (bf16[2,128,128]{2,1,0:T(8,128)(2,1)S(1)}, bf16[2,128,128]{2,1,0:T(8,128)(2,1)S(1)}, u32[]{:S(2)}, u32[]{:S(2)}) collective-permute-start(bf16[2,128,128]{2,1,0:T(8,128)(2,1)S(1)} %pad_maximum_fusion.5), channel_id=1, source_target_pairs={{80,0},{88,8},{96,16},{104,24},{112,32},{120,40},{0,48},{8,56},{16... | collective-permute-start | bytes 196616 | tf_op jit(solution)/shard_map/ppermute | solution.py:25
  10.7 1.8 %collective-permute-done.2 = bf16[128,128]{1,0:T(8,128)(2,1)S(1)} collective-permute-done((bf16[128,128]{1,0:T(8,128)(2,1)S(1)}, bf16[128,128]{1,0:T(8,128)(2,1)S(1)}, u32[]{:S(2)}, u32[]{:S(2)}) %collective-permute-start.2) | collective-permute-done | bytes 32800 | tf_op jit(solution)/shard_map/ppermute | solution.py:25
  12.5 1.0 collective-permute-start.3
  13.5 3.1 %collective-permute-done.1 = bf16[2,128,128]{2,1,0:T(8,128)(2,1)S(1)} collective-permute-done((bf16[2,128,128]{2,1,0:T(8,128)(2,1)S(1)}, bf16[2,128,128]{2,1,0:T(8,128)(2,1)S(1)}, u32[]{:S(2)}, u32[]{:S(2)}) %collective-permute-start.1) | collective-permute-done | bytes 65568 | tf_op jit(solution)/shard_map/ppermute | solution.py:25
  16.7 4.8 %collective-permute-done.3 = bf16[3,128,128]{2,1,0:T(8,128)(2,1)S(1)} collective-permute-done((bf16[3,128,128]{2,1,0:T(8,128)(2,1)S(1)}, bf16[3,128,128]{2,1,0:T(8,128)(2,1)S(1)}, u32[]{:S(2)}, u32[]{:S(2)}) %collective-permute-start.3) | collective-permute-done | bytes 98336 | tf_op jit(solution)/shard_map/ppermute | solution.py:25
  21.6 0.4 collective-permute-start.4
  22.0 7.5 %collective-permute-done.4 = bf16[8,128,128]{2,1,0:T(8,128)(2,1)S(1)} collective-permute-done((bf16[8,128,128]{2,1,0:T(8,128)(2,1)S(1)}, bf16[8,128,128]{2,1,0:T(8,128)(2,1)S(1)}, u32[]{:S(2)}, u32[]{:S(2)}) %collective-permute-start.4) | collective-permute-done | bytes 262176 | tf_op jit(solution)/shard_map/ppermute | solution.py:25
  29.6 0.1 pad_maximum_fusion.1
  29.7 0.1 collective-permute-start.5
  29.8 0.3 fusion
  30.1 1.6 %collective-permute-done.5 = bf16[2,8,128,128]{3,2,1,0:T(8,128)(2,1)S(1)} collective-permute-done((bf16[2,8,128,128]{3,2,1,0:T(8,128)(2,1)S(1)}, bf16[2,8,128,128]{3,2,1,0:T(8,128)(2,1)S(1)}, u32[]{:S(2)}, u32[]{:S(2)}) %collective-permute-start.5) | collective-permute-done | bytes 524320 | tf_op jit(solution)/shard_map/ppermute | solution.py:25
  31.7 0.1 select_bitcast_fusion.1
  31.7 0.1 pad_maximum_fusion
  31.9 0.1 slice_bitcast_fusion
  31.9 0.5 copy.11
  32.5 0.1 copy-done.23
  32.6 0.8 convolution_convert_fusion
  33.4 0.0 copy-start.12
  33.4 0.1 collective-permute-start.8
  33.6 8.3 %collective-permute-done.8.refs_6_ = bf16[512,256]{1,0:T(8,128)(2,1)S(1)} collective-permute-done((bf16[512,256]{1,0:T(8,128)(2,1)S(1)}, bf16[512,256]{1,0:T(8,128)(2,1)S(1)}, u32[]{:S(2)}, u32[]{:S(2)}) %collective-permute-start.8) | collective-permute-done | bytes 262176 | tf_op jit(solution)/shard_map/ppermute | solution.py:25
  41.9 1.3 %collective-permute-start.13 = (bf16[1024,128]{1,0:T(8,128)(2,1)S(1)}, bf16[1024,128]{1,0:T(8,128)(2,1)S(1)}, u32[]{:S(2)}, u32[]{:S(2)}) collective-permute-start(bf16[1024,128]{1,0:T(8,128)(2,1)S(1)} %bitcast.35), channel_id=1, source_target_pairs={{4,0},{5,1},{6,2},{7,3},{0,4},{1,5},{2,6},{3,7},{12,8},{13,9},{14,... | collective-permute-start | bytes 786440 | tf_op jit(solution)/shard_map/ppermute | solution.py:33
  43.2 1.5 %collective-permute-start.12 = (bf16[512,256]{1,0:T(8,128)(2,1)S(1)}, bf16[512,256]{1,0:T(8,128)(2,1)S(1)}, u32[]{:S(2)}, u32[]{:S(2)}) collective-permute-start(bf16[512,256]{1,0:T(8,128)(2,1)S(1)} %collective-permute-done.8.refs_6_), channel_id=1, source_target_pairs={{16,0},{24,8},{32,16},{40,24},{48,32},{56,40},{64,48},{72,56},{80,... | collective-permute-start | bytes 786440 | tf_op jit(solution)/shard_map/ppermute | solution.py:25
  44.6 0.5 collective-permute-start.10
  45.2 4.2 %collective-permute-done.13 = bf16[1024,128]{1,0:T(8,128)(2,1)S(1)} collective-permute-done((bf16[1024,128]{1,0:T(8,128)(2,1)S(1)}, bf16[1024,128]{1,0:T(8,128)(2,1)S(1)}, u32[]{:S(2)}, u32[]{:S(2)}) %collective-permute-start.13) | collective-permute-done | bytes 262176 | tf_op jit(solution)/shard_map/ppermute | solution.py:33
  49.4 0.1 pad_maximum_fusion.2.refs_0_
  49.4 0.9 collective-permute-done.12.refs_10_
  50.4 3.0 %collective-permute-start.17 = (bf16[512,256]{1,0:T(8,128)(2,1)S(1)}, bf16[512,256]{1,0:T(8,128)(2,1)S(1)}, u32[]{:S(2)}, u32[]{:S(2)}) collective-permute-start(bf16[512,256]{1,0:T(8,128)(2,1)S(1)} %collective-permute-done.12.refs_10_), channel_id=1, source_target_pairs={{16,0},{24,8},{32,16},{40,24},{48,32},{56,40},{64,48},{72,56},{80,... | collective-permute-start | bytes 786440 | tf_op jit(solution)/shard_map/ppermute | solution.py:25
  53.4 2.8 %collective-permute-start.22 = (bf16[2,1024,128]{2,1,0:T(8,128)(2,1)S(1)}, bf16[2,1024,128]{2,1,0:T(8,128)(2,1)S(1)}, u32[]{:S(2)}, u32[]{:S(2)}) collective-permute-start(bf16[2,1024,128]{2,1,0:T(8,128)(2,1)S(1)} %pad_maximum_fusion.2.refs_0_), channel_id=1, source_target_pairs={{1,0},{2,1},{3,2},{0,3},{5,4},{6,5},{7,6},{4,7},{9,8},{10,9},{11,1... | collective-permute-start | bytes 1572872 | tf_op jit(solution)/shard_map/ppermute | solution.py:33
  56.2 1.3 %collective-permute-done.17.refs_14_ = bf16[512,256]{1,0:T(8,128)(2,1)S(1)} collective-permute-done((bf16[512,256]{1,0:T(8,128)(2,1)S(1)}, bf16[512,256]{1,0:T(8,128)(2,1)S(1)}, u32[]{:S(2)}, u32[]{:S(2)}) %collective-permute-start.17) | collective-permute-done | bytes 262176 | tf_op jit(solution)/shard_map/ppermute | solution.py:25
  57.5 3.7 %collective-permute-start.21 = (bf16[512,256]{1,0:T(8,128)(2,1)S(1)}, bf16[512,256]{1,0:T(8,128)(2,1)}, u32[]{:S(2)}, u32[]{:S(2)}) collective-permute-start(bf16[512,256]{1,0:T(8,128)(2,1)S(1)} %collective-permute-done.17.refs_14_), channel_id=1, source_target_pairs={{16,0},{24,8},{32,16},{40,24},{48,32},{56,40},{64,48},{72,56},{80,... | collective-permute-start | bytes 786440 | tf_op jit(solution)/shard_map/ppermute | solution.py:25
  61.3 0.1 collective-permute-start.7
  61.4 0.5 collective-permute-start.9
  61.9 0.1 collective-permute-start.11
  62.0 3.1 %collective-permute-done.21.refs_18_ = bf16[512,256]{1,0:T(8,128)(2,1)} collective-permute-done((bf16[512,256]{1,0:T(8,128)(2,1)S(1)}, bf16[512,256]{1,0:T(8,128)(2,1)}, u32[]{:S(2)}, u32[]{:S(2)}) %collective-permute-start.21) | collective-permute-done | bytes 262176 | tf_op jit(solution)/shard_map/ppermute | solution.py:25
  65.1 0.1 broadcast_subtract_fusion
  65.2 0.1 sub.39
  65.9 0.8 collective-permute-start.6
  66.7 0.5 fusion.18
  67.2 5.3 %collective-permute-done.6 = bf16[512,128]{1,0:T(8,128)(2,1)S(1)} collective-permute-done((bf16[512,128]{1,0:T(8,128)(2,1)S(1)}, bf16[512,128]{1,0:T(8,128)(2,1)S(1)}, u32[]{:S(2)}, u32[]{:S(2)}) %collective-permute-start.6) | collective-permute-done | bytes 131104 | tf_op jit(solution)/shard_map/ppermute | solution.py:25
  72.5 0.5 collective-permute-start.16
  73.0 0.1 collective-permute-start.18
  73.1 0.2 collective-permute-done.19.refs_16_
  73.3 0.2 collective-permute-start.20
  73.5 0.3 collective-permute-start.23
  73.9 0.6 compare_select_fusion.12.refs_0_
  74.4 0.7 pad_maximum_fusion.3.refs_3_
  75.2 1.5 %collective-permute-start.25 = (bf16[2,1024,128]{2,1,0:T(8,128)(2,1)S(1)}, bf16[2,1024,128]{2,1,0:T(8,128)(2,1)S(1)}, u32[]{:S(2)}, u32[]{:S(2)}) collective-permute-start(bf16[2,1024,128]{2,1,0:T(8,128)(2,1)S(1)} %pad_maximum_fusion.2.refs_0_), channel_id=1, source_target_pairs={{3,0},{0,1},{1,2},{2,3},{7,4},{4,5},{5,6},{6,7},{11,8},{8,9},{9,10... | collective-permute-start | bytes 1572872 | tf_op jit(solution)/shard_map/ppermute | solution.py:33
  76.7 1.8 %collective-permute-start.26 = (bf16[2,1024,128]{2,1,0:T(8,128)(2,1)S(1)}, bf16[2,1024,128]{2,1,0:T(8,128)(2,1)S(1)}, u32[]{:S(2)}, u32[]{:S(2)}) collective-permute-start(bf16[2,1024,128]{2,1,0:T(8,128)(2,1)S(1)} %collective-permute-done.22.refs_1_), channel_id=1, source_target_pairs={{1,0},{2,1},{3,2},{0,3},{5,4},{6,5},{7,6},{4,7},{9,8},{10,9},{11,1... | collective-permute-start | bytes 1572872 | tf_op jit(solution)/shard_map/ppermute | solution.py:33
  78.5 0.7 copy-done.20
  79.2 0.7 copy-done.21
  79.9 0.7 copy-done.22
  80.6 16.9 %shard_map.91 = (bf16[512,256]{1,0:T(8,128)(2,1)}, f32[512,128]{1,0:T(8,128)}, f32[512,128]{1,0:T(8,128)}) custom-call(f32[32]{0:T(128)} %compare_select_fusion.12.refs_0_, f32[32]{0:T(128)} %get-tuple-element.23.refs_1_, f32[1]{0:T(128)} %mul.57.refs_2_, bf16[1024,128]{1,0:T(8,128)(2,1)} %pad_maximum_fusion.3.refs_3_, bf16[512,256]{1,0:T(8,128)(2,1)} %copy-done.7, ...), custom_call_target="tpu_custom_call" | custom-call | flops 8589934592 | bytes 5242880 | tf_op jit(solution)/shard_map/pallas_call | solution.py:118
  97.5 0.8 collective-permute-start.24
  98.3 9.3 %collective-permute-done.24.got_ref = bf16[512,256]{1,0:T(8,128)(2,1)S(1)} collective-permute-done((bf16[512,256]{1,0:T(8,128)(2,1)}, bf16[512,256]{1,0:T(8,128)(2,1)S(1)}, u32[]{:S(2)}, u32[]{:S(2)}) %collective-permute-start.24) | collective-permute-done | bytes 262176 | tf_op jit(solution)/shard_map/ppermute | solution.py:25
  107.6 0.7 copy-done.6
  108.3 2.1 %shard_map.92 = bf16[512,128]{1,0:T(8,128)(2,1)} custom-call(f32[512,128]{1,0:T(8,128)} %get-tuple-element.19.out_ref, f32[512,128]{1,0:T(8,128)} %get-tuple-element.20.lse_ref, bf16[512,256]{1,0:T(8,128)(2,1)} %copy-done.6), custom_call_target="tpu_custom_call" | custom-call | tf_op jit(solution)/shard_map/pallas_call | solution.py:157
  110.3 3.5 %all-to-all-start = ((bf16[8,64,128]{2,1,0:T(8,128)(2,1)}), bf16[8,64,128]{2,1,0:T(8,128)(2,1)S(1)}, u32[]{:S(2)}, u32[]{:S(2)}) async-start(bf16[8,64,128]{2,1,0:T(8,128)(2,1)} %bitcast.37), calls=%async_computation | async-start | bytes 262144 | tf_op jit(solution)/shard_map/all_to_all | solution.py:259
  113.8 0.5 fusion.8.head_ref
  114.4 6.1 %all-to-all-done.mixed_ref = bf16[8,64,128]{2,1,0:T(8,128)(2,1)S(1)} async-done(((bf16[8,64,128]{2,1,0:T(8,128)(2,1)}), bf16[8,64,128]{2,1,0:T(8,128)(2,1)S(1)}, u32[]{:S(2)}, u32[]{:S(2)}) %all-to-all-start) | async-done | bytes 131104 | tf_op jit(solution)/shard_map/all_to_all | solution.py:259
  120.4 0.7 copy-done.5
  121.1 3.7 %shard_map.93 = bf16[64,1024]{1,0:T(8,128)(2,1)} custom-call(s32[8]{0:T(128)} %fusion.8.head_ref, bf16[8,64,128]{2,1,0:T(8,128)(2,1)} %copy-done.5, bf16[2,1024,128]{2,1,0:T(8,128)(2,1)} %copy-done, bf16[2,1024,128]{2,1,0:T(8,128)(2,1)} %copy-done.2, bf16[2,1024,128]{2,1,0:T(8,128)(2,1)} %copy-done.3, bf16[2,1024,128]{2,1,0:T(8,128)(2,1)} %copy-done.4), custom_call_target="tpu_custom_call" | custom-call | tf_op jit(solution)/shard_map/pallas_call | solution.py:177
  (76 shorter events, 0.4 us)
Async XLA Ops:
  0.0 16.7 %copy-start.8 = (bf16[3,32,128]{2,1,0:T(8,128)(2,1)S(1)}, bf16[3,32,128]{2,1,0:T(8,128)(2,1)}, u32[]{:S(2)}) copy-start(bf16[3,32,128]{2,1,0:T(8,128)(2,1)} %param.11) | copy-start | bytes 73732
  0.0 16.7 %copy-start.9 = (bf16[128,32]{0,1:T(8,128)(2,1)S(1)}, bf16[128,32]{0,1:T(8,128)(2,1)}, u32[]{:S(2)}) copy-start(bf16[128,32]{0,1:T(8,128)(2,1)} %param.13) | copy-start | bytes 24580
  0.8 7.5 %collective-permute-start = (bf16[128,128]{1,0:T(8,128)(2,1)S(1)}, bf16[128,128]{1,0:T(8,128)(2,1)S(1)}, u32[]{:S(2)}, u32[]{:S(2)}) collective-permute-start(bf16[128,128]{1,0:T(8,128)(2,1)S(1)} %get-tuple-element.30), channel_id=1, source_target_pairs={{16,0},{24,8},{32,16},{40,24},{48,32},{56,40},{64,48},{72,56},{80,... | collective-permute-start | bytes 98312 | tf_op jit(solution)/shard_map/ppermute | solution.py:25
  6.8 5.7 %collective-permute-start.2 = (bf16[128,128]{1,0:T(8,128)(2,1)S(1)}, bf16[128,128]{1,0:T(8,128)(2,1)S(1)}, u32[]{:S(2)}, u32[]{:S(2)}) collective-permute-start(bf16[128,128]{1,0:T(8,128)(2,1)S(1)} %get-tuple-element.30), channel_id=1, source_target_pairs={{112,0},{120,8},{0,16},{8,24},{16,32},{24,40},{32,48},{40,56},{48,... | collective-permute-start | bytes 98312 | tf_op jit(solution)/shard_map/ppermute | solution.py:25
  8.4 8.2 %collective-permute-start.1 = (bf16[2,128,128]{2,1,0:T(8,128)(2,1)S(1)}, bf16[2,128,128]{2,1,0:T(8,128)(2,1)S(1)}, u32[]{:S(2)}, u32[]{:S(2)}) collective-permute-start(bf16[2,128,128]{2,1,0:T(8,128)(2,1)S(1)} %pad_maximum_fusion.5), channel_id=1, source_target_pairs={{80,0},{88,8},{96,16},{104,24},{112,32},{120,40},{0,48},{8,56},{16... | collective-permute-start | bytes 196616 | tf_op jit(solution)/shard_map/ppermute | solution.py:25
  12.5 9.1 %collective-permute-start.3 = (bf16[3,128,128]{2,1,0:T(8,128)(2,1)S(1)}, bf16[3,128,128]{2,1,0:T(8,128)(2,1)S(1)}, u32[]{:S(2)}, u32[]{:S(2)}) collective-permute-start(bf16[3,128,128]{2,1,0:T(8,128)(2,1)S(1)} %pad_maximum_fusion.4), channel_id=1, source_target_pairs={{48,0},{56,8},{64,16},{72,24},{80,32},{88,40},{96,48},{104,56},{11... | collective-permute-start | bytes 294920 | tf_op jit(solution)/shard_map/ppermute | solution.py:25
  21.6 8.0 %collective-permute-start.4 = (bf16[8,128,128]{2,1,0:T(8,128)(2,1)S(1)}, bf16[8,128,128]{2,1,0:T(8,128)(2,1)S(1)}, u32[]{:S(2)}, u32[]{:S(2)}) collective-permute-start(bf16[8,128,128]{2,1,0:T(8,128)(2,1)S(1)} %slice_dynamic-update-slice_fusion), channel_id=1, source_target_pairs={{128,0},{136,8},{144,16},{152,24},{160,32},{168,40},{176,48},{184,... | collective-permute-start | bytes 786440 | tf_op jit(solution)/shard_map/ppermute | solution.py:25
  22.0 7.8 %copy-start.1 = (bf16[512,1024]{1,0:T(8,128)(2,1)S(1)}, bf16[512,1024]{1,0:T(8,128)(2,1)}, u32[]{:S(2)}) copy-start(bf16[512,1024]{1,0:T(8,128)(2,1)} %param.9) | copy-start | bytes 3145732
  29.7 2.0 %collective-permute-start.5 = (bf16[2,8,128,128]{3,2,1,0:T(8,128)(2,1)S(1)}, bf16[2,8,128,128]{3,2,1,0:T(8,128)(2,1)S(1)}, u32[]{:S(2)}, u32[]{:S(2)}) collective-permute-start(bf16[2,8,128,128]{3,2,1,0:T(8,128)(2,1)S(1)} %pad_maximum_fusion.1), channel_id=1, source_target_pairs={{8,0},{0,8},{24,16},{16,24},{40,32},{32,40},{56,48},{48,56},{72,64... | collective-permute-start | bytes 1572872 | tf_op jit(solution)/shard_map/ppermute | solution.py:25
  31.9 0.7 copy-start.23
  33.4 27.8 %copy-start.12 = (s32[16]{0:T(128)S(1)}, s32[16]{0:T(128)}, u32[]{:S(2)}) copy-start(s32[16]{0:T(128)} %constant.183.clone) | copy-start | bytes 196
  33.4 27.8 %copy-start.13 = (s32[16]{0:T(128)S(1)}, s32[16]{0:T(128)}, u32[]{:S(2)}) copy-start(s32[16]{0:T(128)} %constant.184.clone) | copy-start | bytes 196
  33.4 41.7 %copy-start.7 = (bf16[512,256]{1,0:T(8,128)(2,1)}, bf16[512,256]{1,0:T(8,128)(2,1)S(1)}, u32[]{:S(2)}) copy-start(bf16[512,256]{1,0:T(8,128)(2,1)S(1)} %slice.45.refs_4_) | copy-start | bytes 786436
  33.4 8.4 %collective-permute-start.8 = (bf16[512,256]{1,0:T(8,128)(2,1)S(1)}, bf16[512,256]{1,0:T(8,128)(2,1)S(1)}, u32[]{:S(2)}, u32[]{:S(2)}) collective-permute-start(bf16[512,256]{1,0:T(8,128)(2,1)S(1)} %slice.45.refs_4_), channel_id=1, source_target_pairs={{16,0},{24,8},{32,16},{40,24},{48,32},{56,40},{64,48},{72,56},{80,... | collective-permute-start | bytes 786440 | tf_op jit(solution)/shard_map/ppermute | solution.py:25
  41.9 38.7 %copy-start.14 = (bf16[512,256]{1,0:T(8,128)(2,1)}, bf16[512,256]{1,0:T(8,128)(2,1)S(1)}, u32[]{:S(2)}) copy-start(bf16[512,256]{1,0:T(8,128)(2,1)S(1)} %collective-permute-done.8.refs_6_) | copy-start | bytes 786436
  41.9 7.5 %collective-permute-start.13 = (bf16[1024,128]{1,0:T(8,128)(2,1)S(1)}, bf16[1024,128]{1,0:T(8,128)(2,1)S(1)}, u32[]{:S(2)}, u32[]{:S(2)}) collective-permute-start(bf16[1024,128]{1,0:T(8,128)(2,1)S(1)} %bitcast.35), channel_id=1, source_target_pairs={{4,0},{5,1},{6,2},{7,3},{0,4},{1,5},{2,6},{3,7},{12,8},{13,9},{14,... | collective-permute-start | bytes 786440 | tf_op jit(solution)/shard_map/ppermute | solution.py:33
  43.2 7.2 %collective-permute-start.12 = (bf16[512,256]{1,0:T(8,128)(2,1)S(1)}, bf16[512,256]{1,0:T(8,128)(2,1)S(1)}, u32[]{:S(2)}, u32[]{:S(2)}) collective-permute-start(bf16[512,256]{1,0:T(8,128)(2,1)S(1)} %collective-permute-done.8.refs_6_), channel_id=1, source_target_pairs={{16,0},{24,8},{32,16},{40,24},{48,32},{56,40},{64,48},{72,56},{80,... | collective-permute-start | bytes 786440 | tf_op jit(solution)/shard_map/ppermute | solution.py:25
  44.6 8.7 %collective-permute-start.10 = (bf16[512,256]{1,0:T(8,128)(2,1)S(1)}, bf16[512,256]{1,0:T(8,128)(2,1)S(1)}, u32[]{:S(2)}, u32[]{:S(2)}) collective-permute-start(bf16[512,256]{1,0:T(8,128)(2,1)S(1)} %slice.45.refs_4_), channel_id=1, source_target_pairs={{112,0},{120,8},{0,16},{8,24},{16,32},{24,40},{32,48},{40,56},{48,... | collective-permute-start | bytes 786440 | tf_op jit(solution)/shard_map/ppermute | solution.py:25
  49.4 48.1 %copy-start = (bf16[2,1024,128]{2,1,0:T(8,128)(2,1)}, bf16[2,1024,128]{2,1,0:T(8,128)(2,1)S(1)}, u32[]{:S(2)}) copy-start(bf16[2,1024,128]{2,1,0:T(8,128)(2,1)S(1)} %pad_maximum_fusion.2.refs_0_) | copy-start | bytes 1572868
  50.4 30.2 %copy-start.15 = (bf16[512,256]{1,0:T(8,128)(2,1)}, bf16[512,256]{1,0:T(8,128)(2,1)S(1)}, u32[]{:S(2)}) copy-start(bf16[512,256]{1,0:T(8,128)(2,1)S(1)} %collective-permute-done.12.refs_10_) | copy-start | bytes 786436
  50.4 7.1 %collective-permute-start.17 = (bf16[512,256]{1,0:T(8,128)(2,1)S(1)}, bf16[512,256]{1,0:T(8,128)(2,1)S(1)}, u32[]{:S(2)}, u32[]{:S(2)}) collective-permute-start(bf16[512,256]{1,0:T(8,128)(2,1)S(1)} %collective-permute-done.12.refs_10_), channel_id=1, source_target_pairs={{16,0},{24,8},{32,16},{40,24},{48,32},{56,40},{64,48},{72,56},{80,... | collective-permute-start | bytes 786440 | tf_op jit(solution)/shard_map/ppermute | solution.py:25
  53.4 27.2 %copy-start.16 = (bf16[512,256]{1,0:T(8,128)(2,1)}, bf16[512,256]{1,0:T(8,128)(2,1)S(1)}, u32[]{:S(2)}) copy-start(bf16[512,256]{1,0:T(8,128)(2,1)S(1)} %collective-permute-done.10.refs_8_) | copy-start | bytes 786436
  53.4 8.5 %collective-permute-start.15 = (bf16[512,256]{1,0:T(8,128)(2,1)S(1)}, bf16[512,256]{1,0:T(8,128)(2,1)S(1)}, u32[]{:S(2)}, u32[]{:S(2)}) collective-permute-start(bf16[512,256]{1,0:T(8,128)(2,1)S(1)} %collective-permute-done.10.refs_8_), channel_id=1, source_target_pairs={{112,0},{120,8},{0,16},{8,24},{16,32},{24,40},{32,48},{40,56},{48,... | collective-permute-start | bytes 786440 | tf_op jit(solution)/shard_map/ppermute | solution.py:25
  53.4 12.6 %collective-permute-start.22 = (bf16[2,1024,128]{2,1,0:T(8,128)(2,1)S(1)}, bf16[2,1024,128]{2,1,0:T(8,128)(2,1)S(1)}, u32[]{:S(2)}, u32[]{:S(2)}) collective-permute-start(bf16[2,1024,128]{2,1,0:T(8,128)(2,1)S(1)} %pad_maximum_fusion.2.refs_0_), channel_id=1, source_target_pairs={{1,0},{2,1},{3,2},{0,3},{5,4},{6,5},{7,6},{4,7},{9,8},{10,9},{11,1... | collective-permute-start | bytes 1572872 | tf_op jit(solution)/shard_map/ppermute | solution.py:33
  57.5 23.1 %copy-start.17 = (bf16[512,256]{1,0:T(8,128)(2,1)}, bf16[512,256]{1,0:T(8,128)(2,1)S(1)}, u32[]{:S(2)}) copy-start(bf16[512,256]{1,0:T(8,128)(2,1)S(1)} %collective-permute-done.17.refs_14_) | copy-start | bytes 786436
  57.5 7.6 %collective-permute-start.21 = (bf16[512,256]{1,0:T(8,128)(2,1)S(1)}, bf16[512,256]{1,0:T(8,128)(2,1)}, u32[]{:S(2)}, u32[]{:S(2)}) collective-permute-start(bf16[512,256]{1,0:T(8,128)(2,1)S(1)} %collective-permute-done.17.refs_14_), channel_id=1, source_target_pairs={{16,0},{24,8},{32,16},{40,24},{48,32},{56,40},{64,48},{72,56},{80,... | collective-permute-start | bytes 786440 | tf_op jit(solution)/shard_map/ppermute | solution.py:25
  61.3 11.3 %collective-permute-start.7 = (bf16[512,256]{1,0:T(8,128)(2,1)S(1)}, bf16[512,256]{1,0:T(8,128)(2,1)}, u32[]{:S(2)}, u32[]{:S(2)}) collective-permute-start(bf16[512,256]{1,0:T(8,128)(2,1)S(1)} %slice.45.refs_4_), channel_id=1, source_target_pairs={{8,0},{0,8},{24,16},{16,24},{40,32},{32,40},{56,48},{48,56},{72,64... | collective-permute-start | bytes 786440 | tf_op jit(solution)/shard_map/ppermute | solution.py:25
  61.4 11.7 %collective-permute-start.9 = (bf16[512,256]{1,0:T(8,128)(2,1)S(1)}, bf16[512,256]{1,0:T(8,128)(2,1)}, u32[]{:S(2)}, u32[]{:S(2)}) collective-permute-start(bf16[512,256]{1,0:T(8,128)(2,1)S(1)} %collective-permute-done.8.refs_6_), channel_id=1, source_target_pairs={{8,0},{0,8},{24,16},{16,24},{40,32},{32,40},{56,48},{48,56},{72,64... | collective-permute-start | bytes 786440 | tf_op jit(solution)/shard_map/ppermute | solution.py:25
  61.9 14.8 %copy-start.18 = (bf16[512,256]{1,0:T(8,128)(2,1)}, bf16[512,256]{1,0:T(8,128)(2,1)S(1)}, u32[]{:S(2)}) copy-start(bf16[512,256]{1,0:T(8,128)(2,1)S(1)} %collective-permute-done.15.refs_12_) | copy-start | bytes 786436
  61.9 11.7 %collective-permute-start.11 = (bf16[512,256]{1,0:T(8,128)(2,1)S(1)}, bf16[512,256]{1,0:T(8,128)(2,1)}, u32[]{:S(2)}, u32[]{:S(2)}) collective-permute-start(bf16[512,256]{1,0:T(8,128)(2,1)S(1)} %collective-permute-done.10.refs_8_), channel_id=1, source_target_pairs={{8,0},{0,8},{24,16},{16,24},{40,32},{32,40},{56,48},{48,56},{72,64... | collective-permute-start | bytes 786440 | tf_op jit(solution)/shard_map/ppermute | solution.py:25
  65.1 8.3 %collective-permute-start.19 = (bf16[512,256]{1,0:T(8,128)(2,1)S(1)}, bf16[512,256]{1,0:T(8,128)(2,1)}, u32[]{:S(2)}, u32[]{:S(2)}) collective-permute-start(bf16[512,256]{1,0:T(8,128)(2,1)S(1)} %collective-permute-done.15.refs_12_), channel_id=1, source_target_pairs={{112,0},{120,8},{0,16},{8,24},{16,32},{24,40},{32,48},{40,56},{48,... | collective-permute-start | bytes 786440 | tf_op jit(solution)/shard_map/ppermute | solution.py:25
  65.9 31.6 %copy-start.2 = (bf16[2,1024,128]{2,1,0:T(8,128)(2,1)}, bf16[2,1024,128]{2,1,0:T(8,128)(2,1)S(1)}, u32[]{:S(2)}) copy-start(bf16[2,1024,128]{2,1,0:T(8,128)(2,1)S(1)} %collective-permute-done.22.refs_1_) | copy-start | bytes 1572868
  65.9 6.6 %collective-permute-start.6 = (bf16[512,128]{1,0:T(8,128)(2,1)S(1)}, bf16[512,128]{1,0:T(8,128)(2,1)S(1)}, u32[]{:S(2)}, u32[]{:S(2)}) collective-permute-start(bf16[512,128]{1,0:T(8,128)(2,1)S(1)} %slice.44), channel_id=1, source_target_pairs={{128,0},{136,8},{144,16},{152,24},{160,32},{168,40},{176,48},{184,... | collective-permute-start | bytes 393224 | tf_op jit(solution)/shard_map/ppermute | solution.py:25
  72.5 2.6 %collective-permute-start.14 = (bf16[512,256]{1,0:T(8,128)(2,1)S(1)}, bf16[512,256]{1,0:T(8,128)(2,1)}, u32[]{:S(2)}, u32[]{:S(2)}) collective-permute-start(bf16[512,256]{1,0:T(8,128)(2,1)S(1)} %collective-permute-done.12.refs_10_), channel_id=1, source_target_pairs={{8,0},{0,8},{24,16},{16,24},{40,32},{32,40},{56,48},{48,56},{72,64... | collective-permute-start | bytes 786440 | tf_op jit(solution)/shard_map/ppermute | solution.py:25
  72.5 4.2 %collective-permute-start.16 = (bf16[512,256]{1,0:T(8,128)(2,1)S(1)}, bf16[512,256]{1,0:T(8,128)(2,1)S(1)}, u32[]{:S(2)}, u32[]{:S(2)}) collective-permute-start(bf16[512,256]{1,0:T(8,128)(2,1)S(1)} %collective-permute-done.15.refs_12_), channel_id=1, source_target_pairs={{8,0},{0,8},{24,16},{16,24},{40,32},{32,40},{56,48},{48,56},{72,64... | collective-permute-start | bytes 786440 | tf_op jit(solution)/shard_map/ppermute | solution.py:25
  73.0 5.5 %collective-permute-start.18 = (bf16[512,256]{1,0:T(8,128)(2,1)S(1)}, bf16[512,256]{1,0:T(8,128)(2,1)S(1)}, u32[]{:S(2)}, u32[]{:S(2)}) collective-permute-start(bf16[512,256]{1,0:T(8,128)(2,1)S(1)} %collective-permute-done.17.refs_14_), channel_id=1, source_target_pairs={{8,0},{0,8},{24,16},{16,24},{40,32},{32,40},{56,48},{48,56},{72,64... | collective-permute-start | bytes 786440 | tf_op jit(solution)/shard_map/ppermute | solution.py:25
  73.3 5.1 %collective-permute-start.20 = (bf16[512,256]{1,0:T(8,128)(2,1)}, bf16[512,256]{1,0:T(8,128)(2,1)S(1)}, u32[]{:S(2)}, u32[]{:S(2)}) collective-permute-start(bf16[512,256]{1,0:T(8,128)(2,1)} %collective-permute-done.19.refs_16_), channel_id=1, source_target_pairs={{8,0},{0,8},{24,16},{16,24},{40,32},{32,40},{56,48},{48,56},{72,64... | collective-permute-start | bytes 786440 | tf_op jit(solution)/shard_map/ppermute | solution.py:25
  73.5 5.6 %collective-permute-start.23 = (bf16[512,256]{1,0:T(8,128)(2,1)}, bf16[512,256]{1,0:T(8,128)(2,1)S(1)}, u32[]{:S(2)}, u32[]{:S(2)}) collective-permute-start(bf16[512,256]{1,0:T(8,128)(2,1)} %collective-permute-done.21.refs_18_), channel_id=1, source_target_pairs={{8,0},{0,8},{24,16},{16,24},{40,32},{32,40},{56,48},{48,56},{72,64... | collective-permute-start | bytes 786440 | tf_op jit(solution)/shard_map/ppermute | solution.py:25
  75.2 39.2 %collective-permute-start.25 = (bf16[2,1024,128]{2,1,0:T(8,128)(2,1)S(1)}, bf16[2,1024,128]{2,1,0:T(8,128)(2,1)S(1)}, u32[]{:S(2)}, u32[]{:S(2)}) collective-permute-start(bf16[2,1024,128]{2,1,0:T(8,128)(2,1)S(1)} %pad_maximum_fusion.2.refs_0_), channel_id=1, source_target_pairs={{3,0},{0,1},{1,2},{2,3},{7,4},{4,5},{5,6},{6,7},{11,8},{8,9},{9,10... | collective-permute-start | bytes 1572872 | tf_op jit(solution)/shard_map/ppermute | solution.py:33
  76.7 1.8 %copy-start.19 = (bf16[512,256]{1,0:T(8,128)(2,1)}, bf16[512,256]{1,0:T(8,128)(2,1)S(1)}, u32[]{:S(2)}) copy-start(bf16[512,256]{1,0:T(8,128)(2,1)S(1)} %collective-permute-done.16.refs_13_) | copy-start | bytes 786436
  76.7 37.6 %collective-permute-start.26 = (bf16[2,1024,128]{2,1,0:T(8,128)(2,1)S(1)}, bf16[2,1024,128]{2,1,0:T(8,128)(2,1)S(1)}, u32[]{:S(2)}, u32[]{:S(2)}) collective-permute-start(bf16[2,1024,128]{2,1,0:T(8,128)(2,1)S(1)} %collective-permute-done.22.refs_1_), channel_id=1, source_target_pairs={{1,0},{2,1},{3,2},{0,3},{5,4},{6,5},{7,6},{4,7},{9,8},{10,9},{11,1... | collective-permute-start | bytes 1572872 | tf_op jit(solution)/shard_map/ppermute | solution.py:33
  78.5 0.7 copy-start.20
  79.2 0.7 copy-start.21
  79.9 0.7 copy-start.22
  97.5 16.3 %copy-start.10 = (s32[8]{0:T(128)S(1)}, s32[8]{0:T(128)}, u32[]{:S(2)}) copy-start(s32[8]{0:T(128)} %constant.185.clone) | copy-start | bytes 100
  97.5 16.3 %copy-start.11 = (s32[8]{0:T(128)S(1)}, s32[8]{0:T(128)}, u32[]{:S(2)}) copy-start(s32[8]{0:T(128)} %constant.186.clone) | copy-start | bytes 100
  97.5 10.1 %collective-permute-start.24 = (bf16[512,256]{1,0:T(8,128)(2,1)}, bf16[512,256]{1,0:T(8,128)(2,1)S(1)}, u32[]{:S(2)}, u32[]{:S(2)}) collective-permute-start(bf16[512,256]{1,0:T(8,128)(2,1)} %get-tuple-element.21), channel_id=1, source_target_pairs={{128,0},{136,8},{144,16},{152,24},{160,32},{168,40},{176,48},{184,... | collective-permute-start | bytes 786440 | tf_op jit(solution)/shard_map/ppermute | solution.py:25
  107.6 0.7 copy-start.6
  110.3 10.1 %all-to-all-start = ((bf16[8,64,128]{2,1,0:T(8,128)(2,1)}), bf16[8,64,128]{2,1,0:T(8,128)(2,1)S(1)}, u32[]{:S(2)}, u32[]{:S(2)}) async-start(bf16[8,64,128]{2,1,0:T(8,128)(2,1)} %bitcast.37), calls=%async_computation | async-start | bytes 262144 | tf_op jit(solution)/shard_map/all_to_all | solution.py:259
  114.3 6.1 %copy-start.3 = (bf16[2,1024,128]{2,1,0:T(8,128)(2,1)}, bf16[2,1024,128]{2,1,0:T(8,128)(2,1)S(1)}, u32[]{:S(2)}) copy-start(bf16[2,1024,128]{2,1,0:T(8,128)(2,1)S(1)} %collective-permute-done.25.refs_2_) | copy-start | bytes 1572868
  114.3 6.1 %copy-start.4 = (bf16[2,1024,128]{2,1,0:T(8,128)(2,1)}, bf16[2,1024,128]{2,1,0:T(8,128)(2,1)S(1)}, u32[]{:S(2)}) copy-start(bf16[2,1024,128]{2,1,0:T(8,128)(2,1)S(1)} %collective-permute-done.26.refs_3_) | copy-start | bytes 1572868
  120.4 0.7 copy-start.5

commit v5 on v4

--- a/solution.py
+++ b/solution.py
@@ -234,24 +234,30 @@
     up = tm_permute(kv, 0, 1, 0)
     down = tm_permute(kv, 0, -1, 0)
     kvs = [kv, tm_permute(kv, 0, 0, 1)]
-    queries = jnp.concatenate([query, tm_permute(query, 1, 0, 0)], axis=0)
+    far_query = tm_permute(query, 1, 0, 0)
     for step in range(1, Z // 2 + 1):
         if step == 1:
-            up, w_out_t = lax.optimization_barrier((up, w_out_t))
-            weights = [jnp.stack([w_out_t, head_permute(w_out_t, 1, 0)])]
+            up, down, far_query, w_out_t = lax.optimization_barrier((up, down, far_query, w_out_t))
         elif step == 2:
-            up, weights[0] = lax.optimization_barrier((up, weights[0]))
-            weights += [head_permute(weights[0], 0, 1), head_permute(weights[0], 0, -1)]
-        elif step == 4:
-            up, weights[1] = lax.optimization_barrier((up, weights[1]))
-            weights.append(head_permute(weights[1], 0, 1))
+            up, down, pair = lax.optimization_barrier((up, down, pair))
+        elif step == 3:
+            up, down = lax.optimization_barrier((up, down))
+        else:
+            up, east = lax.optimization_barrier((up, east))
         got = [up] if step == Z // 2 else [up, down]
         if step < Z // 2:
             up = tm_permute(up, 0, 1, 0)
         if step < Z // 2 - 1:
             down = tm_permute(down, 0, -1, 0)
+        if step == 1:
+            pair = jnp.stack([w_out_t, head_permute(w_out_t, 1, 0)])
+        elif step == 2:
+            east, west = head_permute(pair, 0, 1), head_permute(pair, 0, -1)
+        elif step == Z // 2:
+            weights = [pair, east, west, head_permute(east, 0, 1)]
         for piece in got:
             kvs += [piece, tm_permute(piece, 0, 0, 1)]
+    queries = jnp.concatenate([query, far_query], axis=0)
 
     send, keep, keep_lse = attention(signs, bases, slope, queries, kvs, 128 ** (-0.5) * LOG2E)
     got = tm_permute(send, 1, 0, 0)

time: 127 us -> 121 us (0.953); the launches traced: 125 us -> 121 us
  starting transfers between devices: 32.9 us -> 29.9 us
    ppermute x23, starting transfers between devices: 21.9 us -> 18.9 us  [tm_permute(): return lax.ppermute(x, 'tm', pairs)]
    unnamed x48 -> x52, local copies, waits for them, and re-layouts: 3.64 us -> 3.69 us
  transfers between devices with their start and end apart: 28 -> 28, of which waited for: 15 -> 16; matrix products, arithmetic and copies ran while one was open for 2% -> 3% of each run, Pallas kernels for 15% -> 16%
where the time goes in v5:
time: 121 us
  waiting for transfers between devices  58.3 us (48%)
  starting transfers between devices  29.9 us (25%)
  Pallas kernels  22.6 us (19%)
  local copies, waits for them, and re-layouts  4.56 us (4%)
  other arithmetic  3.96 us (3%)
    ppermute x23, waiting for transfers between devices, tm_permute(): return lax.ppermute(x, 'tm', pairs)  48.2 us
    ppermute x23, starting transfers between devices, tm_permute(): return lax.ppermute(x, 'tm', pairs)  18.9 us
    pallas_call x1, Pallas kernels, attention(): pl.pallas_call(functools.partial(attention_kernel, shards, scale, blocks)...  16.9 us
    ppermute x4, starting transfers between devices, head_permute(): return lax.ppermute(x, 'head', pairs)  7.57 us
    all_to_all x1, waiting for transfers between devices, local(): lax.all_to_all(mixed, 'head', split_axis=0, concat_axis=0, tiled=True)  5.87 us
    ppermute x4, waiting for transfers between devices, head_permute(): return lax.ppermute(x, 'head', pairs)  4.18 us
    pallas_call x1, Pallas kernels, output_projection(): pl.pallas_call(output_kernel, out_shape=jax.ShapeDtypeStruct((rows, width...  3.7 us
    unnamed x52, local copies, waits for them, and re-layouts  3.69 us
  transfers between devices with their start and end apart: 28, of which 16 were waited for; matrix products, arithmetic and copies ran while one was open for 3% of the time, Pallas kernels for 16%

profile of v5, /device:TPU:16, one launch (start us, length us, event | category | flops | bytes accessed | tf_op | source)
XLA Modules:
  0.0 121.1 jit_solution(17487163927663391965)
XLA Ops:
  0.0 0.8 fusion.25
  0.8 5.9 %collective-permute-start = (bf16[128,128]{1,0:T(8,128)(2,1)S(1)}, bf16[128,128]{1,0:T(8,128)(2,1)S(1)}, u32[]{:S(2)}, u32[]{:S(2)}) collective-permute-start(bf16[128,128]{1,0:T(8,128)(2,1)S(1)} %get-tuple-element.40), channel_id=1, source_target_pairs={{16,0},{24,8},{32,16},{40,24},{48,32},{56,40},{64,48},{72,56},{80,... | collective-permute-start | bytes 98312 | tf_op jit(solution)/shard_map/ppermute | solution.py:25
  6.8 1.6 %collective-permute-done = bf16[128,128]{1,0:T(8,128)(2,1)S(1)} collective-permute-done((bf16[128,128]{1,0:T(8,128)(2,1)S(1)}, bf16[128,128]{1,0:T(8,128)(2,1)S(1)}, u32[]{:S(2)}, u32[]{:S(2)}) %collective-permute-start) | collective-permute-done | bytes 32800 | tf_op jit(solution)/shard_map/ppermute | solution.py:25
  8.4 2.4 %collective-permute-start.1 = (bf16[2,128,128]{2,1,0:T(8,128)(2,1)S(1)}, bf16[2,128,128]{2,1,0:T(8,128)(2,1)S(1)}, u32[]{:S(2)}, u32[]{:S(2)}) collective-permute-start(bf16[2,128,128]{2,1,0:T(8,128)(2,1)S(1)} %pad_maximum_fusion.5), channel_id=1, source_target_pairs={{80,0},{88,8},{96,16},{104,24},{112,32},{120,40},{0,48},{8,56},{16... | collective-permute-start | bytes 196616 | tf_op jit(solution)/shard_map/ppermute | solution.py:25
  10.7 1.8 %collective-permute-done.2 = bf16[128,128]{1,0:T(8,128)(2,1)S(1)} collective-permute-done((bf16[128,128]{1,0:T(8,128)(2,1)S(1)}, bf16[128,128]{1,0:T(8,128)(2,1)S(1)}, u32[]{:S(2)}, u32[]{:S(2)}) %collective-permute-start.2) | collective-permute-done | bytes 32800 | tf_op jit(solution)/shard_map/ppermute | solution.py:25
  12.5 1.0 collective-permute-start.3
  13.5 3.1 %collective-permute-done.1 = bf16[2,128,128]{2,1,0:T(8,128)(2,1)S(1)} collective-permute-done((bf16[2,128,128]{2,1,0:T(8,128)(2,1)S(1)}, bf16[2,128,128]{2,1,0:T(8,128)(2,1)S(1)}, u32[]{:S(2)}, u32[]{:S(2)}) %collective-permute-start.1) | collective-permute-done | bytes 65568 | tf_op jit(solution)/shard_map/ppermute | solution.py:25
  16.7 4.8 %collective-permute-done.3 = bf16[3,128,128]{2,1,0:T(8,128)(2,1)S(1)} collective-permute-done((bf16[3,128,128]{2,1,0:T(8,128)(2,1)S(1)}, bf16[3,128,128]{2,1,0:T(8,128)(2,1)S(1)}, u32[]{:S(2)}, u32[]{:S(2)}) %collective-permute-start.3) | collective-permute-done | bytes 98336 | tf_op jit(solution)/shard_map/ppermute | solution.py:25
  21.6 0.4 collective-permute-start.4
  22.0 7.5 %collective-permute-done.4 = bf16[8,128,128]{2,1,0:T(8,128)(2,1)S(1)} collective-permute-done((bf16[8,128,128]{2,1,0:T(8,128)(2,1)S(1)}, bf16[8,128,128]{2,1,0:T(8,128)(2,1)S(1)}, u32[]{:S(2)}, u32[]{:S(2)}) %collective-permute-start.4) | collective-permute-done | bytes 262176 | tf_op jit(solution)/shard_map/ppermute | solution.py:25
  29.6 0.1 pad_maximum_fusion.1
  29.7 0.1 collective-permute-start.5
  29.8 0.3 fusion
  30.1 1.6 %collective-permute-done.5 = bf16[2,8,128,128]{3,2,1,0:T(8,128)(2,1)S(1)} collective-permute-done((bf16[2,8,128,128]{3,2,1,0:T(8,128)(2,1)S(1)}, bf16[2,8,128,128]{3,2,1,0:T(8,128)(2,1)S(1)}, u32[]{:S(2)}, u32[]{:S(2)}) %collective-permute-start.5) | collective-permute-done | bytes 524320 | tf_op jit(solution)/shard_map/ppermute | solution.py:25
  31.7 0.1 select_bitcast_fusion.1
  31.7 0.1 pad_maximum_fusion
  31.9 0.1 slice_bitcast_fusion
  31.9 0.5 copy.11
  32.5 0.1 copy-done.25
  32.6 0.8 convolution_convert_fusion
  33.4 0.1 collective-permute-start.6
  33.5 2.0 %collective-permute-start.7 = (bf16[512,256]{1,0:T(8,128)(2,1)S(1)}, bf16[512,256]{1,0:T(8,128)(2,1)S(1)}, u32[]{:S(2)}, u32[]{:S(2)}) collective-permute-start(bf16[512,256]{1,0:T(8,128)(2,1)S(1)} %slice.45.refs_4_), channel_id=1, source_target_pairs={{112,0},{120,8},{0,16},{8,24},{16,32},{24,40},{32,48},{40,56},{48,... | collective-permute-start | bytes 786440 | tf_op jit(solution)/shard_map/ppermute | solution.py:25
  35.6 0.4 collective-permute-start.8
  36.0 6.1 %collective-permute-done.8 = bf16[512,128]{1,0:T(8,128)(2,1)S(1)} collective-permute-done((bf16[512,128]{1,0:T(8,128)(2,1)S(1)}, bf16[512,128]{1,0:T(8,128)(2,1)S(1)}, u32[]{:S(2)}, u32[]{:S(2)}) %collective-permute-start.8) | collective-permute-done | bytes 131104 | tf_op jit(solution)/shard_map/ppermute | solution.py:25
  42.1 1.0 collective-permute-done.7.refs_8_
  43.2 1.3 %collective-permute-start.14 = (bf16[1024,128]{1,0:T(8,128)(2,1)S(1)}, bf16[1024,128]{1,0:T(8,128)(2,1)S(1)}, u32[]{:S(2)}, u32[]{:S(2)}) collective-permute-start(bf16[1024,128]{1,0:T(8,128)(2,1)S(1)} %bitcast.35), channel_id=1, source_target_pairs={{4,0},{5,1},{6,2},{7,3},{0,4},{1,5},{2,6},{3,7},{12,8},{13,9},{14,... | collective-permute-start | bytes 786440 | tf_op jit(solution)/shard_map/ppermute | solution.py:33
  44.5 0.8 collective-permute-start.12
  45.3 1.2 collective-permute-start.13
  46.5 4.2 %collective-permute-done.14 = bf16[1024,128]{1,0:T(8,128)(2,1)S(1)} collective-permute-done((bf16[1024,128]{1,0:T(8,128)(2,1)S(1)}, bf16[1024,128]{1,0:T(8,128)(2,1)S(1)}, u32[]{:S(2)}, u32[]{:S(2)}) %collective-permute-start.14) | collective-permute-done | bytes 262176 | tf_op jit(solution)/shard_map/ppermute | solution.py:33
  50.7 0.9 collective-permute-done.12.refs_10_
  51.7 1.8 %collective-permute-done.13.refs_12_ = bf16[512,256]{1,0:T(8,128)(2,1)S(1)} collective-permute-done((bf16[512,256]{1,0:T(8,128)(2,1)S(1)}, bf16[512,256]{1,0:T(8,128)(2,1)S(1)}, u32[]{:S(2)}, u32[]{:S(2)}) %collective-permute-start.13) | collective-permute-done | bytes 262176 | tf_op jit(solution)/shard_map/ppermute | solution.py:25
  53.4 0.4 collective-permute-start.17
  53.8 1.7 %collective-permute-start.18 = (bf16[512,256]{1,0:T(8,128)(2,1)S(1)}, bf16[512,256]{1,0:T(8,128)(2,1)}, u32[]{:S(2)}, u32[]{:S(2)}) collective-permute-start(bf16[512,256]{1,0:T(8,128)(2,1)S(1)} %collective-permute-done.13.refs_12_), channel_id=1, source_target_pairs={{112,0},{120,8},{0,16},{8,24},{16,32},{24,40},{32,48},{40,56},{48,... | collective-permute-start | bytes 786440 | tf_op jit(solution)/shard_map/ppermute | solution.py:25
  55.5 2.8 %collective-permute-start.22 = (bf16[2,1024,128]{2,1,0:T(8,128)(2,1)S(1)}, bf16[2,1024,128]{2,1,0:T(8,128)(2,1)S(1)}, u32[]{:S(2)}, u32[]{:S(2)}) collective-permute-start(bf16[2,1024,128]{2,1,0:T(8,128)(2,1)S(1)} %pad_maximum_fusion.2.refs_0_), channel_id=1, source_target_pairs={{1,0},{2,1},{3,2},{0,3},{5,4},{6,5},{7,6},{4,7},{9,8},{10,9},{11,1... | collective-permute-start | bytes 1572872 | tf_op jit(solution)/shard_map/ppermute | solution.py:33
  58.3 0.1 collective-permute-start.9
  58.4 0.5 collective-permute-start.10
  58.9 1.0 collective-permute-done.17.refs_14_
  59.9 1.6 %collective-permute-done.18.refs_16_ = bf16[512,256]{1,0:T(8,128)(2,1)} collective-permute-done((bf16[512,256]{1,0:T(8,128)(2,1)S(1)}, bf16[512,256]{1,0:T(8,128)(2,1)}, u32[]{:S(2)}, u32[]{:S(2)}) %collective-permute-start.18) | collective-permute-done | bytes 262176 | tf_op jit(solution)/shard_map/ppermute | solution.py:25
  61.5 0.1 collective-permute-start.21
  61.6 0.1 broadcast_subtract_fusion
  61.7 0.1 sub.39
  62.4 0.6 fusion.18
  63.0 6.0 %collective-permute-done.21.refs_18_ = bf16[512,256]{1,0:T(8,128)(2,1)} collective-permute-done((bf16[512,256]{1,0:T(8,128)(2,1)}, bf16[512,256]{1,0:T(8,128)(2,1)}, u32[]{:S(2)}, u32[]{:S(2)}) %collective-permute-start.21) | collective-permute-done | bytes 262176 | tf_op jit(solution)/shard_map/ppermute | solution.py:25
  69.0 0.5 collective-permute-start.16
  69.5 0.1 collective-permute-start.19
  69.6 0.4 collective-permute-start.20
  70.0 0.1 collective-permute-start.23
  70.1 0.5 compare_select_fusion.12.refs_0_
  70.6 0.7 pad_maximum_fusion.3.refs_3_
  71.4 1.6 %collective-permute-start.25 = (bf16[2,1024,128]{2,1,0:T(8,128)(2,1)S(1)}, bf16[2,1024,128]{2,1,0:T(8,128)(2,1)S(1)}, u32[]{:S(2)}, u32[]{:S(2)}) collective-permute-start(bf16[2,1024,128]{2,1,0:T(8,128)(2,1)S(1)} %pad_maximum_fusion.2.refs_0_), channel_id=1, source_target_pairs={{3,0},{0,1},{1,2},{2,3},{7,4},{4,5},{5,6},{6,7},{11,8},{8,9},{9,10... | collective-permute-start | bytes 1572872 | tf_op jit(solution)/shard_map/ppermute | solution.py:33
  72.9 1.9 %collective-permute-start.26 = (bf16[2,1024,128]{2,1,0:T(8,128)(2,1)S(1)}, bf16[2,1024,128]{2,1,0:T(8,128)(2,1)S(1)}, u32[]{:S(2)}, u32[]{:S(2)}) collective-permute-start(bf16[2,1024,128]{2,1,0:T(8,128)(2,1)S(1)} %collective-permute-done.22.refs_1_), channel_id=1, source_target_pairs={{1,0},{2,1},{3,2},{0,3},{5,4},{6,5},{7,6},{4,7},{9,8},{10,9},{11,1... | collective-permute-start | bytes 1572872 | tf_op jit(solution)/shard_map/ppermute | solution.py:33
  74.8 0.7 copy-done.22
  75.5 0.7 copy-done.23
  76.2 0.7 copy-done.24
  77.0 16.9 %shard_map.91 = (bf16[512,256]{1,0:T(8,128)(2,1)}, f32[512,128]{1,0:T(8,128)}, f32[512,128]{1,0:T(8,128)}) custom-call(f32[32]{0:T(128)} %compare_select_fusion.12.refs_0_, f32[32]{0:T(128)} %get-tuple-element.33.refs_1_, f32[1]{0:T(128)} %mul.57.refs_2_, bf16[1024,128]{1,0:T(8,128)(2,1)} %pad_maximum_fusion.3.refs_3_, bf16[512,256]{1,0:T(8,128)(2,1)} %copy-done.7, ...), custom_call_target="tpu_custom_call" | custom-call | flops 8589934592 | bytes 5242880 | tf_op jit(solution)/shard_map/pallas_call | solution.py:118
  93.9 0.7 collective-permute-start.24
  94.6 9.4 %collective-permute-done.24.got_ref = bf16[512,256]{1,0:T(8,128)(2,1)S(1)} collective-permute-done((bf16[512,256]{1,0:T(8,128)(2,1)}, bf16[512,256]{1,0:T(8,128)(2,1)S(1)}, u32[]{:S(2)}, u32[]{:S(2)}) %collective-permute-start.24) | collective-permute-done | bytes 262176 | tf_op jit(solution)/shard_map/ppermute | solution.py:25
  104.0 0.7 copy-done.6
  104.8 2.1 %shard_map.92 = bf16[512,128]{1,0:T(8,128)(2,1)} custom-call(f32[512,128]{1,0:T(8,128)} %get-tuple-element.29.out_ref, f32[512,128]{1,0:T(8,128)} %get-tuple-element.30.lse_ref, bf16[512,256]{1,0:T(8,128)(2,1)} %copy-done.6), custom_call_target="tpu_custom_call" | custom-call | tf_op jit(solution)/shard_map/pallas_call | solution.py:157
  106.8 3.4 %all-to-all-start = ((bf16[8,64,128]{2,1,0:T(8,128)(2,1)}), bf16[8,64,128]{2,1,0:T(8,128)(2,1)S(1)}, u32[]{:S(2)}, u32[]{:S(2)}) async-start(bf16[8,64,128]{2,1,0:T(8,128)(2,1)} %bitcast.37), calls=%async_computation | async-start | bytes 262144 | tf_op jit(solution)/shard_map/all_to_all | solution.py:265
  110.2 0.6 fusion.8.head_ref
  110.8 5.9 %all-to-all-done.mixed_ref = bf16[8,64,128]{2,1,0:T(8,128)(2,1)S(1)} async-done(((bf16[8,64,128]{2,1,0:T(8,128)(2,1)}), bf16[8,64,128]{2,1,0:T(8,128)(2,1)S(1)}, u32[]{:S(2)}, u32[]{:S(2)}) %all-to-all-start) | async-done | bytes 131104 | tf_op jit(solution)/shard_map/all_to_all | solution.py:265
  116.7 0.6 copy-done.5
  117.4 3.7 %shard_map.93 = bf16[64,1024]{1,0:T(8,128)(2,1)} custom-call(s32[8]{0:T(128)} %fusion.8.head_ref, bf16[8,64,128]{2,1,0:T(8,128)(2,1)} %copy-done.5, bf16[2,1024,128]{2,1,0:T(8,128)(2,1)} %copy-done, bf16[2,1024,128]{2,1,0:T(8,128)(2,1)} %copy-done.2, bf16[2,1024,128]{2,1,0:T(8,128)(2,1)} %copy-done.3, bf16[2,1024,128]{2,1,0:T(8,128)(2,1)} %copy-done.4), custom_call_target="tpu_custom_call" | custom-call | tf_op jit(solution)/shard_map/pallas_call | solution.py:177
  (80 shorter events, 0.5 us)
Async XLA Ops:
  0.0 16.7 %copy-start.8 = (bf16[3,32,128]{2,1,0:T(8,128)(2,1)S(1)}, bf16[3,32,128]{2,1,0:T(8,128)(2,1)}, u32[]{:S(2)}) copy-start(bf16[3,32,128]{2,1,0:T(8,128)(2,1)} %param.11) | copy-start | bytes 73732
  0.0 16.7 %copy-start.9 = (bf16[128,32]{0,1:T(8,128)(2,1)S(1)}, bf16[128,32]{0,1:T(8,128)(2,1)}, u32[]{:S(2)}) copy-start(bf16[128,32]{0,1:T(8,128)(2,1)} %param.13) | copy-start | bytes 24580
  0.8 7.5 %collective-permute-start = (bf16[128,128]{1,0:T(8,128)(2,1)S(1)}, bf16[128,128]{1,0:T(8,128)(2,1)S(1)}, u32[]{:S(2)}, u32[]{:S(2)}) collective-permute-start(bf16[128,128]{1,0:T(8,128)(2,1)S(1)} %get-tuple-element.40), channel_id=1, source_target_pairs={{16,0},{24,8},{32,16},{40,24},{48,32},{56,40},{64,48},{72,56},{80,... | collective-permute-start | bytes 98312 | tf_op jit(solution)/shard_map/ppermute | solution.py:25
  6.8 5.7 %collective-permute-start.2 = (bf16[128,128]{1,0:T(8,128)(2,1)S(1)}, bf16[128,128]{1,0:T(8,128)(2,1)S(1)}, u32[]{:S(2)}, u32[]{:S(2)}) collective-permute-start(bf16[128,128]{1,0:T(8,128)(2,1)S(1)} %get-tuple-element.40), channel_id=1, source_target_pairs={{112,0},{120,8},{0,16},{8,24},{16,32},{24,40},{32,48},{40,56},{48,... | collective-permute-start | bytes 98312 | tf_op jit(solution)/shard_map/ppermute | solution.py:25
  8.4 8.2 %collective-permute-start.1 = (bf16[2,128,128]{2,1,0:T(8,128)(2,1)S(1)}, bf16[2,128,128]{2,1,0:T(8,128)(2,1)S(1)}, u32[]{:S(2)}, u32[]{:S(2)}) collective-permute-start(bf16[2,128,128]{2,1,0:T(8,128)(2,1)S(1)} %pad_maximum_fusion.5), channel_id=1, source_target_pairs={{80,0},{88,8},{96,16},{104,24},{112,32},{120,40},{0,48},{8,56},{16... | collective-permute-start | bytes 196616 | tf_op jit(solution)/shard_map/ppermute | solution.py:25
  12.5 9.1 %collective-permute-start.3 = (bf16[3,128,128]{2,1,0:T(8,128)(2,1)S(1)}, bf16[3,128,128]{2,1,0:T(8,128)(2,1)S(1)}, u32[]{:S(2)}, u32[]{:S(2)}) collective-permute-start(bf16[3,128,128]{2,1,0:T(8,128)(2,1)S(1)} %pad_maximum_fusion.4), channel_id=1, source_target_pairs={{48,0},{56,8},{64,16},{72,24},{80,32},{88,40},{96,48},{104,56},{11... | collective-permute-start | bytes 294920 | tf_op jit(solution)/shard_map/ppermute | solution.py:25
  21.6 8.0 %collective-permute-start.4 = (bf16[8,128,128]{2,1,0:T(8,128)(2,1)S(1)}, bf16[8,128,128]{2,1,0:T(8,128)(2,1)S(1)}, u32[]{:S(2)}, u32[]{:S(2)}) collective-permute-start(bf16[8,128,128]{2,1,0:T(8,128)(2,1)S(1)} %slice_dynamic-update-slice_fusion), channel_id=1, source_target_pairs={{128,0},{136,8},{144,16},{152,24},{160,32},{168,40},{176,48},{184,... | collective-permute-start | bytes 786440 | tf_op jit(solution)/shard_map/ppermute | solution.py:25
  22.0 7.8 %copy-start.1 = (bf16[512,1024]{1,0:T(8,128)(2,1)S(1)}, bf16[512,1024]{1,0:T(8,128)(2,1)}, u32[]{:S(2)}) copy-start(bf16[512,1024]{1,0:T(8,128)(2,1)} %param.9) | copy-start | bytes 3145732
  29.7 2.0 %collective-permute-start.5 = (bf16[2,8,128,128]{3,2,1,0:T(8,128)(2,1)S(1)}, bf16[2,8,128,128]{3,2,1,0:T(8,128)(2,1)S(1)}, u32[]{:S(2)}, u32[]{:S(2)}) collective-permute-start(bf16[2,8,128,128]{3,2,1,0:T(8,128)(2,1)S(1)} %pad_maximum_fusion.1), channel_id=1, source_target_pairs={{8,0},{0,8},{24,16},{16,24},{40,32},{32,40},{56,48},{48,56},{72,64... | collective-permute-start | bytes 1572872 | tf_op jit(solution)/shard_map/ppermute | solution.py:25
  31.9 0.7 copy-start.25
  33.4 37.9 %copy-start.7 = (bf16[512,256]{1,0:T(8,128)(2,1)}, bf16[512,256]{1,0:T(8,128)(2,1)S(1)}, u32[]{:S(2)}) copy-start(bf16[512,256]{1,0:T(8,128)(2,1)S(1)} %slice.45.refs_4_) | copy-start | bytes 786436
  33.4 22.0 %copy-start.12 = (s32[16]{0:T(128)S(1)}, s32[16]{0:T(128)}, u32[]{:S(2)}) copy-start(s32[16]{0:T(128)} %constant.183.clone) | copy-start | bytes 196
  33.4 22.0 %copy-start.13 = (s32[16]{0:T(128)S(1)}, s32[16]{0:T(128)}, u32[]{:S(2)}) copy-start(s32[16]{0:T(128)} %constant.184.clone) | copy-start | bytes 196
  33.4 8.7 %collective-permute-start.6 = (bf16[512,256]{1,0:T(8,128)(2,1)S(1)}, bf16[512,256]{1,0:T(8,128)(2,1)S(1)}, u32[]{:S(2)}, u32[]{:S(2)}) collective-permute-start(bf16[512,256]{1,0:T(8,128)(2,1)S(1)} %slice.45.refs_4_), channel_id=1, source_target_pairs={{16,0},{24,8},{32,16},{40,24},{48,32},{56,40},{64,48},{72,56},{80,... | collective-permute-start | bytes 786440 | tf_op jit(solution)/shard_map/ppermute | solution.py:25
  33.5 9.6 %collective-permute-start.7 = (bf16[512,256]{1,0:T(8,128)(2,1)S(1)}, bf16[512,256]{1,0:T(8,128)(2,1)S(1)}, u32[]{:S(2)}, u32[]{:S(2)}) collective-permute-start(bf16[512,256]{1,0:T(8,128)(2,1)S(1)} %slice.45.refs_4_), channel_id=1, source_target_pairs={{112,0},{120,8},{0,16},{8,24},{16,32},{24,40},{32,48},{40,56},{48,... | collective-permute-start | bytes 786440 | tf_op jit(solution)/shard_map/ppermute | solution.py:25
  35.6 6.6 %collective-permute-start.8 = (bf16[512,128]{1,0:T(8,128)(2,1)S(1)}, bf16[512,128]{1,0:T(8,128)(2,1)S(1)}, u32[]{:S(2)}, u32[]{:S(2)}) collective-permute-start(bf16[512,128]{1,0:T(8,128)(2,1)S(1)} %slice.44), channel_id=1, source_target_pairs={{128,0},{136,8},{144,16},{152,24},{160,32},{168,40},{176,48},{184,... | collective-permute-start | bytes 393224 | tf_op jit(solution)/shard_map/ppermute | solution.py:25
  42.1 34.8 %copy-start.14 = (bf16[512,256]{1,0:T(8,128)(2,1)}, bf16[512,256]{1,0:T(8,128)(2,1)S(1)}, u32[]{:S(2)}) copy-start(bf16[512,256]{1,0:T(8,128)(2,1)S(1)} %collective-permute-done.6.refs_6_) | copy-start | bytes 786436
  43.2 33.8 %copy-start.15 = (bf16[512,256]{1,0:T(8,128)(2,1)}, bf16[512,256]{1,0:T(8,128)(2,1)S(1)}, u32[]{:S(2)}) copy-start(bf16[512,256]{1,0:T(8,128)(2,1)S(1)} %collective-permute-done.7.refs_8_) | copy-start | bytes 786436
  43.2 7.5 %collective-permute-start.14 = (bf16[1024,128]{1,0:T(8,128)(2,1)S(1)}, bf16[1024,128]{1,0:T(8,128)(2,1)S(1)}, u32[]{:S(2)}, u32[]{:S(2)}) collective-permute-start(bf16[1024,128]{1,0:T(8,128)(2,1)S(1)} %bitcast.35), channel_id=1, source_target_pairs={{4,0},{5,1},{6,2},{7,3},{0,4},{1,5},{2,6},{3,7},{12,8},{13,9},{14,... | collective-permute-start | bytes 786440 | tf_op jit(solution)/shard_map/ppermute | solution.py:33
  44.5 7.2 %collective-permute-start.12 = (bf16[512,256]{1,0:T(8,128)(2,1)S(1)}, bf16[512,256]{1,0:T(8,128)(2,1)S(1)}, u32[]{:S(2)}, u32[]{:S(2)}) collective-permute-start(bf16[512,256]{1,0:T(8,128)(2,1)S(1)} %collective-permute-done.6.refs_6_), channel_id=1, source_target_pairs={{16,0},{24,8},{32,16},{40,24},{48,32},{56,40},{64,48},{72,56},{80,... | collective-permute-start | bytes 786440 | tf_op jit(solution)/shard_map/ppermute | solution.py:25
  45.3 8.1 %collective-permute-start.13 = (bf16[512,256]{1,0:T(8,128)(2,1)S(1)}, bf16[512,256]{1,0:T(8,128)(2,1)S(1)}, u32[]{:S(2)}, u32[]{:S(2)}) collective-permute-start(bf16[512,256]{1,0:T(8,128)(2,1)S(1)} %collective-permute-done.7.refs_8_), channel_id=1, source_target_pairs={{112,0},{120,8},{0,16},{8,24},{16,32},{24,40},{32,48},{40,56},{48,... | collective-permute-start | bytes 786440 | tf_op jit(solution)/shard_map/ppermute | solution.py:25
  50.7 43.2 %copy-start = (bf16[2,1024,128]{2,1,0:T(8,128)(2,1)}, bf16[2,1024,128]{2,1,0:T(8,128)(2,1)S(1)}, u32[]{:S(2)}) copy-start(bf16[2,1024,128]{2,1,0:T(8,128)(2,1)S(1)} %pad_maximum_fusion.2.refs_0_) | copy-start | bytes 1572868
  51.7 25.3 %copy-start.16 = (bf16[512,256]{1,0:T(8,128)(2,1)}, bf16[512,256]{1,0:T(8,128)(2,1)S(1)}, u32[]{:S(2)}) copy-start(bf16[512,256]{1,0:T(8,128)(2,1)S(1)} %collective-permute-done.12.refs_10_) | copy-start | bytes 786436
  53.4 23.5 %copy-start.17 = (bf16[512,256]{1,0:T(8,128)(2,1)}, bf16[512,256]{1,0:T(8,128)(2,1)S(1)}, u32[]{:S(2)}) copy-start(bf16[512,256]{1,0:T(8,128)(2,1)S(1)} %collective-permute-done.13.refs_12_) | copy-start | bytes 786436
  53.4 6.5 %collective-permute-start.17 = (bf16[512,256]{1,0:T(8,128)(2,1)S(1)}, bf16[512,256]{1,0:T(8,128)(2,1)}, u32[]{:S(2)}, u32[]{:S(2)}) collective-permute-start(bf16[512,256]{1,0:T(8,128)(2,1)S(1)} %collective-permute-done.12.refs_10_), channel_id=1, source_target_pairs={{16,0},{24,8},{32,16},{40,24},{48,32},{56,40},{64,48},{72,56},{80,... | collective-permute-start | bytes 786440 | tf_op jit(solution)/shard_map/ppermute | solution.py:25
  53.8 7.7 %collective-permute-start.18 = (bf16[512,256]{1,0:T(8,128)(2,1)S(1)}, bf16[512,256]{1,0:T(8,128)(2,1)}, u32[]{:S(2)}, u32[]{:S(2)}) collective-permute-start(bf16[512,256]{1,0:T(8,128)(2,1)S(1)} %collective-permute-done.13.refs_12_), channel_id=1, source_target_pairs={{112,0},{120,8},{0,16},{8,24},{16,32},{24,40},{32,48},{40,56},{48,... | collective-permute-start | bytes 786440 | tf_op jit(solution)/shard_map/ppermute | solution.py:25
  55.5 13.5 %collective-permute-start.22 = (bf16[2,1024,128]{2,1,0:T(8,128)(2,1)S(1)}, bf16[2,1024,128]{2,1,0:T(8,128)(2,1)S(1)}, u32[]{:S(2)}, u32[]{:S(2)}) collective-permute-start(bf16[2,1024,128]{2,1,0:T(8,128)(2,1)S(1)} %pad_maximum_fusion.2.refs_0_), channel_id=1, source_target_pairs={{1,0},{2,1},{3,2},{0,3},{5,4},{6,5},{7,6},{4,7},{9,8},{10,9},{11,1... | collective-permute-start | bytes 1572872 | tf_op jit(solution)/shard_map/ppermute | solution.py:33
  58.3 11.1 %collective-permute-start.9 = (bf16[512,256]{1,0:T(8,128)(2,1)S(1)}, bf16[512,256]{1,0:T(8,128)(2,1)S(1)}, u32[]{:S(2)}, u32[]{:S(2)}) collective-permute-start(bf16[512,256]{1,0:T(8,128)(2,1)S(1)} %slice.45.refs_4_), channel_id=1, source_target_pairs={{8,0},{0,8},{24,16},{16,24},{40,32},{32,40},{56,48},{48,56},{72,64... | collective-permute-start | bytes 786440 | tf_op jit(solution)/shard_map/ppermute | solution.py:25
  58.4 11.1 %collective-permute-start.10 = (bf16[512,256]{1,0:T(8,128)(2,1)S(1)}, bf16[512,256]{1,0:T(8,128)(2,1)S(1)}, u32[]{:S(2)}, u32[]{:S(2)}) collective-permute-start(bf16[512,256]{1,0:T(8,128)(2,1)S(1)} %collective-permute-done.6.refs_6_), channel_id=1, source_target_pairs={{8,0},{0,8},{24,16},{16,24},{40,32},{32,40},{56,48},{48,56},{72,64... | collective-permute-start | bytes 786440 | tf_op jit(solution)/shard_map/ppermute | solution.py:25
  59.9 10.1 %collective-permute-start.11 = (bf16[512,256]{1,0:T(8,128)(2,1)S(1)}, bf16[512,256]{1,0:T(8,128)(2,1)}, u32[]{:S(2)}, u32[]{:S(2)}) collective-permute-start(bf16[512,256]{1,0:T(8,128)(2,1)S(1)} %collective-permute-done.7.refs_8_), channel_id=1, source_target_pairs={{8,0},{0,8},{24,16},{16,24},{40,32},{32,40},{56,48},{48,56},{72,64... | collective-permute-start | bytes 786440 | tf_op jit(solution)/shard_map/ppermute | solution.py:25
  61.5 7.5 %collective-permute-start.21 = (bf16[512,256]{1,0:T(8,128)(2,1)}, bf16[512,256]{1,0:T(8,128)(2,1)}, u32[]{:S(2)}, u32[]{:S(2)}) collective-permute-start(bf16[512,256]{1,0:T(8,128)(2,1)} %collective-permute-done.17.refs_14_), channel_id=1, source_target_pairs={{16,0},{24,8},{32,16},{40,24},{48,32},{56,40},{64,48},{72,56},{80,... | collective-permute-start | bytes 786440 | tf_op jit(solution)/shard_map/ppermute | solution.py:25
  68.9 2.4 %collective-permute-start.15 = (bf16[512,256]{1,0:T(8,128)(2,1)S(1)}, bf16[512,256]{1,0:T(8,128)(2,1)S(1)}, u32[]{:S(2)}, u32[]{:S(2)}) collective-permute-start(bf16[512,256]{1,0:T(8,128)(2,1)S(1)} %collective-permute-done.12.refs_10_), channel_id=1, source_target_pairs={{8,0},{0,8},{24,16},{16,24},{40,32},{32,40},{56,48},{48,56},{72,64... | collective-permute-start | bytes 786440 | tf_op jit(solution)/shard_map/ppermute | solution.py:25
  68.9 24.9 %copy-start.2 = (bf16[2,1024,128]{2,1,0:T(8,128)(2,1)}, bf16[2,1024,128]{2,1,0:T(8,128)(2,1)S(1)}, u32[]{:S(2)}) copy-start(bf16[2,1024,128]{2,1,0:T(8,128)(2,1)S(1)} %collective-permute-done.22.refs_1_) | copy-start | bytes 1572868
  69.0 4.0 %collective-permute-start.16 = (bf16[512,256]{1,0:T(8,128)(2,1)S(1)}, bf16[512,256]{1,0:T(8,128)(2,1)S(1)}, u32[]{:S(2)}, u32[]{:S(2)}) collective-permute-start(bf16[512,256]{1,0:T(8,128)(2,1)S(1)} %collective-permute-done.13.refs_12_), channel_id=1, source_target_pairs={{8,0},{0,8},{24,16},{16,24},{40,32},{32,40},{56,48},{48,56},{72,64... | collective-permute-start | bytes 786440 | tf_op jit(solution)/shard_map/ppermute | solution.py:25
  69.5 1.9 %copy-start.18 = (bf16[512,256]{1,0:T(8,128)(2,1)}, bf16[512,256]{1,0:T(8,128)(2,1)S(1)}, u32[]{:S(2)}) copy-start(bf16[512,256]{1,0:T(8,128)(2,1)S(1)} %collective-permute-done.9.refs_5_) | copy-start | bytes 786436
  69.5 5.4 %collective-permute-start.19 = (bf16[512,256]{1,0:T(8,128)(2,1)}, bf16[512,256]{1,0:T(8,128)(2,1)S(1)}, u32[]{:S(2)}, u32[]{:S(2)}) collective-permute-start(bf16[512,256]{1,0:T(8,128)(2,1)} %collective-permute-done.17.refs_14_), channel_id=1, source_target_pairs={{8,0},{0,8},{24,16},{16,24},{40,32},{32,40},{56,48},{48,56},{72,64... | collective-permute-start | bytes 786440 | tf_op jit(solution)/shard_map/ppermute | solution.py:25
  69.6 3.4 %copy-start.19 = (bf16[512,256]{1,0:T(8,128)(2,1)}, bf16[512,256]{1,0:T(8,128)(2,1)S(1)}, u32[]{:S(2)}) copy-start(bf16[512,256]{1,0:T(8,128)(2,1)S(1)} %collective-permute-done.10.refs_7_) | copy-start | bytes 786436
  69.6 6.0 %collective-permute-start.20 = (bf16[512,256]{1,0:T(8,128)(2,1)}, bf16[512,256]{1,0:T(8,128)(2,1)S(1)}, u32[]{:S(2)}, u32[]{:S(2)}) collective-permute-start(bf16[512,256]{1,0:T(8,128)(2,1)} %collective-permute-done.18.refs_16_), channel_id=1, source_target_pairs={{8,0},{0,8},{24,16},{16,24},{40,32},{32,40},{56,48},{48,56},{72,64... | collective-permute-start | bytes 786440 | tf_op jit(solution)/shard_map/ppermute | solution.py:25
  70.0 6.3 %collective-permute-start.23 = (bf16[512,256]{1,0:T(8,128)(2,1)}, bf16[512,256]{1,0:T(8,128)(2,1)S(1)}, u32[]{:S(2)}, u32[]{:S(2)}) collective-permute-start(bf16[512,256]{1,0:T(8,128)(2,1)} %collective-permute-done.21.refs_18_), channel_id=1, source_target_pairs={{8,0},{0,8},{24,16},{16,24},{40,32},{32,40},{56,48},{48,56},{72,64... | collective-permute-start | bytes 786440 | tf_op jit(solution)/shard_map/ppermute | solution.py:25
  71.3 1.6 %copy-start.20 = (bf16[512,256]{1,0:T(8,128)(2,1)}, bf16[512,256]{1,0:T(8,128)(2,1)S(1)}, u32[]{:S(2)}) copy-start(bf16[512,256]{1,0:T(8,128)(2,1)S(1)} %collective-permute-done.15.refs_11_) | copy-start | bytes 786436
  71.4 39.5 %collective-permute-start.25 = (bf16[2,1024,128]{2,1,0:T(8,128)(2,1)S(1)}, bf16[2,1024,128]{2,1,0:T(8,128)(2,1)S(1)}, u32[]{:S(2)}, u32[]{:S(2)}) collective-permute-start(bf16[2,1024,128]{2,1,0:T(8,128)(2,1)S(1)} %pad_maximum_fusion.2.refs_0_), channel_id=1, source_target_pairs={{3,0},{0,1},{1,2},{2,3},{7,4},{4,5},{5,6},{6,7},{11,8},{8,9},{9,10... | collective-permute-start | bytes 1572872 | tf_op jit(solution)/shard_map/ppermute | solution.py:33
  72.9 1.9 %copy-start.21 = (bf16[512,256]{1,0:T(8,128)(2,1)}, bf16[512,256]{1,0:T(8,128)(2,1)S(1)}, u32[]{:S(2)}) copy-start(bf16[512,256]{1,0:T(8,128)(2,1)S(1)} %collective-permute-done.16.refs_13_) | copy-start | bytes 786436
  72.9 37.9 %collective-permute-start.26 = (bf16[2,1024,128]{2,1,0:T(8,128)(2,1)S(1)}, bf16[2,1024,128]{2,1,0:T(8,128)(2,1)S(1)}, u32[]{:S(2)}, u32[]{:S(2)}) collective-permute-start(bf16[2,1024,128]{2,1,0:T(8,128)(2,1)S(1)} %collective-permute-done.22.refs_1_), channel_id=1, source_target_pairs={{1,0},{2,1},{3,2},{0,3},{5,4},{6,5},{7,6},{4,7},{9,8},{10,9},{11,1... | collective-permute-start | bytes 1572872 | tf_op jit(solution)/shard_map/ppermute | solution.py:33
  74.8 0.7 copy-start.22
  75.5 0.7 copy-start.23
  76.2 0.7 copy-start.24
  93.9 16.3 %copy-start.10 = (s32[8]{0:T(128)S(1)}, s32[8]{0:T(128)}, u32[]{:S(2)}) copy-start(s32[8]{0:T(128)} %constant.185.clone) | copy-start | bytes 100
  93.9 16.3 %copy-start.11 = (s32[8]{0:T(128)S(1)}, s32[8]{0:T(128)}, u32[]{:S(2)}) copy-start(s32[8]{0:T(128)} %constant.186.clone) | copy-start | bytes 100
  93.9 10.1 %collective-permute-start.24 = (bf16[512,256]{1,0:T(8,128)(2,1)}, bf16[512,256]{1,0:T(8,128)(2,1)S(1)}, u32[]{:S(2)}, u32[]{:S(2)}) collective-permute-start(bf16[512,256]{1,0:T(8,128)(2,1)} %get-tuple-element.31), channel_id=1, source_target_pairs={{128,0},{136,8},{144,16},{152,24},{160,32},{168,40},{176,48},{184,... | collective-permute-start | bytes 786440 | tf_op jit(solution)/shard_map/ppermute | solution.py:25
  104.0 0.7 copy-start.6
  106.8 9.9 %all-to-all-start = ((bf16[8,64,128]{2,1,0:T(8,128)(2,1)}), bf16[8,64,128]{2,1,0:T(8,128)(2,1)S(1)}, u32[]{:S(2)}, u32[]{:S(2)}) async-start(bf16[8,64,128]{2,1,0:T(8,128)(2,1)} %bitcast.37), calls=%async_computation | async-start | bytes 262144 | tf_op jit(solution)/shard_map/all_to_all | solution.py:265
  110.8 5.9 %copy-start.3 = (bf16[2,1024,128]{2,1,0:T(8,128)(2,1)}, bf16[2,1024,128]{2,1,0:T(8,128)(2,1)S(1)}, u32[]{:S(2)}) copy-start(bf16[2,1024,128]{2,1,0:T(8,128)(2,1)S(1)} %collective-permute-done.25.refs_2_) | copy-start | bytes 1572868
  110.8 5.9 %copy-start.4 = (bf16[2,1024,128]{2,1,0:T(8,128)(2,1)}, bf16[2,1024,128]{2,1,0:T(8,128)(2,1)S(1)}, u32[]{:S(2)}) copy-start(bf16[2,1024,128]{2,1,0:T(8,128)(2,1)S(1)} %collective-permute-done.26.refs_3_) | copy-start | bytes 1572868
  116.7 0.7 copy-start.5

commit v6 on v5

--- a/solution.py
+++ b/solution.py
@@ -252,15 +252,15 @@
         if step == 1:
             pair = jnp.stack([w_out_t, head_permute(w_out_t, 1, 0)])
         elif step == 2:
-            east, west = head_permute(pair, 0, 1), head_permute(pair, 0, -1)
-        elif step == Z // 2:
-            weights = [pair, east, west, head_permute(east, 0, 1)]
+            east = head_permute(pair, 0, 1)
         for piece in got:
             kvs += [piece, tm_permute(piece, 0, 0, 1)]
     queries = jnp.concatenate([query, far_query], axis=0)
 
     send, keep, keep_lse = attention(signs, bases, slope, queries, kvs, 128 ** (-0.5) * LOG2E)
+    send, keep, east, pair = lax.optimization_barrier((send, keep, east, pair))
     got = tm_permute(send, 1, 0, 0)
+    weights = [pair, east, head_permute(pair, 0, -1), head_permute(east, 0, 1)]
     mixed = merge_halves(keep, keep_lse, got).reshape(YL * X, rows // (YL * X), 128)
     mixed = lax.all_to_all(mixed, "head", split_axis=0, concat_axis=0, tiled=True)
     place = lax.axis_index("head")

time: 121 us -> 123 us (1.017)
  starting transfers between devices: 29.9 us -> 31.5 us
    ppermute x23, starting transfers between devices: 18.9 us -> 20.6 us  [tm_permute(): return lax.ppermute(x, 'tm', pairs)]
    unnamed x52 -> x54, local copies, waits for them, and re-layouts: 3.69 us -> 4.49 us
  transfers between devices with their start and end apart: 28 -> 28, of which waited for: 16 -> 16; matrix products, arithmetic and copies ran while one was open for 3% -> 2% of each run, Pallas kernels for 16% -> 2%
where the time goes in v6:
time: 123 us
  waiting for transfers between devices  58 us (47%)
  starting transfers between devices  31.5 us (26%)
  Pallas kernels  22.6 us (18%)
  local copies, waits for them, and re-layouts  5.35 us (4%)
  other arithmetic  3.92 us (3%)
    ppermute x23, waiting for transfers between devices, tm_permute(): return lax.ppermute(x, 'tm', pairs)  48.6 us
    ppermute x23, starting transfers between devices, tm_permute(): return lax.ppermute(x, 'tm', pairs)  20.6 us
    pallas_call x1, Pallas kernels, attention(): pl.pallas_call(functools.partial(attention_kernel, shards, scale, blocks)...  16.9 us
    ppermute x4, starting transfers between devices, head_permute(): return lax.ppermute(x, 'head', pairs)  7.5 us
    all_to_all x1, waiting for transfers between devices, local(): lax.all_to_all(mixed, 'head', split_axis=0, concat_axis=0, tiled=True)  5.97 us
    unnamed x54, local copies, waits for them, and re-layouts  4.49 us
    pallas_call x1, Pallas kernels, output_projection(): pl.pallas_call(output_kernel, out_shape=jax.ShapeDtypeStruct((rows, width...  3.7 us
    all_to_all x1, starting transfers between devices, local(): lax.all_to_all(mixed, 'head', split_axis=0, concat_axis=0, tiled=True)  3.37 us
  transfers between devices with their start and end apart: 28, of which 16 were waited for; matrix products, arithmetic and copies ran while one was open for 2% of the time, Pallas kernels for 2%

profile of v6, /device:TPU:16, one launch (start us, length us, event | category | flops | bytes accessed | tf_op | source)
XLA Modules:
  0.0 123.1 jit_solution(532869187774259290)
XLA Ops:
  0.0 0.8 fusion.25
  0.8 5.9 %collective-permute-start = (bf16[128,128]{1,0:T(8,128)(2,1)S(1)}, bf16[128,128]{1,0:T(8,128)(2,1)S(1)}, u32[]{:S(2)}, u32[]{:S(2)}) collective-permute-start(bf16[128,128]{1,0:T(8,128)(2,1)S(1)} %get-tuple-element.48), channel_id=1, source_target_pairs={{16,0},{24,8},{32,16},{40,24},{48,32},{56,40},{64,48},{72,56},{80,... | collective-permute-start | bytes 98312 | tf_op jit(solution)/shard_map/ppermute | solution.py:25
  6.8 1.6 %collective-permute-done = bf16[128,128]{1,0:T(8,128)(2,1)S(1)} collective-permute-done((bf16[128,128]{1,0:T(8,128)(2,1)S(1)}, bf16[128,128]{1,0:T(8,128)(2,1)S(1)}, u32[]{:S(2)}, u32[]{:S(2)}) %collective-permute-start) | collective-permute-done | bytes 32800 | tf_op jit(solution)/shard_map/ppermute | solution.py:25
  8.4 2.4 %collective-permute-start.1 = (bf16[2,128,128]{2,1,0:T(8,128)(2,1)S(1)}, bf16[2,128,128]{2,1,0:T(8,128)(2,1)S(1)}, u32[]{:S(2)}, u32[]{:S(2)}) collective-permute-start(bf16[2,128,128]{2,1,0:T(8,128)(2,1)S(1)} %pad_maximum_fusion.5), channel_id=1, source_target_pairs={{80,0},{88,8},{96,16},{104,24},{112,32},{120,40},{0,48},{8,56},{16... | collective-permute-start | bytes 196616 | tf_op jit(solution)/shard_map/ppermute | solution.py:25
  10.7 1.8 %collective-permute-done.2 = bf16[128,128]{1,0:T(8,128)(2,1)S(1)} collective-permute-done((bf16[128,128]{1,0:T(8,128)(2,1)S(1)}, bf16[128,128]{1,0:T(8,128)(2,1)S(1)}, u32[]{:S(2)}, u32[]{:S(2)}) %collective-permute-start.2) | collective-permute-done | bytes 32800 | tf_op jit(solution)/shard_map/ppermute | solution.py:25
  12.5 1.0 collective-permute-start.3
  13.5 3.1 %collective-permute-done.1 = bf16[2,128,128]{2,1,0:T(8,128)(2,1)S(1)} collective-permute-done((bf16[2,128,128]{2,1,0:T(8,128)(2,1)S(1)}, bf16[2,128,128]{2,1,0:T(8,128)(2,1)S(1)}, u32[]{:S(2)}, u32[]{:S(2)}) %collective-permute-start.1) | collective-permute-done | bytes 65568 | tf_op jit(solution)/shard_map/ppermute | solution.py:25
  16.7 4.8 %collective-permute-done.3 = bf16[3,128,128]{2,1,0:T(8,128)(2,1)S(1)} collective-permute-done((bf16[3,128,128]{2,1,0:T(8,128)(2,1)S(1)}, bf16[3,128,128]{2,1,0:T(8,128)(2,1)S(1)}, u32[]{:S(2)}, u32[]{:S(2)}) %collective-permute-start.3) | collective-permute-done | bytes 98336 | tf_op jit(solution)/shard_map/ppermute | solution.py:25
  21.6 0.4 collective-permute-start.4
  22.0 7.5 %collective-permute-done.4 = bf16[8,128,128]{2,1,0:T(8,128)(2,1)S(1)} collective-permute-done((bf16[8,128,128]{2,1,0:T(8,128)(2,1)S(1)}, bf16[8,128,128]{2,1,0:T(8,128)(2,1)S(1)}, u32[]{:S(2)}, u32[]{:S(2)}) %collective-permute-start.4) | collective-permute-done | bytes 262176 | tf_op jit(solution)/shard_map/ppermute | solution.py:25
  29.7 0.1 collective-permute-start.5
  29.8 0.3 fusion
  30.1 1.6 %collective-permute-done.5 = bf16[2,8,128,128]{3,2,1,0:T(8,128)(2,1)S(1)} collective-permute-done((bf16[2,8,128,128]{3,2,1,0:T(8,128)(2,1)S(1)}, bf16[2,8,128,128]{3,2,1,0:T(8,128)(2,1)S(1)}, u32[]{:S(2)}, u32[]{:S(2)}) %collective-permute-start.5) | collective-permute-done | bytes 524320 | tf_op jit(solution)/shard_map/ppermute | solution.py:25
  31.7 0.1 select_bitcast_fusion.1
  31.7 0.1 pad_maximum_fusion
  31.9 0.5 copy.11
  32.5 0.1 copy-done.26
  32.6 0.8 convolution_convert_fusion
  33.4 1.2 collective-permute-start.7
  34.6 2.1 %collective-permute-start.6 = (bf16[512,256]{1,0:T(8,128)(2,1)S(1)}, bf16[512,256]{1,0:T(8,128)(2,1)S(1)}, u32[]{:S(2)}, u32[]{:S(2)}) collective-permute-start(bf16[512,256]{1,0:T(8,128)(2,1)S(1)} %slice.45.refs_4_), channel_id=1, source_target_pairs={{16,0},{24,8},{32,16},{40,24},{48,32},{56,40},{64,48},{72,56},{80,... | collective-permute-start | bytes 786440 | tf_op jit(solution)/shard_map/ppermute | solution.py:25
  36.8 0.4 collective-permute-start.8
  37.2 6.1 %collective-permute-done.8 = bf16[512,128]{1,0:T(8,128)(2,1)S(1)} collective-permute-done((bf16[512,128]{1,0:T(8,128)(2,1)S(1)}, bf16[512,128]{1,0:T(8,128)(2,1)S(1)}, u32[]{:S(2)}, u32[]{:S(2)}) %collective-permute-start.8) | collective-permute-done | bytes 131104 | tf_op jit(solution)/shard_map/ppermute | solution.py:25
  43.4 1.4 %collective-permute-start.14 = (bf16[1024,128]{1,0:T(8,128)(2,1)S(1)}, bf16[1024,128]{1,0:T(8,128)(2,1)S(1)}, u32[]{:S(2)}, u32[]{:S(2)}) collective-permute-start(bf16[1024,128]{1,0:T(8,128)(2,1)S(1)} %bitcast.35), channel_id=1, source_target_pairs={{4,0},{5,1},{6,2},{7,3},{0,4},{1,5},{2,6},{3,7},{12,8},{13,9},{14,... | collective-permute-start | bytes 786440 | tf_op jit(solution)/shard_map/ppermute | solution.py:33
  44.7 2.6 %collective-permute-start.12 = (bf16[512,256]{1,0:T(8,128)(2,1)S(1)}, bf16[512,256]{1,0:T(8,128)(2,1)S(1)}, u32[]{:S(2)}, u32[]{:S(2)}) collective-permute-start(bf16[512,256]{1,0:T(8,128)(2,1)S(1)} %collective-permute-done.6.refs_6_), channel_id=1, source_target_pairs={{16,0},{24,8},{32,16},{40,24},{48,32},{56,40},{64,48},{72,56},{80,... | collective-permute-start | bytes 786440 | tf_op jit(solution)/shard_map/ppermute | solution.py:25
  47.3 3.3 %collective-permute-done.14 = bf16[1024,128]{1,0:T(8,128)(2,1)S(1)} collective-permute-done((bf16[1024,128]{1,0:T(8,128)(2,1)S(1)}, bf16[1024,128]{1,0:T(8,128)(2,1)S(1)}, u32[]{:S(2)}, u32[]{:S(2)}) %collective-permute-start.14) | collective-permute-done | bytes 262176 | tf_op jit(solution)/shard_map/ppermute | solution.py:33
  50.8 1.0 collective-permute-done.12.refs_10_
  51.8 3.4 %collective-permute-done.13.refs_12_ = bf16[512,256]{1,0:T(8,128)(2,1)S(1)} collective-permute-done((bf16[512,256]{1,0:T(8,128)(2,1)S(1)}, bf16[512,256]{1,0:T(8,128)(2,1)S(1)}, u32[]{:S(2)}, u32[]{:S(2)}) %collective-permute-start.13) | collective-permute-done | bytes 262176 | tf_op jit(solution)/shard_map/ppermute | solution.py:25
  55.2 0.4 collective-permute-start.17
  55.6 1.7 %collective-permute-start.18 = (bf16[512,256]{1,0:T(8,128)(2,1)S(1)}, bf16[512,256]{1,0:T(8,128)(2,1)S(1)}, u32[]{:S(2)}, u32[]{:S(2)}) collective-permute-start(bf16[512,256]{1,0:T(8,128)(2,1)S(1)} %collective-permute-done.13.refs_12_), channel_id=1, source_target_pairs={{112,0},{120,8},{0,16},{8,24},{16,32},{24,40},{32,48},{40,56},{48,... | collective-permute-start | bytes 786440 | tf_op jit(solution)/shard_map/ppermute | solution.py:25
  57.3 2.8 %collective-permute-start.22 = (bf16[2,1024,128]{2,1,0:T(8,128)(2,1)S(1)}, bf16[2,1024,128]{2,1,0:T(8,128)(2,1)S(1)}, u32[]{:S(2)}, u32[]{:S(2)}) collective-permute-start(bf16[2,1024,128]{2,1,0:T(8,128)(2,1)S(1)} %pad_maximum_fusion.2.refs_0_), channel_id=1, source_target_pairs={{1,0},{2,1},{3,2},{0,3},{5,4},{6,5},{7,6},{4,7},{9,8},{10,9},{11,1... | collective-permute-start | bytes 1572872 | tf_op jit(solution)/shard_map/ppermute | solution.py:33
  60.1 0.1 collective-permute-start.9
  60.2 0.5 collective-permute-start.10
  60.7 0.9 collective-permute-done.17.refs_14_
  61.6 1.6 %collective-permute-done.18.refs_16_ = bf16[512,256]{1,0:T(8,128)(2,1)S(1)} collective-permute-done((bf16[512,256]{1,0:T(8,128)(2,1)S(1)}, bf16[512,256]{1,0:T(8,128)(2,1)S(1)}, u32[]{:S(2)}, u32[]{:S(2)}) %collective-permute-start.18) | collective-permute-done | bytes 262176 | tf_op jit(solution)/shard_map/ppermute | solution.py:25
  63.2 0.1 collective-permute-start.21
  64.0 0.1 sub.39
  64.1 0.5 fusion.18
  64.6 5.8 %collective-permute-done.21.refs_18_ = bf16[512,256]{1,0:T(8,128)(2,1)} collective-permute-done((bf16[512,256]{1,0:T(8,128)(2,1)S(1)}, bf16[512,256]{1,0:T(8,128)(2,1)}, u32[]{:S(2)}, u32[]{:S(2)}) %collective-permute-start.21) | collective-permute-done | bytes 262176 | tf_op jit(solution)/shard_map/ppermute | solution.py:25
  70.4 0.5 collective-permute-start.16
  70.9 0.1 collective-permute-start.19
  71.1 0.4 collective-permute-start.20
  71.5 0.1 collective-permute-start.23
  71.6 0.6 compare_select_fusion.12.refs_0_
  72.1 0.7 pad_maximum_fusion.3.refs_3_
  72.9 0.2 collective-permute-done.20.refs_17_
  73.1 0.5 copy-done.21
  73.6 0.1 copy-done.22
  73.7 0.1 copy-done.24
  73.8 0.5 copy-done.23
  74.3 0.7 copy-done.25
  75.0 16.9 %shard_map.91 = (bf16[512,256]{1,0:T(8,128)(2,1)}, f32[512,128]{1,0:T(8,128)}, f32[512,128]{1,0:T(8,128)}) custom-call(f32[32]{0:T(128)} %compare_select_fusion.12.refs_0_, f32[32]{0:T(128)} %get-tuple-element.41.refs_1_, f32[1]{0:T(128)} %mul.57.refs_2_, bf16[1024,128]{1,0:T(8,128)(2,1)} %pad_maximum_fusion.3.refs_3_, bf16[512,256]{1,0:T(8,128)(2,1)} %copy-done.7, ...), custom_call_target="tpu_custom_call" | custom-call | flops 8589934592 | bytes 5242880 | tf_op jit(solution)/shard_map/pallas_call | solution.py:118
  92.0 1.5 %collective-permute-start.25 = (bf16[2,1024,128]{2,1,0:T(8,128)(2,1)S(1)}, bf16[2,1024,128]{2,1,0:T(8,128)(2,1)S(1)}, u32[]{:S(2)}, u32[]{:S(2)}) collective-permute-start(bf16[2,1024,128]{2,1,0:T(8,128)(2,1)S(1)} %pad_maximum_fusion.2.refs_0_), channel_id=1, source_target_pairs={{3,0},{0,1},{1,2},{2,3},{7,4},{4,5},{5,6},{6,7},{11,8},{8,9},{9,10... | collective-permute-start | bytes 1572872 | tf_op jit(solution)/shard_map/ppermute | solution.py:33
  93.5 1.8 %collective-permute-start.26 = (bf16[2,1024,128]{2,1,0:T(8,128)(2,1)S(1)}, bf16[2,1024,128]{2,1,0:T(8,128)(2,1)S(1)}, u32[]{:S(2)}, u32[]{:S(2)}) collective-permute-start(bf16[2,1024,128]{2,1,0:T(8,128)(2,1)S(1)} %collective-permute-done.22.refs_1_), channel_id=1, source_target_pairs={{1,0},{2,1},{3,2},{0,3},{5,4},{6,5},{7,6},{4,7},{9,8},{10,9},{11,1... | collective-permute-start | bytes 1572872 | tf_op jit(solution)/shard_map/ppermute | solution.py:33
  95.3 0.6 collective-permute-start.24
  95.9 9.2 %collective-permute-done.24.got_ref = bf16[512,256]{1,0:T(8,128)(2,1)S(1)} collective-permute-done((bf16[512,256]{1,0:T(8,128)(2,1)}, bf16[512,256]{1,0:T(8,128)(2,1)S(1)}, u32[]{:S(2)}, u32[]{:S(2)}) %collective-permute-start.24) | collective-permute-done | bytes 262176 | tf_op jit(solution)/shard_map/ppermute | solution.py:25
  105.1 0.7 copy-done.6
  105.8 2.1 %shard_map.92 = bf16[512,128]{1,0:T(8,128)(2,1)} custom-call(f32[512,128]{1,0:T(8,128)} %get-tuple-element.36.out_ref, f32[512,128]{1,0:T(8,128)} %get-tuple-element.37.lse_ref, bf16[512,256]{1,0:T(8,128)(2,1)} %copy-done.6), custom_call_target="tpu_custom_call" | custom-call | tf_op jit(solution)/shard_map/pallas_call | solution.py:157
  107.8 3.4 %all-to-all-start = ((bf16[8,64,128]{2,1,0:T(8,128)(2,1)}), bf16[8,64,128]{2,1,0:T(8,128)(2,1)S(1)}, u32[]{:S(2)}, u32[]{:S(2)}) async-start(bf16[8,64,128]{2,1,0:T(8,128)(2,1)} %bitcast.37), calls=%async_computation | async-start | bytes 262144 | tf_op jit(solution)/shard_map/all_to_all | solution.py:265
  111.2 0.5 fusion.8.head_ref
  111.8 6.0 %all-to-all-done.mixed_ref = bf16[8,64,128]{2,1,0:T(8,128)(2,1)S(1)} async-done(((bf16[8,64,128]{2,1,0:T(8,128)(2,1)}), bf16[8,64,128]{2,1,0:T(8,128)(2,1)S(1)}, u32[]{:S(2)}, u32[]{:S(2)}) %all-to-all-start) | async-done | bytes 131104 | tf_op jit(solution)/shard_map/all_to_all | solution.py:265
  117.7 0.6 copy-done.5
  118.4 0.2 copy-done.3
  118.6 0.8 copy-done.4
  119.4 3.7 %shard_map.93 = bf16[64,1024]{1,0:T(8,128)(2,1)} custom-call(s32[8]{0:T(128)} %fusion.8.head_ref, bf16[8,64,128]{2,1,0:T(8,128)(2,1)} %copy-done.5, bf16[2,1024,128]{2,1,0:T(8,128)(2,1)} %copy-done, bf16[2,1024,128]{2,1,0:T(8,128)(2,1)} %copy-done.2, bf16[2,1024,128]{2,1,0:T(8,128)(2,1)} %copy-done.3, bf16[2,1024,128]{2,1,0:T(8,128)(2,1)} %copy-done.4), custom_call_target="tpu_custom_call" | custom-call | tf_op jit(solution)/shard_map/pallas_call | solution.py:177
  (82 shorter events, 0.7 us)
Async XLA Ops:
  0.0 16.7 %copy-start.9 = (bf16[128,32]{0,1:T(8,128)(2,1)S(1)}, bf16[128,32]{0,1:T(8,128)(2,1)}, u32[]{:S(2)}) copy-start(bf16[128,32]{0,1:T(8,128)(2,1)} %param.13) | copy-start | bytes 24580
  0.0 16.7 %copy-start.8 = (bf16[3,32,128]{2,1,0:T(8,128)(2,1)S(1)}, bf16[3,32,128]{2,1,0:T(8,128)(2,1)}, u32[]{:S(2)}) copy-start(bf16[3,32,128]{2,1,0:T(8,128)(2,1)} %param.11) | copy-start | bytes 73732
  0.8 7.5 %collective-permute-start = (bf16[128,128]{1,0:T(8,128)(2,1)S(1)}, bf16[128,128]{1,0:T(8,128)(2,1)S(1)}, u32[]{:S(2)}, u32[]{:S(2)}) collective-permute-start(bf16[128,128]{1,0:T(8,128)(2,1)S(1)} %get-tuple-element.48), channel_id=1, source_target_pairs={{16,0},{24,8},{32,16},{40,24},{48,32},{56,40},{64,48},{72,56},{80,... | collective-permute-start | bytes 98312 | tf_op jit(solution)/shard_map/ppermute | solution.py:25
  6.8 5.7 %collective-permute-start.2 = (bf16[128,128]{1,0:T(8,128)(2,1)S(1)}, bf16[128,128]{1,0:T(8,128)(2,1)S(1)}, u32[]{:S(2)}, u32[]{:S(2)}) collective-permute-start(bf16[128,128]{1,0:T(8,128)(2,1)S(1)} %get-tuple-element.48), channel_id=1, source_target_pairs={{112,0},{120,8},{0,16},{8,24},{16,32},{24,40},{32,48},{40,56},{48,... | collective-permute-start | bytes 98312 | tf_op jit(solution)/shard_map/ppermute | solution.py:25
  8.4 8.2 %collective-permute-start.1 = (bf16[2,128,128]{2,1,0:T(8,128)(2,1)S(1)}, bf16[2,128,128]{2,1,0:T(8,128)(2,1)S(1)}, u32[]{:S(2)}, u32[]{:S(2)}) collective-permute-start(bf16[2,128,128]{2,1,0:T(8,128)(2,1)S(1)} %pad_maximum_fusion.5), channel_id=1, source_target_pairs={{80,0},{88,8},{96,16},{104,24},{112,32},{120,40},{0,48},{8,56},{16... | collective-permute-start | bytes 196616 | tf_op jit(solution)/shard_map/ppermute | solution.py:25
  12.5 9.1 %collective-permute-start.3 = (bf16[3,128,128]{2,1,0:T(8,128)(2,1)S(1)}, bf16[3,128,128]{2,1,0:T(8,128)(2,1)S(1)}, u32[]{:S(2)}, u32[]{:S(2)}) collective-permute-start(bf16[3,128,128]{2,1,0:T(8,128)(2,1)S(1)} %pad_maximum_fusion.4), channel_id=1, source_target_pairs={{48,0},{56,8},{64,16},{72,24},{80,32},{88,40},{96,48},{104,56},{11... | collective-permute-start | bytes 294920 | tf_op jit(solution)/shard_map/ppermute | solution.py:25
  21.6 8.0 %collective-permute-start.4 = (bf16[8,128,128]{2,1,0:T(8,128)(2,1)S(1)}, bf16[8,128,128]{2,1,0:T(8,128)(2,1)S(1)}, u32[]{:S(2)}, u32[]{:S(2)}) collective-permute-start(bf16[8,128,128]{2,1,0:T(8,128)(2,1)S(1)} %slice_dynamic-update-slice_fusion), channel_id=1, source_target_pairs={{128,0},{136,8},{144,16},{152,24},{160,32},{168,40},{176,48},{184,... | collective-permute-start | bytes 786440 | tf_op jit(solution)/shard_map/ppermute | solution.py:25
  22.0 7.8 %copy-start.1 = (bf16[512,1024]{1,0:T(8,128)(2,1)S(1)}, bf16[512,1024]{1,0:T(8,128)(2,1)}, u32[]{:S(2)}) copy-start(bf16[512,1024]{1,0:T(8,128)(2,1)} %param.9) | copy-start | bytes 3145732
  29.7 2.0 %collective-permute-start.5 = (bf16[2,8,128,128]{3,2,1,0:T(8,128)(2,1)S(1)}, bf16[2,8,128,128]{3,2,1,0:T(8,128)(2,1)S(1)}, u32[]{:S(2)}, u32[]{:S(2)}) collective-permute-start(bf16[2,8,128,128]{3,2,1,0:T(8,128)(2,1)S(1)} %pad_maximum_fusion.1), channel_id=1, source_target_pairs={{8,0},{0,8},{24,16},{16,24},{40,32},{32,40},{56,48},{48,56},{72,64... | collective-permute-start | bytes 1572872 | tf_op jit(solution)/shard_map/ppermute | solution.py:25
  31.9 0.7 copy-start.26
  33.4 39.5 %copy-start.7 = (bf16[512,256]{1,0:T(8,128)(2,1)}, bf16[512,256]{1,0:T(8,128)(2,1)S(1)}, u32[]{:S(2)}) copy-start(bf16[512,256]{1,0:T(8,128)(2,1)S(1)} %slice.45.refs_4_) | copy-start | bytes 786436
  33.4 23.8 %copy-start.12 = (s32[16]{0:T(128)S(1)}, s32[16]{0:T(128)}, u32[]{:S(2)}) copy-start(s32[16]{0:T(128)} %constant.184.clone) | copy-start | bytes 196
  33.4 23.8 %copy-start.13 = (s32[16]{0:T(128)S(1)}, s32[16]{0:T(128)}, u32[]{:S(2)}) copy-start(s32[16]{0:T(128)} %constant.183.clone) | copy-start | bytes 196
  33.4 9.9 %collective-permute-start.7 = (bf16[512,256]{1,0:T(8,128)(2,1)S(1)}, bf16[512,256]{1,0:T(8,128)(2,1)S(1)}, u32[]{:S(2)}, u32[]{:S(2)}) collective-permute-start(bf16[512,256]{1,0:T(8,128)(2,1)S(1)} %slice.45.refs_4_), channel_id=1, source_target_pairs={{112,0},{120,8},{0,16},{8,24},{16,32},{24,40},{32,48},{40,56},{48,... | collective-permute-start | bytes 786440 | tf_op jit(solution)/shard_map/ppermute | solution.py:25
  34.6 8.8 %collective-permute-start.6 = (bf16[512,256]{1,0:T(8,128)(2,1)S(1)}, bf16[512,256]{1,0:T(8,128)(2,1)S(1)}, u32[]{:S(2)}, u32[]{:S(2)}) collective-permute-start(bf16[512,256]{1,0:T(8,128)(2,1)S(1)} %slice.45.refs_4_), channel_id=1, source_target_pairs={{16,0},{24,8},{32,16},{40,24},{48,32},{56,40},{64,48},{72,56},{80,... | collective-permute-start | bytes 786440 | tf_op jit(solution)/shard_map/ppermute | solution.py:25
  36.8 6.6 %collective-permute-start.8 = (bf16[512,128]{1,0:T(8,128)(2,1)S(1)}, bf16[512,128]{1,0:T(8,128)(2,1)S(1)}, u32[]{:S(2)}, u32[]{:S(2)}) collective-permute-start(bf16[512,128]{1,0:T(8,128)(2,1)S(1)} %slice.44), channel_id=1, source_target_pairs={{128,0},{136,8},{144,16},{152,24},{160,32},{168,40},{176,48},{184,... | collective-permute-start | bytes 393224 | tf_op jit(solution)/shard_map/ppermute | solution.py:25
  43.4 31.6 %copy-start.14 = (bf16[512,256]{1,0:T(8,128)(2,1)}, bf16[512,256]{1,0:T(8,128)(2,1)S(1)}, u32[]{:S(2)}) copy-start(bf16[512,256]{1,0:T(8,128)(2,1)S(1)} %collective-permute-done.7.refs_8_) | copy-start | bytes 786436
  43.4 31.6 %copy-start.15 = (bf16[512,256]{1,0:T(8,128)(2,1)}, bf16[512,256]{1,0:T(8,128)(2,1)S(1)}, u32[]{:S(2)}) copy-start(bf16[512,256]{1,0:T(8,128)(2,1)S(1)} %collective-permute-done.6.refs_6_) | copy-start | bytes 786436
  43.4 7.3 %collective-permute-start.14 = (bf16[1024,128]{1,0:T(8,128)(2,1)S(1)}, bf16[1024,128]{1,0:T(8,128)(2,1)S(1)}, u32[]{:S(2)}, u32[]{:S(2)}) collective-permute-start(bf16[1024,128]{1,0:T(8,128)(2,1)S(1)} %bitcast.35), channel_id=1, source_target_pairs={{4,0},{5,1},{6,2},{7,3},{0,4},{1,5},{2,6},{3,7},{12,8},{13,9},{14,... | collective-permute-start | bytes 786440 | tf_op jit(solution)/shard_map/ppermute | solution.py:33
  44.7 7.1 %collective-permute-start.12 = (bf16[512,256]{1,0:T(8,128)(2,1)S(1)}, bf16[512,256]{1,0:T(8,128)(2,1)S(1)}, u32[]{:S(2)}, u32[]{:S(2)}) collective-permute-start(bf16[512,256]{1,0:T(8,128)(2,1)S(1)} %collective-permute-done.6.refs_6_), channel_id=1, source_target_pairs={{16,0},{24,8},{32,16},{40,24},{48,32},{56,40},{64,48},{72,56},{80,... | collective-permute-start | bytes 786440 | tf_op jit(solution)/shard_map/ppermute | solution.py:25
  47.3 7.9 %collective-permute-start.13 = (bf16[512,256]{1,0:T(8,128)(2,1)S(1)}, bf16[512,256]{1,0:T(8,128)(2,1)S(1)}, u32[]{:S(2)}, u32[]{:S(2)}) collective-permute-start(bf16[512,256]{1,0:T(8,128)(2,1)S(1)} %collective-permute-done.7.refs_8_), channel_id=1, source_target_pairs={{112,0},{120,8},{0,16},{8,24},{16,32},{24,40},{32,48},{40,56},{48,... | collective-permute-start | bytes 786440 | tf_op jit(solution)/shard_map/ppermute | solution.py:25
  50.7 41.2 %copy-start = (bf16[2,1024,128]{2,1,0:T(8,128)(2,1)}, bf16[2,1024,128]{2,1,0:T(8,128)(2,1)S(1)}, u32[]{:S(2)}) copy-start(bf16[2,1024,128]{2,1,0:T(8,128)(2,1)S(1)} %pad_maximum_fusion.2.refs_0_) | copy-start | bytes 1572868
  51.8 23.2 %copy-start.16 = (bf16[512,256]{1,0:T(8,128)(2,1)}, bf16[512,256]{1,0:T(8,128)(2,1)S(1)}, u32[]{:S(2)}) copy-start(bf16[512,256]{1,0:T(8,128)(2,1)S(1)} %collective-permute-done.12.refs_10_) | copy-start | bytes 786436
  55.2 19.8 %copy-start.17 = (bf16[512,256]{1,0:T(8,128)(2,1)}, bf16[512,256]{1,0:T(8,128)(2,1)S(1)}, u32[]{:S(2)}) copy-start(bf16[512,256]{1,0:T(8,128)(2,1)S(1)} %collective-permute-done.13.refs_12_) | copy-start | bytes 786436
  55.2 6.4 %collective-permute-start.17 = (bf16[512,256]{1,0:T(8,128)(2,1)S(1)}, bf16[512,256]{1,0:T(8,128)(2,1)S(1)}, u32[]{:S(2)}, u32[]{:S(2)}) collective-permute-start(bf16[512,256]{1,0:T(8,128)(2,1)S(1)} %collective-permute-done.12.refs_10_), channel_id=1, source_target_pairs={{16,0},{24,8},{32,16},{40,24},{48,32},{56,40},{64,48},{72,56},{80,... | collective-permute-start | bytes 786440 | tf_op jit(solution)/shard_map/ppermute | solution.py:25
  55.6 7.6 %collective-permute-start.18 = (bf16[512,256]{1,0:T(8,128)(2,1)S(1)}, bf16[512,256]{1,0:T(8,128)(2,1)S(1)}, u32[]{:S(2)}, u32[]{:S(2)}) collective-permute-start(bf16[512,256]{1,0:T(8,128)(2,1)S(1)} %collective-permute-done.13.refs_12_), channel_id=1, source_target_pairs={{112,0},{120,8},{0,16},{8,24},{16,32},{24,40},{32,48},{40,56},{48,... | collective-permute-start | bytes 786440 | tf_op jit(solution)/shard_map/ppermute | solution.py:25
  57.3 13.2 %collective-permute-start.22 = (bf16[2,1024,128]{2,1,0:T(8,128)(2,1)S(1)}, bf16[2,1024,128]{2,1,0:T(8,128)(2,1)S(1)}, u32[]{:S(2)}, u32[]{:S(2)}) collective-permute-start(bf16[2,1024,128]{2,1,0:T(8,128)(2,1)S(1)} %pad_maximum_fusion.2.refs_0_), channel_id=1, source_target_pairs={{1,0},{2,1},{3,2},{0,3},{5,4},{6,5},{7,6},{4,7},{9,8},{10,9},{11,1... | collective-permute-start | bytes 1572872 | tf_op jit(solution)/shard_map/ppermute | solution.py:33
  60.1 10.8 %collective-permute-start.9 = (bf16[512,256]{1,0:T(8,128)(2,1)S(1)}, bf16[512,256]{1,0:T(8,128)(2,1)S(1)}, u32[]{:S(2)}, u32[]{:S(2)}) collective-permute-start(bf16[512,256]{1,0:T(8,128)(2,1)S(1)} %slice.45.refs_4_), channel_id=1, source_target_pairs={{8,0},{0,8},{24,16},{16,24},{40,32},{32,40},{56,48},{48,56},{72,64... | collective-permute-start | bytes 786440 | tf_op jit(solution)/shard_map/ppermute | solution.py:25
  60.2 10.9 %collective-permute-start.10 = (bf16[512,256]{1,0:T(8,128)(2,1)S(1)}, bf16[512,256]{1,0:T(8,128)(2,1)}, u32[]{:S(2)}, u32[]{:S(2)}) collective-permute-start(bf16[512,256]{1,0:T(8,128)(2,1)S(1)} %collective-permute-done.6.refs_6_), channel_id=1, source_target_pairs={{8,0},{0,8},{24,16},{16,24},{40,32},{32,40},{56,48},{48,56},{72,64... | collective-permute-start | bytes 786440 | tf_op jit(solution)/shard_map/ppermute | solution.py:25
  61.6 13.4 %copy-start.18 = (bf16[512,256]{1,0:T(8,128)(2,1)}, bf16[512,256]{1,0:T(8,128)(2,1)S(1)}, u32[]{:S(2)}) copy-start(bf16[512,256]{1,0:T(8,128)(2,1)S(1)} %collective-permute-done.17.refs_14_) | copy-start | bytes 786436
  61.6 9.9 %collective-permute-start.11 = (bf16[512,256]{1,0:T(8,128)(2,1)S(1)}, bf16[512,256]{1,0:T(8,128)(2,1)}, u32[]{:S(2)}, u32[]{:S(2)}) collective-permute-start(bf16[512,256]{1,0:T(8,128)(2,1)S(1)} %collective-permute-done.7.refs_8_), channel_id=1, source_target_pairs={{8,0},{0,8},{24,16},{16,24},{40,32},{32,40},{56,48},{48,56},{72,64... | collective-permute-start | bytes 786440 | tf_op jit(solution)/shard_map/ppermute | solution.py:25
  63.2 11.9 %copy-start.19 = (bf16[512,256]{1,0:T(8,128)(2,1)}, bf16[512,256]{1,0:T(8,128)(2,1)S(1)}, u32[]{:S(2)}) copy-start(bf16[512,256]{1,0:T(8,128)(2,1)S(1)} %collective-permute-done.18.refs_16_) | copy-start | bytes 786436
  63.2 7.3 %collective-permute-start.21 = (bf16[512,256]{1,0:T(8,128)(2,1)S(1)}, bf16[512,256]{1,0:T(8,128)(2,1)}, u32[]{:S(2)}, u32[]{:S(2)}) collective-permute-start(bf16[512,256]{1,0:T(8,128)(2,1)S(1)} %collective-permute-done.17.refs_14_), channel_id=1, source_target_pairs={{16,0},{24,8},{32,16},{40,24},{48,32},{56,40},{64,48},{72,56},{80,... | collective-permute-start | bytes 786440 | tf_op jit(solution)/shard_map/ppermute | solution.py:25
  70.4 2.4 %collective-permute-start.15 = (bf16[512,256]{1,0:T(8,128)(2,1)S(1)}, bf16[512,256]{1,0:T(8,128)(2,1)S(1)}, u32[]{:S(2)}, u32[]{:S(2)}) collective-permute-start(bf16[512,256]{1,0:T(8,128)(2,1)S(1)} %collective-permute-done.12.refs_10_), channel_id=1, source_target_pairs={{8,0},{0,8},{24,16},{16,24},{40,32},{32,40},{56,48},{48,56},{72,64... | collective-permute-start | bytes 786440 | tf_op jit(solution)/shard_map/ppermute | solution.py:25
  70.4 23.1 %copy-start.2 = (bf16[2,1024,128]{2,1,0:T(8,128)(2,1)}, bf16[2,1024,128]{2,1,0:T(8,128)(2,1)S(1)}, u32[]{:S(2)}) copy-start(bf16[2,1024,128]{2,1,0:T(8,128)(2,1)S(1)} %collective-permute-done.22.refs_1_) | copy-start | bytes 1572868
  70.4 2.4 %collective-permute-start.16 = (bf16[512,256]{1,0:T(8,128)(2,1)S(1)}, bf16[512,256]{1,0:T(8,128)(2,1)S(1)}, u32[]{:S(2)}, u32[]{:S(2)}) collective-permute-start(bf16[512,256]{1,0:T(8,128)(2,1)S(1)} %collective-permute-done.13.refs_12_), channel_id=1, source_target_pairs={{8,0},{0,8},{24,16},{16,24},{40,32},{32,40},{56,48},{48,56},{72,64... | collective-permute-start | bytes 786440 | tf_op jit(solution)/shard_map/ppermute | solution.py:25
  70.9 4.1 %copy-start.20 = (bf16[512,256]{1,0:T(8,128)(2,1)}, bf16[512,256]{1,0:T(8,128)(2,1)S(1)}, u32[]{:S(2)}) copy-start(bf16[512,256]{1,0:T(8,128)(2,1)S(1)} %collective-permute-done.9.refs_5_) | copy-start | bytes 786436
  70.9 2.1 %collective-permute-start.19 = (bf16[512,256]{1,0:T(8,128)(2,1)S(1)}, bf16[512,256]{1,0:T(8,128)(2,1)S(1)}, u32[]{:S(2)}, u32[]{:S(2)}) collective-permute-start(bf16[512,256]{1,0:T(8,128)(2,1)S(1)} %collective-permute-done.17.refs_14_), channel_id=1, source_target_pairs={{8,0},{0,8},{24,16},{16,24},{40,32},{32,40},{56,48},{48,56},{72,64... | collective-permute-start | bytes 786440 | tf_op jit(solution)/shard_map/ppermute | solution.py:25
  71.1 2.0 %collective-permute-start.20 = (bf16[512,256]{1,0:T(8,128)(2,1)S(1)}, bf16[512,256]{1,0:T(8,128)(2,1)S(1)}, u32[]{:S(2)}, u32[]{:S(2)}) collective-permute-start(bf16[512,256]{1,0:T(8,128)(2,1)S(1)} %collective-permute-done.18.refs_16_), channel_id=1, source_target_pairs={{8,0},{0,8},{24,16},{16,24},{40,32},{32,40},{56,48},{48,56},{72,64... | collective-permute-start | bytes 786440 | tf_op jit(solution)/shard_map/ppermute | solution.py:25
  71.5 2.1 %collective-permute-start.23 = (bf16[512,256]{1,0:T(8,128)(2,1)}, bf16[512,256]{1,0:T(8,128)(2,1)S(1)}, u32[]{:S(2)}, u32[]{:S(2)}) collective-permute-start(bf16[512,256]{1,0:T(8,128)(2,1)} %collective-permute-done.21.refs_18_), channel_id=1, source_target_pairs={{8,0},{0,8},{24,16},{16,24},{40,32},{32,40},{56,48},{48,56},{72,64... | collective-permute-start | bytes 786440 | tf_op jit(solution)/shard_map/ppermute | solution.py:25
  72.9 0.7 copy-start.21
  72.9 0.8 copy-start.22
  73.1 0.7 copy-start.24
  73.6 0.7 copy-start.23
  74.3 0.7 copy-start.25
  91.9 19.3 %copy-start.10 = (s32[8]{0:T(128)S(1)}, s32[8]{0:T(128)}, u32[]{:S(2)}) copy-start(s32[8]{0:T(128)} %constant.186.clone) | copy-start | bytes 100
  91.9 19.3 %copy-start.11 = (s32[8]{0:T(128)S(1)}, s32[8]{0:T(128)}, u32[]{:S(2)}) copy-start(s32[8]{0:T(128)} %constant.185.clone) | copy-start | bytes 100
  92.0 25.8 %collective-permute-start.25 = (bf16[2,1024,128]{2,1,0:T(8,128)(2,1)S(1)}, bf16[2,1024,128]{2,1,0:T(8,128)(2,1)S(1)}, u32[]{:S(2)}, u32[]{:S(2)}) collective-permute-start(bf16[2,1024,128]{2,1,0:T(8,128)(2,1)S(1)} %pad_maximum_fusion.2.refs_0_), channel_id=1, source_target_pairs={{3,0},{0,1},{1,2},{2,3},{7,4},{4,5},{5,6},{6,7},{11,8},{8,9},{9,10... | collective-permute-start | bytes 1572872 | tf_op jit(solution)/shard_map/ppermute | solution.py:33
  93.5 24.2 %collective-permute-start.26 = (bf16[2,1024,128]{2,1,0:T(8,128)(2,1)S(1)}, bf16[2,1024,128]{2,1,0:T(8,128)(2,1)S(1)}, u32[]{:S(2)}, u32[]{:S(2)}) collective-permute-start(bf16[2,1024,128]{2,1,0:T(8,128)(2,1)S(1)} %collective-permute-done.22.refs_1_), channel_id=1, source_target_pairs={{1,0},{2,1},{3,2},{0,3},{5,4},{6,5},{7,6},{4,7},{9,8},{10,9},{11,1... | collective-permute-start | bytes 1572872 | tf_op jit(solution)/shard_map/ppermute | solution.py:33
  95.3 9.8 %collective-permute-start.24 = (bf16[512,256]{1,0:T(8,128)(2,1)}, bf16[512,256]{1,0:T(8,128)(2,1)S(1)}, u32[]{:S(2)}, u32[]{:S(2)}) collective-permute-start(bf16[512,256]{1,0:T(8,128)(2,1)} %get-tuple-element.38), channel_id=1, source_target_pairs={{128,0},{136,8},{144,16},{152,24},{160,32},{168,40},{176,48},{184,... | collective-permute-start | bytes 786440 | tf_op jit(solution)/shard_map/ppermute | solution.py:25
  105.1 0.7 copy-start.6
  107.8 9.9 %all-to-all-start = ((bf16[8,64,128]{2,1,0:T(8,128)(2,1)}), bf16[8,64,128]{2,1,0:T(8,128)(2,1)S(1)}, u32[]{:S(2)}, u32[]{:S(2)}) async-start(bf16[8,64,128]{2,1,0:T(8,128)(2,1)} %bitcast.37), calls=%async_computation | async-start | bytes 262144 | tf_op jit(solution)/shard_map/all_to_all | solution.py:265
  117.7 0.7 copy-start.5
  117.7 0.9 copy-start.3
  118.6 0.8 copy-start.4
